TPU v7x, 32 devices: a whole 2x2x4 slice. The times are simulated.
32 devices in a mesh: seq: 8 (over z, y), dp: 4 (over x, core).
Axes of the slice: x: 2, y: 2, z: 4, core: 2. Of those that a mesh axis runs over, the one named last changes fastest.
Arguments:
- embeddings: bfloat16 [24, 768, 768], P('dp', 'seq'), may hold values from -6 to 6
- kernels: bfloat16 [2, 3, 768, 768], replicated, may hold values from -0.125 to 0.125
- cotangent: bfloat16 [24, 768, 768], P('dp', 'seq'), may hold values from -6 to 6
Outputs:
- block_output: bfloat16 [24, 768, 768], P('dp', 'seq')
- input_grad: bfloat16 [24, 768, 768], P('dp', 'seq')
- kernel_grad: float32 [2, 3, 768, 768], P(None, None, 'dp', 'seq')
All inputs are finite; a program needn't handle non-finite values.
Results may differ from a plain program's by a relative error of at most 0.0054.
Values may be sent and summed in bfloat16 or wider, within the bound.
No kernel may reach another device: no remote copies, remote signals or barrier semaphores. Data moves between devices by JAX's collectives and lax.ppermute only.
A program may use at most 128 MiB of HBM per device.

v0:
```python
from functools import partial
import math

import jax
import jax.numpy as jnp
from jax import lax
from jax.sharding import PartitionSpec as P

FIRST_DILATION = 8


def extended(cells, sides, width):
    for axis, dim in sides:
        count = lax.axis_size(axis)
        ends = count - 1
        head = lax.slice_in_dim(cells, 0, width, axis=dim)
        tail = lax.slice_in_dim(cells, cells.shape[dim] - width, cells.shape[dim], axis=dim)
        cells = jnp.concatenate(
            [
                lax.ppermute(tail, axis, [(i, (i + 1) % count) for i in range(ends)]),
                cells,
                lax.ppermute(head, axis, [((i + 1) % count, i) for i in range(ends)]),
            ],
            axis=dim,
        )
    return cells


def normed(hidden):
    wide = hidden.astype(jnp.float32)
    recip = lax.rsqrt(jnp.mean(wide * wide, axis=-1, keepdims=True) + 1e-05)
    return (wide * recip, recip, wide)


def dilated(padded, weight, dilation_rate, output_length, offsets):
    batches = padded.shape[0]
    channels = padded.shape[2]
    summed = jnp.zeros((batches * output_length, weight.shape[2]), jnp.float32)
    for kernel_tap in range(3):
        start = offsets[kernel_tap] * dilation_rate
        window = padded[:, start : start + output_length, :].reshape(
            batches * output_length, channels
        )
        summed = summed + jnp.dot(window, weight[kernel_tap], preferred_element_type=jnp.float32)
    return summed.reshape(batches, output_length, weight.shape[2])


def tap_grads(padded, upstream_gradient, dilation_rate, output_length):
    channels = padded.shape[2]
    flat_up = upstream_gradient.reshape(-1, upstream_gradient.shape[2])
    piece_parts = []
    for kernel_tap in range(3):
        start = kernel_tap * dilation_rate
        window = padded[:, start : start + output_length, :].reshape(-1, channels)
        piece_parts.append(
            lax.dot_general(
                window, flat_up, (((0,), (0,)), ((), ())), preferred_element_type=jnp.float32
            )
        )
    return jnp.stack(piece_parts)


def per_device(embeddings, kernels, cotangent):
    batches, rows_here, channels = embeddings.shape
    layers = kernels.shape[0]
    seq_devices = lax.axis_size("seq")
    saved_h = []
    saved_pad = []
    current = embeddings
    for layer_index in range(layers):
        dilation_rate = FIRST_DILATION * 2**layer_index
        normal_activation, recip, wide = normed(current)
        active = jax.nn.gelu(normal_activation, approximate=True).astype(jnp.bfloat16)
        padded = extended(active, (("seq", 1),), dilation_rate)
        saved_h.append(current)
        saved_pad.append(padded)
        mixed = dilated(padded, kernels[layer_index], dilation_rate, rows_here, (0, 1, 2))
        current = (current.astype(jnp.float32) + mixed).astype(jnp.bfloat16)
    factor = 1.0 / math.sqrt(batches * lax.axis_size("dp") * rows_here * seq_devices)
    grad_h = cotangent.astype(jnp.float32)
    grads = [None] * layers
    for layer_index in reversed(range(layers)):
        dilation_rate = FIRST_DILATION * 2**layer_index
        upstream_gradient = grad_h.astype(jnp.bfloat16)
        padded_up = extended(upstream_gradient, (("seq", 1),), dilation_rate)
        partial_grad = (
            tap_grads(saved_pad[layer_index], upstream_gradient, dilation_rate, rows_here) * factor
        )
        reduced = lax.psum_scatter(partial_grad, "dp", scatter_dimension=1, tiled=True)
        reduced = lax.psum_scatter(reduced, "seq", scatter_dimension=2, tiled=True)
        grads[layer_index] = reduced
        swapped = jnp.swapaxes(kernels[layer_index], 1, 2)
        back_conv = dilated(padded_up, swapped, dilation_rate, rows_here, (2, 1, 0))
        normal_activation, recip, wide = normed(saved_h[layer_index])
        primal, pullback = jax.vjp(partial(jax.nn.gelu, approximate=True), normal_activation)
        through = pullback(back_conv)[0]
        inner = jnp.mean(through * wide, axis=-1, keepdims=True)
        grad_h = grad_h + recip * through - wide * recip * recip * recip * inner
    return (current, grad_h.astype(jnp.bfloat16), jnp.stack(grads))


def solution(mesh):
    placed = (P("dp", "seq", None), P(), P("dp", "seq", None))
    return jax.shard_map(
        per_device,
        mesh=mesh,
        in_specs=placed,
        out_specs=(P("dp", "seq", None), P("dp", "seq", None), P(None, None, "dp", "seq")),
        check_vma=False,
    )
```

profile of v0, /device:TPU:0, one launch (start us, length us, event | category | flops | bytes accessed | tf_op | source)
XLA Modules:
  0.0 325.7 jit_solution(3256833273233376335)
XLA Ops:
  7.2 1.5 fusion.28
  8.7 1.9 fusion.21
  10.6 1.3 collective-permute-start.1
  11.9 5.5 %collective-permute-start = (bf16[6,8,768]{2,1,0:T(8,128)(2,1)S(1)}, bf16[6,8,768]{2,1,0:T(8,128)(2,1)S(1)}, u32[]{:S(2)}, u32[]{:S(2)}) collective-permute-start(bf16[6,8,768]{2,1,0:T(8,128)(2,1)S(1)} %get-tuple-element.24), channel_id=1, source_target_pairs={{0,4},{4,8},{8,12},{12,16},{16,20},{20,24},{24,28},{1,5},{5,9},{9,... | collective-permute-start | bytes 221192 | tf_op jit(solution)/shard_map/ppermute | solution.py:20
  17.5 4.8 %collective-permute-start.5 = (bf16[6,16,768]{2,1,0:T(8,128)(2,1)S(1)}, bf16[6,16,768]{2,1,0:T(8,128)(2,1)S(1)}, u32[]{:S(2)}, u32[]{:S(2)}) collective-permute-start(bf16[6,16,768]{2,1,0:T(8,128)(2,1)S(1)} %get-tuple-element.15), channel_id=1, source_target_pairs={{0,4},{4,8},{8,12},{12,16},{16,20},{20,24},{24,28},{1,5},{5,9},{9,... | collective-permute-start | bytes 442376 | tf_op jit(solution)/shard_map/ppermute | solution.py:20
  22.4 1.6 collective-permute-start.4
  23.9 5.8 %slice_bitcast_fusion = (bf16[3,768,768]{1,2,0:T(8,128)(2,1)}, bf16[3,768,768]{1,2,0:T(8,128)(2,1)S(1)}) fusion(bf16[2,3,768,768]{3,2,1,0:T(8,128)(2,1)} %param.4), kind=kLoop, calls=%fused_computation.2 | loop fusion | bytes 14155776 | tf_op jit(solution)/shard_map/transpose | solution.py:92
  36.0 1.8 fusion.42
  37.9 1.9 fusion.71
  43.2 3.1 maximum_multiply_fusion
  47.4 4.1 %collective-permute-start.7 = (bf16[6,8,768]{2,1,0:T(8,128)(2,1)S(1)}, bf16[6,8,768]{2,1,0:T(8,128)(2,1)S(1)}, u32[]{:S(2)}, u32[]{:S(2)}) collective-permute-start(bf16[6,8,768]{2,1,0:T(8,128)(2,1)S(1)} %get-tuple-element.11), channel_id=1, source_target_pairs={{0,4},{4,8},{8,12},{12,16},{16,20},{20,24},{24,28},{1,5},{5,9},{9,... | collective-permute-start | bytes 221192 | tf_op jit(solution)/shard_map/ppermute | solution.py:20
  51.5 1.5 collective-permute-start.6
  53.0 2.7 fusion.44
  55.7 2.1 collective-permute-done.6
  59.7 1.8 fusion.30
  61.5 4.5 %fusion.27 = (bf16[6,96,768]{2,1,0:T(8,128)(2,1)}, bf16[6,96,768]{2,1,0:T(8,128)(2,1)S(1)}) fusion(bf16[6,96,768]{2,1,0:T(8,128)(2,1)S(1)} %copy-done, f32[6,96]{1,0:T(8,128)S(1)} %broadcast_multiply_fusion, f32[6,96]{1,0:T(8,128)S(1)} %add_rsqrt_fusion.1, f32[6,96]{1,0:T(8,128)S(1)} %broadcast_multiply_fusion.1, ...), kind=kLoop, calls=%fused_computation.39 | loop fusion | flops 25657344 | bytes 7971840 | tf_op jit(solution)/shard_map/convert_element_type | solution.py:99
  66.1 1.3 collective-permute-start.3
  67.4 5.1 %collective-permute-start.2 = (bf16[6,16,768]{2,1,0:T(8,128)(2,1)S(1)}, bf16[6,16,768]{2,1,0:T(8,128)(2,1)S(1)}, u32[]{:S(2)}, u32[]{:S(2)}) collective-permute-start(bf16[6,16,768]{2,1,0:T(8,128)(2,1)S(1)} %get-tuple-element.20), channel_id=1, source_target_pairs={{0,4},{4,8},{8,12},{12,16},{16,20},{20,24},{24,28},{1,5},{5,9},{9,... | collective-permute-start | bytes 442376 | tf_op jit(solution)/shard_map/ppermute | solution.py:20
  73.6 2.0 collective-permute-done.2
  78.1 3.3 maximum_multiply_fusion.1
  81.4 29.7 %reduce-scatter.9.cloned.1.call-done = f32[3,192,768]{2,1,0:T(8,128)} async-done(((f32[3,768,768]{2,1,0:T(8,128)}), f32[3,192,768]{2,1,0:T(8,128)}) %reduce-scatter.9.cloned.1.call-update) | async-done | bytes 1769488 | tf_op jit(solution)/shard_map/reduce_scatter | solution.py:89
  111.1 4.2 %copy.6 = f32[3,192,768]{1,0,2:T(4,128)} copy(f32[3,192,768]{2,1,0:T(8,128)} %reduce-scatter.9.cloned.1.call-done) | data formatting | bytes 3538944
  115.3 4.7 %reshape.120 = f32[768,576]{1,0:T(8,128)} reshape(f32[768,3,192]{2,1,0:T(4,128)} %bitcast.123) | data formatting | bytes 3538944
  120.3 57.3 %reduce-scatter.11.cloned.1.call-done = f32[3,192,768]{2,1,0:T(8,128)} async-done(((f32[3,768,768]{2,1,0:T(8,128)}), f32[3,192,768]{2,1,0:T(8,128)}) %reduce-scatter.11.cloned.1.call-update) | async-done | bytes 1769488 | tf_op jit(solution)/shard_map/reduce_scatter | solution.py:89
  177.6 4.2 %copy.8 = f32[3,192,768]{1,0,2:T(4,128)} copy(f32[3,192,768]{2,1,0:T(8,128)} %reduce-scatter.11.cloned.1.call-done) | data formatting | bytes 3538944
  181.8 4.6 %reshape.122 = f32[768,576]{1,0:T(8,128)} reshape(f32[768,3,192]{2,1,0:T(4,128)} %bitcast.124) | data formatting | bytes 3538944
  186.4 1.1 copy-done.6
  187.6 2.2 fusion.53
  189.8 2.1 fusion.55
  191.9 2.2 add_add_fusion.2
  195.1 52.5 %reduce-scatter.13.cloned.1.call-done = f32[96,576]{1,0:T(8,128)} async-done(((f32[768,576]{1,0:T(8,128)}), f32[96,576]{1,0:T(8,128)}) %reduce-scatter.13.cloned.1.call-update) | async-done | bytes 221200
  249.0 68.0 %reduce-scatter.15.cloned.1.call-done = f32[96,576]{1,0:T(8,128)} async-done(((f32[768,576]{1,0:T(8,128)}), f32[96,576]{1,0:T(8,128)}) %reduce-scatter.15.cloned.1.call-update) | async-done | bytes 221200
  (69 shorter events, 21.2 us)
Async XLA Ops:
  7.2 10.3 %copy-start.1 = (bf16[6,96,768]{2,1,0:T(8,128)(2,1)S(1)}, bf16[6,96,768]{2,1,0:T(8,128)(2,1)}, u32[]{:S(2)}) copy-start(bf16[6,96,768]{2,1,0:T(8,128)(2,1)} %param.5) | copy-start | bytes 2654212
  7.2 104.0 %reduce-scatter.9.cloned.1.call-start = ((), (), s32[]{:S(2)}) async-start(), calls=%async_computation.4 | async-start | bytes 8847360 | tf_op jit(solution)/shard_map/reduce_scatter | solution.py:89
  10.6 20.8 %collective-permute-start.1 = (bf16[6,8,768]{2,1,0:T(8,128)(2,1)S(1)}, bf16[6,8,768]{2,1,0:T(8,128)(2,1)S(1)}, u32[]{:S(2)}, u32[]{:S(2)}) collective-permute-start(bf16[6,8,768]{2,1,0:T(8,128)(2,1)S(1)} %get-tuple-element.23), channel_id=1, source_target_pairs={{4,0},{8,4},{12,8},{16,12},{20,16},{24,20},{28,24},{5,1},{9,5},{13... | collective-permute-start | bytes 221192 | tf_op jit(solution)/shard_map/ppermute | solution.py:22
  11.9 19.5 %collective-permute-start = (bf16[6,8,768]{2,1,0:T(8,128)(2,1)S(1)}, bf16[6,8,768]{2,1,0:T(8,128)(2,1)S(1)}, u32[]{:S(2)}, u32[]{:S(2)}) collective-permute-start(bf16[6,8,768]{2,1,0:T(8,128)(2,1)S(1)} %get-tuple-element.24), channel_id=1, source_target_pairs={{0,4},{4,8},{8,12},{12,16},{16,20},{20,24},{24,28},{1,5},{5,9},{9,... | collective-permute-start | bytes 221192 | tf_op jit(solution)/shard_map/ppermute | solution.py:20
  17.5 16.5 %collective-permute-start.5 = (bf16[6,16,768]{2,1,0:T(8,128)(2,1)S(1)}, bf16[6,16,768]{2,1,0:T(8,128)(2,1)S(1)}, u32[]{:S(2)}, u32[]{:S(2)}) collective-permute-start(bf16[6,16,768]{2,1,0:T(8,128)(2,1)S(1)} %get-tuple-element.15), channel_id=1, source_target_pairs={{0,4},{4,8},{8,12},{12,16},{16,20},{20,24},{24,28},{1,5},{5,9},{9,... | collective-permute-start | bytes 442376 | tf_op jit(solution)/shard_map/ppermute | solution.py:20
  22.3 7.4 %slice-start = ((s8[7077888]{0:T(1024)(128)(4,1)}), s8[4194304]{0:T(1024)(128)(4,1)S(1)}, s32[]{:S(2)}) async-start(s8[7077888]{0:T(1024)(128)(4,1)} %bitcast.121), calls=%async_computation.8 | async-start | bytes 8388608
  22.3 7.4 %slice-start.1 = ((s8[7077888]{0:T(1024)(128)(4,1)}), s8[2883584]{0:T(1024)(128)(4,1)S(1)}, s32[]{:S(2)}) async-start(s8[7077888]{0:T(1024)(128)(4,1)} %bitcast.121), calls=%async_computation.9 | async-start | bytes 5767168
  22.4 11.7 %collective-permute-start.4 = (bf16[6,16,768]{2,1,0:T(8,128)(2,1)S(1)}, bf16[6,16,768]{2,1,0:T(8,128)(2,1)S(1)}, u32[]{:S(2)}, u32[]{:S(2)}) collective-permute-start(bf16[6,16,768]{2,1,0:T(8,128)(2,1)S(1)} %get-tuple-element.16), channel_id=1, source_target_pairs={{4,0},{8,4},{12,8},{16,12},{20,16},{24,20},{28,24},{5,1},{9,5},{13... | collective-permute-start | bytes 442376 | tf_op jit(solution)/shard_map/ppermute | solution.py:22
  32.5 1.2 copy-start
  36.0 1.8 copy-start.2
  39.8 2.3 copy-start.7
  46.3 131.2 %reduce-scatter.11.cloned.1.call-start = ((), (), s32[]{:S(2)}) async-start(), calls=%async_computation.5 | async-start | bytes 8847360 | tf_op jit(solution)/shard_map/reduce_scatter | solution.py:89
  46.4 11.4 %copy-start.8 = (bf16[6,96,768]{2,1,0:T(8,128)(2,1)S(1)}, bf16[6,96,768]{2,1,0:T(8,128)(2,1)}, u32[]{:S(2)}) copy-start(bf16[6,96,768]{2,1,0:T(8,128)(2,1)} %copy-done.7) | copy-start | bytes 2654212
  47.4 8.3 %collective-permute-start.7 = (bf16[6,8,768]{2,1,0:T(8,128)(2,1)S(1)}, bf16[6,8,768]{2,1,0:T(8,128)(2,1)S(1)}, u32[]{:S(2)}, u32[]{:S(2)}) collective-permute-start(bf16[6,8,768]{2,1,0:T(8,128)(2,1)S(1)} %get-tuple-element.11), channel_id=1, source_target_pairs={{0,4},{4,8},{8,12},{12,16},{16,20},{20,24},{24,28},{1,5},{5,9},{9,... | collective-permute-start | bytes 221192 | tf_op jit(solution)/shard_map/ppermute | solution.py:20
  51.5 6.2 %collective-permute-start.6 = (bf16[6,8,768]{2,1,0:T(8,128)(2,1)S(1)}, bf16[6,8,768]{2,1,0:T(8,128)(2,1)S(1)}, u32[]{:S(2)}, u32[]{:S(2)}) collective-permute-start(bf16[6,8,768]{2,1,0:T(8,128)(2,1)S(1)} %get-tuple-element.12), channel_id=1, source_target_pairs={{4,0},{8,4},{12,8},{16,12},{20,16},{24,20},{28,24},{5,1},{9,5},{13... | collective-permute-start | bytes 221192 | tf_op jit(solution)/shard_map/ppermute | solution.py:22
  53.0 4.9 %copy-start.4 = (bf16[3,768,768]{1,2,0:T(8,128)(2,1)S(1)}, bf16[3,768,768]{1,2,0:T(8,128)(2,1)}, u32[]{:S(2)}) copy-start(bf16[3,768,768]{1,2,0:T(8,128)(2,1)} %get-tuple-element.5) | copy-start | bytes 10616836
  59.7 1.9 copy-start.3
  66.0 9.6 %copy-start.5 = (bf16[6,96,768]{2,1,0:T(8,128)(2,1)}, bf16[6,96,768]{2,1,0:T(8,128)(2,1)S(1)}, u32[]{:S(2)}) copy-start(bf16[6,96,768]{2,1,0:T(8,128)(2,1)S(1)} %get-tuple-element.8) | copy-start | bytes 2654212
  66.1 7.6 %collective-permute-start.3 = (bf16[6,16,768]{2,1,0:T(8,128)(2,1)S(1)}, bf16[6,16,768]{2,1,0:T(8,128)(2,1)S(1)}, u32[]{:S(2)}, u32[]{:S(2)}) collective-permute-start(bf16[6,16,768]{2,1,0:T(8,128)(2,1)S(1)} %get-tuple-element.19), channel_id=1, source_target_pairs={{4,0},{8,4},{12,8},{16,12},{20,16},{24,20},{28,24},{5,1},{9,5},{13... | collective-permute-start | bytes 442376 | tf_op jit(solution)/shard_map/ppermute | solution.py:22
  67.4 8.3 %collective-permute-start.2 = (bf16[6,16,768]{2,1,0:T(8,128)(2,1)S(1)}, bf16[6,16,768]{2,1,0:T(8,128)(2,1)S(1)}, u32[]{:S(2)}, u32[]{:S(2)}) collective-permute-start(bf16[6,16,768]{2,1,0:T(8,128)(2,1)S(1)} %get-tuple-element.20), channel_id=1, source_target_pairs={{0,4},{4,8},{8,12},{12,16},{16,20},{20,24},{24,28},{1,5},{5,9},{9,... | collective-permute-start | bytes 442376 | tf_op jit(solution)/shard_map/ppermute | solution.py:20
  81.4 166.3 %reduce-scatter.13.cloned.1.call-start = ((), (), s32[]{:S(2)}) async-start(), calls=%async_computation.6 | async-start | bytes 2211840
  120.0 197.0 %reduce-scatter.15.cloned.1.call-start = ((), (), s32[]{:S(2)}) async-start(), calls=%async_computation.7 | async-start | bytes 2211840
  186.4 1.2 copy-start.6
Sparse Core Ops, SparseCore 0:
  46.5 64.6 reduce-scatter.8
  113.8 63.6 reduce-scatter.10
  181.0 66.6 reduce-scatter.12
  251.4 65.5 reduce-scatter.14
where the time goes:
time: 327 us; the launch traced here: 326 us
  waiting for transfers between devices  212 us (65%)
  local copies, waits for them, and re-layouts  28.6 us (9%)
  starting transfers between devices  25.5 us (8%)
  matrix products  22.9 us (7%)
  other arithmetic  22.7 us (7%)
  between operations  14.2 us (4%)
    unnamed x6, waiting for transfers between devices  121 us
    reduce_scatter x2, waiting for transfers between devices, per_device(): lax.psum_scatter(partial_grad, 'dp', scatter_dimension=1, tiled=True)  87 us
    unnamed x30, local copies, waits for them, and re-layouts  21.7 us
    ppermute x4, starting transfers between devices, extended(): lax.ppermute(tail, axis, [(i, (i + 1) % count) for i in range(ends)])  19.5 us
    dot_general x12, matrix products, dilated(): jnp.dot(window, weight[kernel_tap], preferred_element_type=jnp.float32)  16.2 us
    dot_general x6, matrix products, tap_grads(): lax.dot_general(window, flat_up, (((0,), (0,)), ((), ())), preferred_elem...  6.74 us
  transfers between devices with their start and end apart: 12, of which 6 were waited for; matrix products, arithmetic and copies ran while one was open for 17% of the time, Pallas kernels for 0%

commit v1 on v0

v1 whole, which is shorter than its diff:
```python
import math
from functools import partial

import jax
import jax.numpy as jnp
from jax import lax
from jax.experimental import pallas as pl
from jax.experimental.pallas import tpu as pltpu
from jax.sharding import PartitionSpec as P

FIRST_DILATION = 8
F32 = jnp.float32
BF16 = jnp.bfloat16
VMEM = pl.BlockSpec(memory_space=pltpu.VMEM)
SMEM = pl.BlockSpec(memory_space=pltpu.SMEM)
VMEM_LIMIT = 28 * 2**20
ROOT = math.sqrt(2.0 / math.pi)
CUBE = 0.044715


def kernel_call(body, args, outs, flops=0, scalars=None, scratch=()):
    moved = sum(a.size * a.dtype.itemsize for a in args)
    moved += sum(math.prod(o.shape) * o.dtype.itemsize for o in outs)
    specs = [VMEM] * len(args)
    if scalars is not None:
        args, specs = [scalars, *args], [SMEM, *specs]
    return pl.pallas_call(
        body,
        out_shape=tuple(outs),
        in_specs=specs,
        out_specs=tuple(VMEM for _ in outs),
        scratch_shapes=list(scratch),
        compiler_params=pltpu.CompilerParams(vmem_limit_bytes=VMEM_LIMIT),
        cost_estimate=pl.CostEstimate(flops=flops, bytes_accessed=moved, transcendentals=0),
    )(*args)


def shape(dims, dtype=BF16):
    return jax.ShapeDtypeStruct(tuple(dims), dtype)


def normed(hidden):
    wide = hidden.astype(F32)
    recip = lax.rsqrt(jnp.mean(wide * wide, axis=-1, keepdims=True) + 1e-05)
    return wide * recip, recip, wide


def gelu(v):
    return 0.5 * v * (1.0 + jnp.tanh(ROOT * (v + CUBE * (v * v * v))))


def gelu_slope(v):
    square = v * v
    t = jnp.tanh(ROOT * v * (1.0 + CUBE * square))
    return 0.5 * (1.0 + t) + 0.5 * v * (1.0 - t * t) * (ROOT * (1.0 + 3.0 * CUBE * square))


def flat(cells):
    return cells.reshape(-1, cells.shape[-1])


def dot(a, b):
    return jnp.dot(a, b, preferred_element_type=F32)


def dot_nt(a, b):
    return lax.dot_general(a, b, (((1,), (1,)), ((), ())), preferred_element_type=F32)


def dot_tn(a, b):
    return lax.dot_general(a, b, (((0,), (0,)), ((), ())), preferred_element_type=F32)


def windows(above, own, below):
    width, rows = above.shape[1], own.shape[1]
    before = jnp.concatenate([above, own[:, : rows - width]], axis=1)
    after = jnp.concatenate([own[:, width:], below], axis=1)
    return flat(before), flat(own), flat(after)


def halves(cells, parity):
    q = cells.shape[-1] // 4
    even = jnp.concatenate([cells[..., :q], cells[..., 2 * q : 3 * q]], axis=-1)
    odd = jnp.concatenate([cells[..., q : 2 * q], cells[..., 3 * q :]], axis=-1)
    first = parity == 0
    return jnp.where(first, even, odd), jnp.where(first, odd, even)


def by_low_bit(cells, count):
    w = cells.shape[-1] // count
    order = [*range(0, count, 2), *range(1, count, 2)]
    return jnp.concatenate([cells[..., j * w : (j + 1) * w] for j in order], axis=-1)


def first_body(h_ref, w_ref, s_ref, z_ref):
    act, _, _ = normed(h_ref[...])
    s = gelu(act)
    edge = jnp.zeros((s.shape[0], FIRST_DILATION, s.shape[2]), F32)
    before, own, after = (v.astype(BF16) for v in windows(edge, s, edge))
    s_ref[...] = own.reshape(s_ref.shape)
    z = dot(own, w_ref[1]) + dot(before, w_ref[0]) + dot(after, w_ref[2])
    z_ref[...] = z.reshape(z_ref.shape)


def second_body(where_ref, z_ref, h_ref, s_ref, up_ref, down_ref, w_ref, h1_ref, s1_ref, keep_ref, send_ref, kx_ref, sx_ref):
    width = up_ref.shape[1]
    rows = h_ref.shape[1]
    parity = where_ref[0]
    above = gelu(normed(up_ref[...])[0])
    below = gelu(normed(down_ref[...])[0])
    s = s_ref[...]
    ext = jnp.concatenate([above, s.astype(F32), below], axis=1).astype(BF16)
    kept, sent = halves(ext, parity)
    kx_ref[...] = kept
    sx_ref[...] = sent
    add_top = dot(flat(above).astype(BF16), w_ref[0]).reshape(above.shape)
    add_low = dot(flat(below).astype(BF16), w_ref[2]).reshape(below.shape)
    z = z_ref[...]
    z = jnp.concatenate([z[:, :width] + add_top, z[:, width : rows - width], z[:, rows - width :] + add_low], axis=1)
    h1 = (h_ref[...].astype(F32) + z).astype(BF16)
    h1_ref[...] = h1
    s1 = gelu(normed(h1)[0]).astype(BF16)
    s1_ref[...] = s1
    kept, sent = halves(s1, parity)
    keep_ref[...] = kept
    send_ref[...] = sent


def extend_body(count, up_ref, own_ref, down_ref, out_ref):
    ext = jnp.concatenate([up_ref[...], own_ref[...], down_ref[...]], axis=1)
    out_ref[...] = by_low_bit(ext, count)


def back_conv(q_ref, up_ref, down_ref, w_ref, h_ref, g):
    wide_q = q_ref[...].astype(F32)
    before, own, after = windows(up_ref[...].astype(F32), wide_q, down_ref[...].astype(F32))
    e = dot_nt(own.astype(BF16), w_ref[1])
    e += dot_nt(after.astype(BF16), w_ref[0])
    e += dot_nt(before.astype(BF16), w_ref[2])
    act, recip, wide = normed(h_ref[...])
    through = e.reshape(act.shape) * gelu_slope(act)
    inner = jnp.mean(through * wide, axis=-1, keepdims=True)
    return g + recip * through - wide * (recip * recip * recip * inner)


def back_body(count, q_ref, up_ref, down_ref, w_ref, h_ref, g_ref, out_ref, mixed_ref):
    g = back_conv(q_ref, up_ref, down_ref, w_ref, h_ref, q_ref[...].astype(F32))
    g_ref[...] = g
    q = g.astype(BF16)
    out_ref[...] = q
    mixed_ref[...] = by_low_bit(q, count)


def last_back_body(q_ref, up_ref, down_ref, w_ref, h_ref, g_ref, out_ref):
    out_ref[...] = back_conv(q_ref, up_ref, down_ref, w_ref, h_ref, g_ref[...]).astype(BF16)


def last_body(s_ref, up_ref, down_ref, w_ref, h_ref, out_ref):
    before, own, after = windows(up_ref[...], s_ref[...], down_ref[...])
    z = dot(before, w_ref[0]) + dot(own, w_ref[1]) + dot(after, w_ref[2])
    out_ref[...] = (h_ref[...].astype(F32) + z.reshape(h_ref.shape)).astype(BF16)


def grad_body(taps_of_s, where_ref, s_ref, s2_ref, q_ref, q2_ref, keep_ref, send_ref, d_ref):
    rows = s_ref.shape[1] if not taps_of_s else q_ref.shape[1]
    wide = q_ref.shape[2] // 2
    tall = s_ref.shape[2] // 2

    def cut(ref, start):
        return flat(ref[:, start : start + rows, :])

    def pair(a_ref, b_ref, start):
        return jnp.concatenate([cut(a_ref, start), cut(b_ref, start)], axis=0)

    if taps_of_s:
        step = (s_ref.shape[1] - rows) // 2
        q = pair(q_ref, q2_ref, 0)
    else:
        step = (q_ref.shape[1] - rows) // 2
        s = pair(s_ref, s2_ref, 0)
    for tap in range(3):
        if taps_of_s:
            s = pair(s_ref, s2_ref, tap * step)
        else:
            q = pair(q_ref, q2_ref, (2 - tap) * step)
        d = dot_tn(s, q)
        for i in range(2):
            for j in range(2):
                d_ref[tap, i, j] = d[i * tall : (i + 1) * tall, j * wide : (j + 1) * wide]
    first = where_ref[0] == 0
    x, y = where_ref[1], where_ref[2]
    for i in range(2):
        kx, ky = jnp.where(first, x, i), jnp.where(first, i, y)
        gx, gy = jnp.where(first, 1 - x, i), jnp.where(first, i, 1 - y)
        for tap in range(3):
            keep_ref[i, tap] = d_ref[tap, kx, ky]
            send_ref[i, tap] = d_ref[tap, gx, gy].astype(BF16)


def weave_body(count, keep_ref, got_ref, out_ref):
    total = flat(keep_ref[...] + got_ref[...].astype(F32))
    w, r = total.shape[1] // count, total.shape[0] // count
    for block in range(count):
        out_ref[block] = jnp.concatenate(
            [total[g * r : (g + 1) * r, block * w : (block + 1) * w] for g in range(count)], axis=1
        )


def unweave_body(count, factor, keep_ref, got_ref, out_ref):
    total = (keep_ref[...] + got_ref[...].astype(F32)) * factor
    w = total.shape[1] // count
    rows = jnp.concatenate([total[:, g * w : (g + 1) * w] for g in range(count)], axis=0)
    out_ref[...] = rows.reshape(out_ref.shape)


def pick(cells, bit, axis):
    return lax.dynamic_index_in_dim(cells, bit, axis, keepdims=False)


def per_device(embeddings, kernels, cotangent):
    batches, rows, channels = embeddings.shape
    seqs, dps = lax.axis_size("seq"), lax.axis_size("dp")
    axes = ("seq", "dp")
    near, far = FIRST_DILATION, 2 * FIRST_DILATION
    seq, dp = lax.axis_index("seq"), lax.axis_index("dp")
    where = jnp.stack([dp % 2, (dp // 2) % 2, seq % 2]).astype(jnp.int32)
    tokens = batches * rows
    conv_flops = 6 * tokens * channels * channels
    own = (batches, rows, channels)

    up = partial(lax.ppermute, axis_name="seq", perm=[(i, i + 1) for i in range(seqs - 1)])
    down = partial(lax.ppermute, axis_name="seq", perm=[(i + 1, i) for i in range(seqs - 1)])
    swap = partial(lax.ppermute, axis_name="dp", perm=[(i, i ^ 1) for i in range(dps)])

    def crossed(first):
        pairs = []
        for s in range(seqs):
            for d in range(dps):
                along_dp = (d % 2 == 0) == first
                t = (s, d ^ 2) if along_dp else (s ^ 1, d)
                pairs.append((s * dps + d, t[0] * dps + t[1]))
        return partial(lax.ppermute, axis_name=axes, perm=pairs)

    def along(bit):
        return partial(lax.ppermute, axis_name="seq", perm=[(i, i ^ bit) for i in range(seqs)])

    h_up, h_down = up(embeddings[:, rows - near :]), down(embeddings[:, :near])
    q_up, q_down = up(cotangent[:, rows - far :]), down(cotangent[:, :far])

    s0, z0 = kernel_call(
        first_body, [embeddings, kernels[0]], [shape(own), shape(own, F32)], conv_flops
    )
    (qx,) = kernel_call(
        partial(extend_body, seqs), [q_up, cotangent, q_down], [shape((batches, rows + 2 * far, channels))]
    )
    qx2 = swap(qx)
    half = channels // 2
    h1, s1, s1_keep, s1_send, s0_keep, s0_send = kernel_call(
        second_body,
        [z0, embeddings, s0, h_up, h_down, kernels[0]],
        [
            shape(own),
            shape(own),
            shape((batches, rows, half)),
            shape((batches, rows, half)),
            shape((batches, rows + 2 * near, half)),
            shape((batches, rows + 2 * near, half)),
        ],
        conv_flops // 10,
        where,
    )
    s1_other, s0_other = swap(s1_send), swap(s0_send)

    blocks = (2, 3, half // 2, half)

    def grad(taps_of_s, s, s2, q, q2):
        return kernel_call(
            partial(grad_body, taps_of_s),
            [s, s2, q, q2],
            [shape(blocks, F32), shape(blocks)],
            conv_flops,
            where,
            [pltpu.VMEM((3, 2, 2, half // 2, half), F32)],
        )

    count = seqs // 2
    strip = 3 * (half // 2) // count
    woven = strip % 16 == 0
    turn = jnp.where(dp % 2 == 0, seq % 2, (dp // 2) % 2)
    factor = 1.0 / math.sqrt(batches * dps * rows * seqs)

    def reduced(keep, send):
        got = crossed(True)(send)
        total = keep + got.astype(F32)
        keep, send = pick(total, turn, 0), pick(total, 1 - turn, 0).astype(BF16)
        got = crossed(False)(send)
        if woven:
            (total,) = kernel_call(
                partial(weave_body, count), [keep, got], [shape((count, strip, half), F32)]
            )
        else:
            total = (keep + got.astype(F32)).reshape(count, strip, count, half // count)
            total = total.transpose(2, 1, 0, 3).reshape(count, strip, half)
        bit = 1
        while 2 * bit < seqs:
            mine = (seq // (2 * bit)) % 2
            pairs = total.reshape(total.shape[0] // 2, 2, strip, half)
            keep, send = pick(pairs, mine, 1), pick(pairs, 1 - mine, 1).astype(BF16)
            got = along(2 * bit)(send)
            bit *= 2
            if 2 * bit < seqs:
                total = keep + got.astype(F32)
        final = (3, half // 2, half // count)
        if woven:
            (out,) = kernel_call(partial(unweave_body, count, factor), [keep[0], got[0]], [shape(final, F32)])
            return out
        total = (keep[0] + got[0].astype(F32)) * factor
        return total.reshape(strip, count, half // count).transpose(1, 0, 2).reshape(final)

    keep1, send1 = grad(False, s1_keep, s1_other, qx, qx2)
    grad1 = reduced(keep1, send1)

    g1, q0, q0_mixed = kernel_call(
        partial(back_body, seqs),
        [cotangent, q_up, q_down, kernels[1], h1],
        [shape(own, F32), shape(own), shape(own)],
        conv_flops,
    )
    q0_other = swap(q0_mixed)
    keep0, send0 = grad(True, s0_keep, s0_other, q0_mixed, q0_other)
    grad0 = reduced(keep0, send0)

    s1_up, s1_down = up(s1[:, rows - far :]), down(s1[:, :far])
    q0_up, q0_down = up(q0[:, rows - near :]), down(q0[:, :near])
    (out,) = kernel_call(last_body, [s1, s1_up, s1_down, kernels[1], h1], [shape(own)], conv_flops)
    (grad_in,) = kernel_call(
        last_back_body, [q0, q0_up, q0_down, kernels[0], embeddings, g1], [shape(own)], conv_flops
    )
    return out, grad_in, jnp.stack([grad0, grad1])


def solution(mesh):
    placed = (P("dp", "seq", None), P(), P("dp", "seq", None))
    return jax.shard_map(
        per_device,
        mesh=mesh,
        in_specs=placed,
        out_specs=(P("dp", "seq", None), P("dp", "seq", None), P(None, None, "dp", "seq")),
        check_vma=False,
    )
```

time: 327 us -> 122 us (0.37)
  waiting for transfers between devices: 212 us -> 25.6 us
  Pallas kernels: 0 us -> 31.9 us
  matrix products: 22.9 us -> 0 us
  other arithmetic: 22.7 us -> 2.61 us
  starting transfers between devices: 25.5 us -> 39.7 us
  between operations: 14.2 us -> 0.98 us
  local copies, waits for them, and re-layouts: 28.6 us -> 19.1 us
    unnamed x6 -> x0, waiting for transfers between devices: 121 us -> none
    reduce_scatter x2 -> x0, waiting for transfers between devices: 87 us -> none  [per_device(): lax.psum_scatter(partial_grad, 'dp', scatter_dimension=1, tiled=True)]
    pallas_call x0 -> x12, Pallas kernels: none -> 31.9 us  [kernel_call(): pl.pallas_call(body, out_shape=tuple(outs), in_specs=specs, out_specs=tup...]
    dot_general x18 -> x0, matrix products: 22.9 us -> none  [the longest x12 16.2 us: dilated(): jnp.dot(window, weight[kernel_tap], preferred_element_type=jnp.float32)]
    ppermute x8 -> x20, waiting for transfers between devices: 4.13 us -> 25.6 us  [the longest x4 10.4 us: reduced(): got = along(2 * bit)(send)]
    ppermute x8 -> x20, starting transfers between devices: 25.1 us -> 39.7 us  [the longest x2 6.78 us: per_device(): h_up, h_down = (up(embeddings[:, rows - near:]), down(embeddings[:, :near]))]
    unnamed x30 -> x44, local copies, waits for them, and re-layouts: 21.7 us -> 10 us
    convert_element_type x4 -> x0, other arithmetic: 9.38 us -> none  [the longest x1 4.5 us: per_device(): return (current, grad_h.astype(jnp.bfloat16), jnp.stack(grads))]
  transfers between devices with their start and end apart: 12 -> 20, of which waited for: 6 -> 6; matrix products, arithmetic and copies ran while one was open for 17% -> 8% of each run, Pallas kernels for 0% -> 22%
where the time goes in v1:
time: 122 us; the launch traced here: 120 us
  starting transfers between devices  39.7 us (33%)
  Pallas kernels  31.9 us (26%)
  waiting for transfers between devices  25.6 us (21%)
  local copies, waits for them, and re-layouts  19.1 us (16%)
  other arithmetic  2.61 us (2%)
    pallas_call x12, Pallas kernels, kernel_call(): pl.pallas_call(body, out_shape=tuple(outs), in_specs=specs, out_specs=tup...  31.9 us
    ppermute x4, waiting for transfers between devices, reduced(): got = along(2 * bit)(send)  10.4 us
    ppermute x2, waiting for transfers between devices, reduced(): got = crossed(False)(send)  10.2 us
    unnamed x44, local copies, waits for them, and re-layouts  10 us
    ppermute x2, starting transfers between devices, per_device(): h_up, h_down = (up(embeddings[:, rows - near:]), down(embeddings[:, :near]))  6.78 us
    ppermute x4, starting transfers between devices, reduced(): got = along(2 * bit)(send)  6.65 us
    ppermute x2, starting transfers between devices, per_device(): q_up, q_down = (up(cotangent[:, rows - far:]), down(cotangent[:, :far]))  6.62 us
    ppermute x2, starting transfers between devices, per_device(): q0_up, q0_down = (up(q0[:, rows - near:]), down(q0[:, :near]))  5.88 us
  transfers between devices with their start and end apart: 20, of which 6 were waited for; matrix products, arithmetic and copies ran while one was open for 8% of the time, Pallas kernels for 22%

profile of v1, /device:TPU:0, one launch (start us, length us, event | category | flops | bytes accessed | tf_op | source)
XLA Modules:
  0.0 120.0 jit_solution(11968037808825876850)
XLA Ops:
  0.6 1.6 %fusion.7 = (bf16[6,8,768]{2,1,0:T(8,128)(2,1)}, bf16[6,8,768]{2,1,0:T(8,128)(2,1)}) fusion(bf16[6,96,768]{2,1,0:T(8,128)(2,1)} %h_ref.5), kind=kLoop, calls=%fused_computation.25 | loop fusion | bytes 294912 | tf_op jit(solution)/shard_map/slice | solution.py:247
  2.2 5.5 %collective-permute-start = (bf16[6,8,768]{2,1,0:T(8,128)(2,1)}, bf16[6,8,768]{2,1,0:T(8,128)(2,1)}, u32[]{:S(2)}, u32[]{:S(2)}) collective-permute-start(bf16[6,8,768]{2,1,0:T(8,128)(2,1)} %get-tuple-element.42), channel_id=1, source_target_pairs={{0,4},{4,8},{8,12},{12,16},{16,20},{20,24},{24,28},{1,5},{5,9},{9,... | collective-permute-start | bytes 221192 | tf_op jit(solution)/shard_map/ppermute | solution.py:247
  7.7 1.3 %collective-permute-start.1 = (bf16[6,8,768]{2,1,0:T(8,128)(2,1)}, bf16[6,8,768]{2,1,0:T(8,128)(2,1)}, u32[]{:S(2)}, u32[]{:S(2)}) collective-permute-start(bf16[6,8,768]{2,1,0:T(8,128)(2,1)} %get-tuple-element.41), channel_id=1, source_target_pairs={{4,0},{8,4},{12,8},{16,12},{20,16},{24,20},{28,24},{5,1},{9,5},{13... | collective-permute-start | bytes 221192 | tf_op jit(solution)/shard_map/ppermute | solution.py:247
  9.0 1.7 %fusion.5 = (bf16[6,16,768]{2,1,0:T(8,128)(2,1)}, bf16[6,16,768]{2,1,0:T(8,128)(2,1)}) fusion(bf16[6,96,768]{2,1,0:T(8,128)(2,1)} %own_ref.1), kind=kLoop, calls=%fused_computation.23 | loop fusion | bytes 589824 | tf_op jit(solution)/shard_map/slice | solution.py:248
  10.7 5.2 %collective-permute-start.4 = (bf16[6,16,768]{2,1,0:T(8,128)(2,1)}, bf16[6,16,768]{2,1,0:T(8,128)(2,1)}, u32[]{:S(2)}, u32[]{:S(2)}) collective-permute-start(bf16[6,16,768]{2,1,0:T(8,128)(2,1)} %get-tuple-element.38), channel_id=1, source_target_pairs={{0,4},{4,8},{8,12},{12,16},{16,20},{20,24},{24,28},{1,5},{5,9},{9,... | collective-permute-start | bytes 442376 | tf_op jit(solution)/shard_map/ppermute | solution.py:248
  15.9 1.4 %collective-permute-start.5 = (bf16[6,16,768]{2,1,0:T(8,128)(2,1)}, bf16[6,16,768]{2,1,0:T(8,128)(2,1)}, u32[]{:S(2)}, u32[]{:S(2)}) collective-permute-start(bf16[6,16,768]{2,1,0:T(8,128)(2,1)} %get-tuple-element.37), channel_id=1, source_target_pairs={{4,0},{8,4},{12,8},{16,12},{20,16},{24,20},{28,24},{5,1},{9,5},{13... | collective-permute-start | bytes 442376 | tf_op jit(solution)/shard_map/ppermute | solution.py:248
  17.3 5.3 %slice_bitcast_fusion = (bf16[3,768,768]{2,1,0:T(8,128)(2,1)}, bf16[3,768,768]{2,1,0:T(8,128)(2,1)S(1)}) fusion(bf16[2,3,768,768]{3,2,1,0:T(8,128)(2,1)} %param.4), kind=kLoop, calls=%fused_computation | loop fusion | bytes 14155776 | tf_op jit(solution)/shard_map/squeeze | solution.py:335
  22.6 2.7 %shard_map.58 = (bf16[6,96,768]{2,1,0:T(8,128)(2,1)S(1)}, f32[6,96,768]{2,1,0:T(8,128)S(1)}) custom-call(bf16[6,96,768]{2,1,0:T(8,128)(2,1)S(1)} %copy-done, bf16[3,768,768]{2,1,0:T(8,128)(2,1)S(1)} %get-tuple-element.34.w_ref), custom_call_target="tpu_custom_call" | custom-call | flops 2038431744 | bytes 7077888 | tf_op jit(solution)/shard_map/pallas_call | solution.py:27
  28.8 1.5 %copy-done.6 = f32[6,96,768]{2,1,0:T(8,128)S(1)} copy-done((f32[6,96,768]{2,1,0:T(8,128)S(1)}, f32[6,96,768]{2,1,0:T(8,128)}, u32[]{:S(2)}) %copy-start.6) | copy-done | bytes 1769496
  31.4 3.3 %shard_map.59 = (bf16[6,96,768]{2,1,0:T(8,128)(2,1)S(1)}, bf16[6,96,768]{2,1,0:T(8,128)(2,1)S(1)}, bf16[6,96,384]{2,1,0:T(8,128)(2,1)S(1)}, bf16[6,96,384]{2,1,0...) custom-call(s32[3]{0:T(128)S(1)} %pad_add_fusion.where_ref, ...), custom_call_target="tpu_custom_call" | custom-call | flops 203843168 | bytes 10911744 | tf_op jit(solution)/shard_map/pallas_call | solution.py:27
  35.7 5.3 %shard_map.61 = (f32[6,96,768]{2,1,0:T(8,128)S(1)}, bf16[6,96,768]{2,1,0:T(8,128)(2,1)S(1)}, bf16[6,96,768]{2,1,0:T(8,128)(2,1)S(1)}) custom-call(bf16[6,96,768]{2,1,0:T(8,128)(2,1)S(1)} %copy-done.11, bf16[6,16,768]{2,1,0:T(8,128)(2,1)} %collective-permute-done.4.up_ref, bf16[6,16,768]{2,1,0:T(8,128)(2,1)} %collective-permute-done.5.down_ref, ...), custom_call_target="tpu_custom_call" | custom-call | flops 2038431744 | bytes 9142272 | tf_op jit(solution)/shard_map/pallas_call | solution.py:27
  42.0 2.9 %shard_map.66.q_ref = bf16[6,128,768]{2,1,0:T(8,128)(2,1)} custom-call(bf16[6,16,768]{2,1,0:T(8,128)(2,1)} %collective-permute-done.4.up_ref, bf16[6,96,768]{2,1,0:T(8,128)(2,1)S(1)} %copy-done.11, bf16[6,16,768]{2,1,0:T(8,128)(2,1)} %collective-permute-done.5.down_ref), custom_call_target="tpu_custom_call" | custom-call | bytes 2359296 | tf_op jit(solution)/shard_map/pallas_call | solution.py:27
  45.6 3.5 %collective-permute-done.8.s2_ref = bf16[6,112,384]{2,1,0:T(8,128)(2,1)S(1)} collective-permute-done((bf16[6,112,384]{2,1,0:T(8,128)(2,1)S(1)}, bf16[6,112,384]{2,1,0:T(8,128)(2,1)S(1)}, u32[]{:S(2)}, u32[]{:S(2)}) %collective-permute-start.8) | collective-permute-done | bytes 516128 | tf_op jit(solution)/shard_map/ppermute | solution.py:272
  49.1 4.2 %shard_map.63 = (f32[2,3,192,384]{3,2,1,0:T(8,128)S(1)}, bf16[2,3,192,384]{3,2,1,0:T(8,128)(2,1)}) custom-call(s32[3]{0:T(128)S(1)} %pad_add_fusion.where_ref, bf16[6,112,384]{2,1,0:T(8,128)(2,1)S(1)} %get-tuple-element.24.s_ref, bf16[6,112,384]{2,1,0:T(8,128)(2,1)S(1)} %collective-permute-done.8.s2_ref, bf16[6,96,768]{2,1,0:T(8,128)(2,1)S(1)} %get-tuple-element.26.q_ref, ...), custom_call_target="tpu_custom_call" | custom-call | flops 2038431744 | bytes 5455872 | tf_op jit(solution)/shard_map/pallas_call | solution.py:27
  54.5 1.5 %collective-permute-start.10 = (bf16[2,3,192,384]{3,2,1,0:T(8,128)(2,1)}, bf16[2,3,192,384]{3,2,1,0:T(8,128)(2,1)}, u32[]{:S(2)}, u32[]{:S(2)}) collective-permute-start(bf16[2,3,192,384]{3,2,1,0:T(8,128)(2,1)} %get-tuple-element.28), channel_id=1, source_target_pairs={{0,2},{1,5},{2,0},{3,7},{4,6},{5,1},{6,4},{7,3},{8,10},{9,13},{10,... | collective-permute-start | bytes 2654216 | tf_op jit(solution)/shard_map/ppermute | solution.py:293
  57.0 4.8 %shard_map.67 = (f32[2,3,192,384]{3,2,1,0:T(8,128)S(1)}, bf16[2,3,192,384]{3,2,1,0:T(8,128)(2,1)S(1)}) custom-call(s32[3]{0:T(128)S(1)} %pad_add_fusion.where_ref, bf16[6,96,384]{2,1,0:T(8,128)(2,1)S(1)} %copy-done.21, bf16[6,96,384]{2,1,0:T(8,128)(2,1)} %collective-permute-done.14.s2_ref, bf16[6,128,768]{2,1,0:T(8,128)(2,1)} %shard_map.66.q_ref, ...), custom_call_target="tpu_custom_call" | custom-call | flops 2038431744 | bytes 5898240 | tf_op jit(solution)/shard_map/pallas_call | solution.py:27
  62.5 4.6 %collective-permute-start.2 = (bf16[6,16,768]{2,1,0:T(8,128)(2,1)S(1)}, bf16[6,16,768]{2,1,0:T(8,128)(2,1)S(1)}, u32[]{:S(2)}, u32[]{:S(2)}) collective-permute-start(bf16[6,16,768]{2,1,0:T(8,128)(2,1)S(1)} %get-tuple-element.40), channel_id=1, source_target_pairs={{0,4},{4,8},{8,12},{12,16},{16,20},{20,24},{24,28},{1,5},{5,9},{9,... | collective-permute-start | bytes 442376 | tf_op jit(solution)/shard_map/ppermute | solution.py:333
  67.0 1.3 %collective-permute-start.3 = (bf16[6,16,768]{2,1,0:T(8,128)(2,1)S(1)}, bf16[6,16,768]{2,1,0:T(8,128)(2,1)S(1)}, u32[]{:S(2)}, u32[]{:S(2)}) collective-permute-start(bf16[6,16,768]{2,1,0:T(8,128)(2,1)S(1)} %get-tuple-element.39), channel_id=1, source_target_pairs={{4,0},{8,4},{12,8},{16,12},{20,16},{24,20},{28,24},{5,1},{9,5},{13... | collective-permute-start | bytes 442376 | tf_op jit(solution)/shard_map/ppermute | solution.py:333
  68.4 4.6 %collective-permute-start.6 = (bf16[6,8,768]{2,1,0:T(8,128)(2,1)S(1)}, bf16[6,8,768]{2,1,0:T(8,128)(2,1)S(1)}, u32[]{:S(2)}, u32[]{:S(2)}) collective-permute-start(bf16[6,8,768]{2,1,0:T(8,128)(2,1)S(1)} %get-tuple-element.36), channel_id=1, source_target_pairs={{0,4},{4,8},{8,12},{12,16},{16,20},{20,24},{24,28},{1,5},{5,9},{9,... | collective-permute-start | bytes 221192 | tf_op jit(solution)/shard_map/ppermute | solution.py:334
  73.0 1.3 %collective-permute-start.7 = (bf16[6,8,768]{2,1,0:T(8,128)(2,1)S(1)}, bf16[6,8,768]{2,1,0:T(8,128)(2,1)S(1)}, u32[]{:S(2)}, u32[]{:S(2)}) collective-permute-start(bf16[6,8,768]{2,1,0:T(8,128)(2,1)S(1)} %get-tuple-element.35), channel_id=1, source_target_pairs={{4,0},{8,4},{12,8},{16,12},{20,16},{24,20},{28,24},{5,1},{9,5},{13... | collective-permute-start | bytes 221192 | tf_op jit(solution)/shard_map/ppermute | solution.py:334
  74.3 1.4 %convert_add_fusion.1 = f32[2,3,192,384]{3,2,1,0:T(8,128)S(1)} fusion(f32[2,3,192,384]{3,2,1,0:T(8,128)S(1)} %copy-done.8, bf16[2,3,192,384]{3,2,1,0:T(8,128)(2,1)} %collective-permute-done.10), kind=kLoop, calls=%fused_computation.3 | loop fusion | flops 884736 | bytes 4423680 | tf_op jit(solution)/shard_map/add | solution.py:294
  75.8 1.5 %collective-permute-done.16 = bf16[2,3,192,384]{3,2,1,0:T(8,128)(2,1)S(1)} collective-permute-done((bf16[2,3,192,384]{3,2,1,0:T(8,128)(2,1)S(1)}, bf16[2,3,192,384]{3,2,1,0:T(8,128)(2,1)S(1)}, u32[]{:S(2)}, u32[]{:S(2)}) %collective-permute-start.16) | collective-permute-done | bytes 884768 | tf_op jit(solution)/shard_map/ppermute | solution.py:293
  77.2 2.6 %collective-permute-start.11 = (bf16[3,192,384]{2,1,0:T(8,128)(2,1)S(1)}, bf16[3,192,384]{2,1,0:T(8,128)(2,1)S(1)}, u32[]{:S(2)}, u32[]{:S(2)}) collective-permute-start(bf16[3,192,384]{2,1,0:T(8,128)(2,1)S(1)} %fusion), channel_id=1, source_target_pairs={{0,4},{1,3},{2,6},{3,1},{4,0},{5,7},{6,2},{7,5},{8,12},{9,11},{10,... | collective-permute-start | bytes 1327112 | tf_op jit(solution)/shard_map/ppermute | solution.py:296
  80.4 10.2 %collective-permute-done.11.got_ref = bf16[3,192,384]{2,1,0:T(8,128)(2,1)S(1)} collective-permute-done((bf16[3,192,384]{2,1,0:T(8,128)(2,1)S(1)}, bf16[3,192,384]{2,1,0:T(8,128)(2,1)S(1)}, u32[]{:S(2)}, u32[]{:S(2)}) %collective-permute-start.11) | collective-permute-done | bytes 442400 | tf_op jit(solution)/shard_map/ppermute | solution.py:296
  90.5 2.5 %collective-permute-start.17 = (bf16[3,192,384]{2,1,0:T(8,128)(2,1)S(1)}, bf16[3,192,384]{2,1,0:T(8,128)(2,1)S(1)}, u32[]{:S(2)}, u32[]{:S(2)}) collective-permute-start(bf16[3,192,384]{2,1,0:T(8,128)(2,1)S(1)} %fusion.1), channel_id=1, source_target_pairs={{0,4},{1,3},{2,6},{3,1},{4,0},{5,7},{6,2},{7,5},{8,12},{9,11},{10,... | collective-permute-start | bytes 1327112 | tf_op jit(solution)/shard_map/ppermute | solution.py:296
  93.5 1.3 %collective-permute-start.12 = (bf16[2,144,384]{2,1,0:T(8,128)(2,1)S(1)}, bf16[2,144,384]{2,1,0:T(8,128)(2,1)S(1)}, u32[]{:S(2)}, u32[]{:S(2)}) collective-permute-start(bf16[2,144,384]{2,1,0:T(8,128)(2,1)S(1)} %fusion.2), channel_id=1, source_target_pairs={{0,8},{4,12},{8,0},{12,4},{16,24},{20,28},{24,16},{28,20},{1,9},{5... | collective-permute-start | bytes 663560 | tf_op jit(solution)/shard_map/ppermute | solution.py:309
  94.8 3.1 %shard_map.60 = bf16[6,96,768]{2,1,0:T(8,128)(2,1)} custom-call(bf16[6,96,768]{2,1,0:T(8,128)(2,1)S(1)} %copy-done.17, bf16[6,16,768]{2,1,0:T(8,128)(2,1)S(1)} %collective-permute-done.2.up_ref, bf16[6,16,768]{2,1,0:T(8,128)(2,1)S(1)} %collective-permute-done.3.down_ref, bf16[3,768,768]{2,1,0:T(8,128)(2,1)S(1)} %copy-done.4, bf16[6,96,768]{2,1,0:T(8,128)(2,1)S(1)} %copy-done.19), custom_call_target="tpu_custom_call" | custom-call | flops 2038431744 | bytes 6488064 | tf_op jit(solution)/shard_map/pallas_call | solution.py:27
  97.9 4.4 %shard_map.62 = bf16[6,96,768]{2,1,0:T(8,128)(2,1)} custom-call(bf16[6,96,768]{2,1,0:T(8,128)(2,1)S(1)} %copy-done.13, bf16[6,8,768]{2,1,0:T(8,128)(2,1)S(1)} %collective-permute-done.6.up_ref, bf16[6,8,768]{2,1,0:T(8,128)(2,1)S(1)} %collective-permute-done.7.down_ref, bf16[3,768,768]{2,1,0:T(8,128)(2,1)S(1)} %get-tuple-element.34.w_ref, ...), custom_call_target="tpu_custom_call" | custom-call | flops 2038431744 | bytes 8110080 | tf_op jit(solution)/shard_map/pallas_call | solution.py:27
  103.7 2.3 %collective-permute-start.13 = (bf16[1,144,384]{2,1,0:T(8,128)(2,1)S(1)}, bf16[1,144,384]{2,1,0:T(8,128)(2,1)S(1)}, u32[]{:S(2)}, u32[]{:S(2)}) collective-permute-start(bf16[1,144,384]{2,1,0:T(8,128)(2,1)S(1)} %dynamic-slice_convert_fusion.3), channel_id=1, source_target_pairs={{0,16},{4,20},{8,24},{12,28},{16,0},{20,4},{24,8},{28,12},{1,17},{... | collective-permute-start | bytes 331784 | tf_op jit(solution)/shard_map/ppermute | solution.py:309
  106.0 4.1 %collective-permute-done.13 = bf16[1,144,384]{2,1,0:T(8,128)(2,1)S(1)} collective-permute-done((bf16[1,144,384]{2,1,0:T(8,128)(2,1)S(1)}, bf16[1,144,384]{2,1,0:T(8,128)(2,1)S(1)}, u32[]{:S(2)}, u32[]{:S(2)}) %collective-permute-start.13) | collective-permute-done | bytes 110624 | tf_op jit(solution)/shard_map/ppermute | solution.py:309
  111.7 2.2 %collective-permute-start.19 = (bf16[1,144,384]{2,1,0:T(8,128)(2,1)S(1)}, bf16[1,144,384]{2,1,0:T(8,128)(2,1)S(1)}, u32[]{:S(2)}, u32[]{:S(2)}) collective-permute-start(bf16[1,144,384]{2,1,0:T(8,128)(2,1)S(1)} %dynamic-slice_convert_fusion.2), channel_id=1, source_target_pairs={{0,16},{4,20},{8,24},{12,28},{16,0},{20,4},{24,8},{28,12},{1,17},{... | collective-permute-start | bytes 331784 | tf_op jit(solution)/shard_map/ppermute | solution.py:309
  113.9 5.1 %collective-permute-done.19 = bf16[1,144,384]{2,1,0:T(8,128)(2,1)S(1)} collective-permute-done((bf16[1,144,384]{2,1,0:T(8,128)(2,1)S(1)}, bf16[1,144,384]{2,1,0:T(8,128)(2,1)S(1)}, u32[]{:S(2)}, u32[]{:S(2)}) %collective-permute-start.19) | collective-permute-done | bytes 110624 | tf_op jit(solution)/shard_map/ppermute | solution.py:309
  (84 shorter events, 14.9 us)
Async XLA Ops:
  2.2 25.4 %collective-permute-start = (bf16[6,8,768]{2,1,0:T(8,128)(2,1)}, bf16[6,8,768]{2,1,0:T(8,128)(2,1)}, u32[]{:S(2)}, u32[]{:S(2)}) collective-permute-start(bf16[6,8,768]{2,1,0:T(8,128)(2,1)} %get-tuple-element.42), channel_id=1, source_target_pairs={{0,4},{4,8},{8,12},{12,16},{16,20},{20,24},{24,28},{1,5},{5,9},{9,... | collective-permute-start | bytes 221192 | tf_op jit(solution)/shard_map/ppermute | solution.py:247
  7.7 19.9 %collective-permute-start.1 = (bf16[6,8,768]{2,1,0:T(8,128)(2,1)}, bf16[6,8,768]{2,1,0:T(8,128)(2,1)}, u32[]{:S(2)}, u32[]{:S(2)}) collective-permute-start(bf16[6,8,768]{2,1,0:T(8,128)(2,1)} %get-tuple-element.41), channel_id=1, source_target_pairs={{4,0},{8,4},{12,8},{16,12},{20,16},{24,20},{28,24},{5,1},{9,5},{13... | collective-permute-start | bytes 221192 | tf_op jit(solution)/shard_map/ppermute | solution.py:247
  10.7 25.0 %collective-permute-start.4 = (bf16[6,16,768]{2,1,0:T(8,128)(2,1)}, bf16[6,16,768]{2,1,0:T(8,128)(2,1)}, u32[]{:S(2)}, u32[]{:S(2)}) collective-permute-start(bf16[6,16,768]{2,1,0:T(8,128)(2,1)} %get-tuple-element.38), channel_id=1, source_target_pairs={{0,4},{4,8},{8,12},{12,16},{16,20},{20,24},{24,28},{1,5},{5,9},{9,... | collective-permute-start | bytes 442376 | tf_op jit(solution)/shard_map/ppermute | solution.py:248
  15.9 6.7 %copy-start = (bf16[6,96,768]{2,1,0:T(8,128)(2,1)S(1)}, bf16[6,96,768]{2,1,0:T(8,128)(2,1)}, u32[]{:S(2)}) copy-start(bf16[6,96,768]{2,1,0:T(8,128)(2,1)} %h_ref.5) | copy-start | bytes 2654212
  15.9 19.8 %collective-permute-start.5 = (bf16[6,16,768]{2,1,0:T(8,128)(2,1)}, bf16[6,16,768]{2,1,0:T(8,128)(2,1)}, u32[]{:S(2)}, u32[]{:S(2)}) collective-permute-start(bf16[6,16,768]{2,1,0:T(8,128)(2,1)} %get-tuple-element.37), channel_id=1, source_target_pairs={{4,0},{8,4},{12,8},{16,12},{20,16},{24,20},{28,24},{5,1},{9,5},{13... | collective-permute-start | bytes 442376 | tf_op jit(solution)/shard_map/ppermute | solution.py:248
  31.4 4.3 %copy-start.11 = (bf16[6,96,768]{2,1,0:T(8,128)(2,1)S(1)}, bf16[6,96,768]{2,1,0:T(8,128)(2,1)}, u32[]{:S(2)}) copy-start(bf16[6,96,768]{2,1,0:T(8,128)(2,1)} %own_ref.1) | copy-start | bytes 2654212
  35.7 5.4 %copy-start.18 = (bf16[6,96,768]{2,1,0:T(8,128)(2,1)}, bf16[6,96,768]{2,1,0:T(8,128)(2,1)S(1)}, u32[]{:S(2)}) copy-start(bf16[6,96,768]{2,1,0:T(8,128)(2,1)S(1)} %get-tuple-element.21.h_ref) | copy-start | bytes 2654212
  35.7 5.4 %copy-start.20 = (bf16[6,96,384]{2,1,0:T(8,128)(2,1)}, bf16[6,96,384]{2,1,0:T(8,128)(2,1)S(1)}, u32[]{:S(2)}) copy-start(bf16[6,96,384]{2,1,0:T(8,128)(2,1)S(1)} %get-tuple-element.29.s_ref) | copy-start | bytes 1327108
  42.0 11.3 %copy-start.9 = (f32[6,96,768]{2,1,0:T(8,128)}, f32[6,96,768]{2,1,0:T(8,128)S(1)}, u32[]{:S(2)}) copy-start(f32[6,96,768]{2,1,0:T(8,128)S(1)} %get-tuple-element.23.g_ref) | copy-start | bytes 5308420
  42.0 7.2 %collective-permute-start.9 = (bf16[6,96,768]{2,1,0:T(8,128)(2,1)S(1)}, bf16[6,96,768]{2,1,0:T(8,128)(2,1)S(1)}, u32[]{:S(2)}, u32[]{:S(2)}) collective-permute-start(bf16[6,96,768]{2,1,0:T(8,128)(2,1)S(1)} %get-tuple-element.26.q_ref), channel_id=1, source_target_pairs={{0,1},{1,0},{2,3},{3,2},{4,5},{5,4},{6,7},{7,6},{8,9},{9,8},{10,11... | collective-permute-start | bytes 2654216 | tf_op jit(solution)/shard_map/ppermute | solution.py:329
  44.9 11.1 %collective-permute-start.15 = (bf16[6,128,768]{2,1,0:T(8,128)(2,1)}, bf16[6,128,768]{2,1,0:T(8,128)(2,1)}, u32[]{:S(2)}, u32[]{:S(2)}) collective-permute-start(bf16[6,128,768]{2,1,0:T(8,128)(2,1)} %shard_map.66.q_ref), channel_id=1, source_target_pairs={{0,1},{1,0},{2,3},{3,2},{4,5},{5,4},{6,7},{7,6},{8,9},{9,8},{10,11... | collective-permute-start | bytes 3538952 | tf_op jit(solution)/shard_map/ppermute | solution.py:256
  45.1 4.0 %collective-permute-start.8 = (bf16[6,112,384]{2,1,0:T(8,128)(2,1)S(1)}, bf16[6,112,384]{2,1,0:T(8,128)(2,1)S(1)}, u32[]{:S(2)}, u32[]{:S(2)}) collective-permute-start(bf16[6,112,384]{2,1,0:T(8,128)(2,1)S(1)} %get-tuple-element.25), channel_id=1, source_target_pairs={{0,1},{1,0},{2,3},{3,2},{4,5},{5,4},{6,7},{7,6},{8,9},{9,8},{10,11... | collective-permute-start | bytes 1548296 | tf_op jit(solution)/shard_map/ppermute | solution.py:272
  45.4 10.6 %collective-permute-start.14 = (bf16[6,96,384]{2,1,0:T(8,128)(2,1)}, bf16[6,96,384]{2,1,0:T(8,128)(2,1)}, u32[]{:S(2)}, u32[]{:S(2)}) collective-permute-start(bf16[6,96,384]{2,1,0:T(8,128)(2,1)} %get-tuple-element.30), channel_id=1, source_target_pairs={{0,1},{1,0},{2,3},{3,2},{4,5},{5,4},{6,7},{7,6},{8,9},{9,8},{10,11... | collective-permute-start | bytes 1327112 | tf_op jit(solution)/shard_map/ppermute | solution.py:272
  54.5 18.5 %collective-permute-start.10 = (bf16[2,3,192,384]{3,2,1,0:T(8,128)(2,1)}, bf16[2,3,192,384]{3,2,1,0:T(8,128)(2,1)}, u32[]{:S(2)}, u32[]{:S(2)}) collective-permute-start(bf16[2,3,192,384]{3,2,1,0:T(8,128)(2,1)} %get-tuple-element.28), channel_id=1, source_target_pairs={{0,2},{1,5},{2,0},{3,7},{4,6},{5,1},{6,4},{7,3},{8,10},{9,13},{10,... | collective-permute-start | bytes 2654216 | tf_op jit(solution)/shard_map/ppermute | solution.py:293
  57.0 5.4 %copy-start.17 = (bf16[6,96,768]{2,1,0:T(8,128)(2,1)S(1)}, bf16[6,96,768]{2,1,0:T(8,128)(2,1)}, u32[]{:S(2)}) copy-start(bf16[6,96,768]{2,1,0:T(8,128)(2,1)} %copy-done.16) | copy-start | bytes 2654212
  57.0 11.3 %copy-start.13 = (bf16[6,96,768]{2,1,0:T(8,128)(2,1)S(1)}, bf16[6,96,768]{2,1,0:T(8,128)(2,1)}, u32[]{:S(2)}) copy-start(bf16[6,96,768]{2,1,0:T(8,128)(2,1)} %copy-done.12) | copy-start | bytes 2654212
  57.0 17.3 %copy-start.8 = (f32[2,3,192,384]{3,2,1,0:T(8,128)S(1)}, f32[2,3,192,384]{3,2,1,0:T(8,128)}, u32[]{:S(2)}) copy-start(f32[2,3,192,384]{3,2,1,0:T(8,128)} %copy-done.7) | copy-start | bytes 5308420
  61.9 15.4 %collective-permute-start.16 = (bf16[2,3,192,384]{3,2,1,0:T(8,128)(2,1)S(1)}, bf16[2,3,192,384]{3,2,1,0:T(8,128)(2,1)S(1)}, u32[]{:S(2)}, u32[]{:S(2)}) collective-permute-start(bf16[2,3,192,384]{3,2,1,0:T(8,128)(2,1)S(1)} %get-tuple-element.32), channel_id=1, source_target_pairs={{0,2},{1,5},{2,0},{3,7},{4,6},{5,1},{6,4},{7,3},{8,10},{9,13},{10,... | collective-permute-start | bytes 2654216 | tf_op jit(solution)/shard_map/ppermute | solution.py:293
  62.5 31.0 %collective-permute-start.2 = (bf16[6,16,768]{2,1,0:T(8,128)(2,1)S(1)}, bf16[6,16,768]{2,1,0:T(8,128)(2,1)S(1)}, u32[]{:S(2)}, u32[]{:S(2)}) collective-permute-start(bf16[6,16,768]{2,1,0:T(8,128)(2,1)S(1)} %get-tuple-element.40), channel_id=1, source_target_pairs={{0,4},{4,8},{8,12},{12,16},{16,20},{20,24},{24,28},{1,5},{5,9},{9,... | collective-permute-start | bytes 442376 | tf_op jit(solution)/shard_map/ppermute | solution.py:333
  67.0 27.7 %collective-permute-start.3 = (bf16[6,16,768]{2,1,0:T(8,128)(2,1)S(1)}, bf16[6,16,768]{2,1,0:T(8,128)(2,1)S(1)}, u32[]{:S(2)}, u32[]{:S(2)}) collective-permute-start(bf16[6,16,768]{2,1,0:T(8,128)(2,1)S(1)} %get-tuple-element.39), channel_id=1, source_target_pairs={{4,0},{8,4},{12,8},{16,12},{20,16},{24,20},{28,24},{5,1},{9,5},{13... | collective-permute-start | bytes 442376 | tf_op jit(solution)/shard_map/ppermute | solution.py:333
  68.4 29.5 %collective-permute-start.6 = (bf16[6,8,768]{2,1,0:T(8,128)(2,1)S(1)}, bf16[6,8,768]{2,1,0:T(8,128)(2,1)S(1)}, u32[]{:S(2)}, u32[]{:S(2)}) collective-permute-start(bf16[6,8,768]{2,1,0:T(8,128)(2,1)S(1)} %get-tuple-element.36), channel_id=1, source_target_pairs={{0,4},{4,8},{8,12},{12,16},{16,20},{20,24},{24,28},{1,5},{5,9},{9,... | collective-permute-start | bytes 221192 | tf_op jit(solution)/shard_map/ppermute | solution.py:334
  73.0 24.9 %collective-permute-start.7 = (bf16[6,8,768]{2,1,0:T(8,128)(2,1)S(1)}, bf16[6,8,768]{2,1,0:T(8,128)(2,1)S(1)}, u32[]{:S(2)}, u32[]{:S(2)}) collective-permute-start(bf16[6,8,768]{2,1,0:T(8,128)(2,1)S(1)} %get-tuple-element.35), channel_id=1, source_target_pairs={{4,0},{8,4},{12,8},{16,12},{20,16},{24,20},{28,24},{5,1},{9,5},{13... | collective-permute-start | bytes 221192 | tf_op jit(solution)/shard_map/ppermute | solution.py:334
  77.2 13.3 %collective-permute-start.11 = (bf16[3,192,384]{2,1,0:T(8,128)(2,1)S(1)}, bf16[3,192,384]{2,1,0:T(8,128)(2,1)S(1)}, u32[]{:S(2)}, u32[]{:S(2)}) collective-permute-start(bf16[3,192,384]{2,1,0:T(8,128)(2,1)S(1)} %fusion), channel_id=1, source_target_pairs={{0,4},{1,3},{2,6},{3,1},{4,0},{5,7},{6,2},{7,5},{8,12},{9,11},{10,... | collective-permute-start | bytes 1327112 | tf_op jit(solution)/shard_map/ppermute | solution.py:296
  80.1 14.7 %copy-start.19 = (bf16[6,96,768]{2,1,0:T(8,128)(2,1)S(1)}, bf16[6,96,768]{2,1,0:T(8,128)(2,1)}, u32[]{:S(2)}) copy-start(bf16[6,96,768]{2,1,0:T(8,128)(2,1)} %copy-done.18) | copy-start | bytes 2654212
  80.3 14.5 %copy-start.4 = (bf16[3,768,768]{2,1,0:T(8,128)(2,1)S(1)}, bf16[3,768,768]{2,1,0:T(8,128)(2,1)}, u32[]{:S(2)}) copy-start(bf16[3,768,768]{2,1,0:T(8,128)(2,1)} %get-tuple-element.33.w_ref) | copy-start | bytes 10616836
  90.5 11.8 %collective-permute-start.17 = (bf16[3,192,384]{2,1,0:T(8,128)(2,1)S(1)}, bf16[3,192,384]{2,1,0:T(8,128)(2,1)S(1)}, u32[]{:S(2)}, u32[]{:S(2)}) collective-permute-start(bf16[3,192,384]{2,1,0:T(8,128)(2,1)S(1)} %fusion.1), channel_id=1, source_target_pairs={{0,4},{1,3},{2,6},{3,1},{4,0},{5,7},{6,2},{7,5},{8,12},{9,11},{10,... | collective-permute-start | bytes 1327112 | tf_op jit(solution)/shard_map/ppermute | solution.py:296
  93.5 4.5 %copy-start.2 = (bf16[6,96,768]{2,1,0:T(8,128)(2,1)S(1)}, bf16[6,96,768]{2,1,0:T(8,128)(2,1)}, u32[]{:S(2)}) copy-start(bf16[6,96,768]{2,1,0:T(8,128)(2,1)} %h_ref.5) | copy-start | bytes 2654212
  93.5 4.5 %copy-start.10 = (f32[6,96,768]{2,1,0:T(8,128)S(1)}, f32[6,96,768]{2,1,0:T(8,128)}, u32[]{:S(2)}) copy-start(f32[6,96,768]{2,1,0:T(8,128)} %copy-done.9) | copy-start | bytes 5308420
  93.5 8.8 %collective-permute-start.12 = (bf16[2,144,384]{2,1,0:T(8,128)(2,1)S(1)}, bf16[2,144,384]{2,1,0:T(8,128)(2,1)S(1)}, u32[]{:S(2)}, u32[]{:S(2)}) collective-permute-start(bf16[2,144,384]{2,1,0:T(8,128)(2,1)S(1)} %fusion.2), channel_id=1, source_target_pairs={{0,8},{4,12},{8,0},{12,4},{16,24},{20,28},{24,16},{28,20},{1,9},{5... | collective-permute-start | bytes 663560 | tf_op jit(solution)/shard_map/ppermute | solution.py:309
  102.8 8.8 %collective-permute-start.18 = (bf16[2,144,384]{2,1,0:T(8,128)(2,1)S(1)}, bf16[2,144,384]{2,1,0:T(8,128)(2,1)S(1)}, u32[]{:S(2)}, u32[]{:S(2)}) collective-permute-start(bf16[2,144,384]{2,1,0:T(8,128)(2,1)S(1)} %fusion.3), channel_id=1, source_target_pairs={{0,8},{4,12},{8,0},{12,4},{16,24},{20,28},{24,16},{28,20},{1,9},{5... | collective-permute-start | bytes 663560 | tf_op jit(solution)/shard_map/ppermute | solution.py:309
  103.7 6.4 %collective-permute-start.13 = (bf16[1,144,384]{2,1,0:T(8,128)(2,1)S(1)}, bf16[1,144,384]{2,1,0:T(8,128)(2,1)S(1)}, u32[]{:S(2)}, u32[]{:S(2)}) collective-permute-start(bf16[1,144,384]{2,1,0:T(8,128)(2,1)S(1)} %dynamic-slice_convert_fusion.3), channel_id=1, source_target_pairs={{0,16},{4,20},{8,24},{12,28},{16,0},{20,4},{24,8},{28,12},{1,17},{... | collective-permute-start | bytes 331784 | tf_op jit(solution)/shard_map/ppermute | solution.py:309
  111.7 7.3 %collective-permute-start.19 = (bf16[1,144,384]{2,1,0:T(8,128)(2,1)S(1)}, bf16[1,144,384]{2,1,0:T(8,128)(2,1)S(1)}, u32[]{:S(2)}, u32[]{:S(2)}) collective-permute-start(bf16[1,144,384]{2,1,0:T(8,128)(2,1)S(1)} %dynamic-slice_convert_fusion.2), channel_id=1, source_target_pairs={{0,16},{4,20},{8,24},{12,28},{16,0},{20,4},{24,8},{28,12},{1,17},{... | collective-permute-start | bytes 331784 | tf_op jit(solution)/shard_map/ppermute | solution.py:309
  (10 other events, 14.3 us)

commit v2 on v1

v2 whole, which is shorter than its diff:
```python
import math
from functools import partial

import jax
import jax.numpy as jnp
from jax import lax
from jax.experimental import pallas as pl
from jax.experimental.pallas import tpu as pltpu
from jax.sharding import PartitionSpec as P

FIRST_DILATION = 8
F32 = jnp.float32
BF16 = jnp.bfloat16
VMEM = pl.BlockSpec(memory_space=pltpu.VMEM)
VMEM_LIMIT = 20 * 2**20
ROOT = math.sqrt(2.0 / math.pi)
CUBE = 0.044715


def kernel_call(body, args, outs, flops=0):
    moved = sum(a.size * a.dtype.itemsize for a in args)
    moved += sum(math.prod(o.shape) * o.dtype.itemsize for o in outs)
    return pl.pallas_call(
        body,
        out_shape=tuple(outs),
        in_specs=[VMEM] * len(args),
        out_specs=tuple(VMEM for _ in outs),
        compiler_params=pltpu.CompilerParams(vmem_limit_bytes=VMEM_LIMIT),
        cost_estimate=pl.CostEstimate(flops=flops, bytes_accessed=moved, transcendentals=0),
    )(*args)


def shape(dims, dtype=BF16):
    return jax.ShapeDtypeStruct(tuple(dims), dtype)


def bit_of(axis, bit):
    return (lax.axis_index(axis) >> bit) & 1


def normed(hidden):
    wide = hidden.astype(F32)
    recip = lax.rsqrt(jnp.mean(wide * wide, axis=-1, keepdims=True) + 1e-05)
    return wide * recip, recip, wide


def gelu(v):
    return 0.5 * v * (1.0 + jnp.tanh(ROOT * (v + CUBE * (v * v * v))))


def gelu_slope(v):
    square = v * v
    t = jnp.tanh(ROOT * v * (1.0 + CUBE * square))
    return 0.5 * (1.0 + t) + 0.5 * v * (1.0 - t * t) * (ROOT * (1.0 + 3.0 * CUBE * square))


def flat(cells):
    return cells.reshape(-1, cells.shape[-1])


def dot(a, b):
    return jnp.dot(a, b, preferred_element_type=F32)


def dot_nt(a, b):
    return lax.dot_general(a, b, (((1,), (1,)), ((), ())), preferred_element_type=F32)


def dot_tn(a, b):
    return lax.dot_general(a, b, (((0,), (0,)), ((), ())), preferred_element_type=F32)


def windows(above, own, below):
    width, rows = above.shape[1], own.shape[1]
    before = jnp.concatenate([above, own[:, : rows - width]], axis=1)
    after = jnp.concatenate([own[:, width:], below], axis=1)
    return flat(before), flat(own), flat(after)


def quarters(cells, parity, turn):
    q = cells.shape[-1] // 4
    a, b, c, d = (cells[..., i * q : (i + 1) * q] for i in range(4))
    even, odd = jnp.concatenate([a, c], axis=-1), jnp.concatenate([b, d], axis=-1)
    even_back, odd_back = jnp.concatenate([c, a], axis=-1), jnp.concatenate([d, b], axis=-1)
    even, odd = jnp.where(turn == 0, even, even_back), jnp.where(turn == 0, odd, odd_back)
    return jnp.where(parity == 0, even, odd), jnp.where(parity == 0, odd, even)


def by_low_bit(cells, count, turn):
    w = cells.shape[-1] // count
    even = jnp.concatenate([cells[..., j * w : (j + 1) * w] for j in range(0, count, 2)], axis=-1)
    odd = jnp.concatenate([cells[..., j * w : (j + 1) * w] for j in range(1, count, 2)], axis=-1)
    return jnp.concatenate([jnp.where(turn == 0, even, odd), jnp.where(turn == 0, odd, even)], axis=-1)


def store_edges(cells, ref_a, ref_b, at):
    width = cells.shape[1] // 2
    even = bit_of("seq", 0) == 0
    head, tail = cells[:, :width], cells[:, width:]
    ref_a[:, at : at + width] = jnp.where(even, tail, head)
    ref_b[:, at : at + width] = jnp.where(even, head, tail)


def halos(ref_a, ref_b, at, width):
    even = bit_of("seq", 0) == 0
    a, b = ref_a[:, at : at + width], ref_b[:, at : at + width]
    return jnp.where(even, b, a), jnp.where(even, a, b)


def edge_body(near, far, h_ref, q_ref, a_ref, b_ref):
    rows = h_ref.shape[1]
    q = jnp.concatenate([q_ref[:, :far], q_ref[:, rows - far :]], axis=1)
    h = jnp.concatenate([h_ref[:, :near], h_ref[:, rows - near :]], axis=1)
    store_edges(q, a_ref, b_ref, 0)
    store_edges(h, a_ref, b_ref, far)


def first_body(near, h_ref, w_ref, s_ref, z_ref):
    act, _, _ = normed(h_ref[...])
    s = gelu(act)
    edge = jnp.zeros((s.shape[0], near, s.shape[2]), F32)
    before, own, after = (v.astype(BF16) for v in windows(edge, s, edge))
    s_ref[...] = own.reshape(s_ref.shape)
    z = dot(own, w_ref[0, 1]) + dot(before, w_ref[0, 0]) + dot(after, w_ref[0, 2])
    z_ref[...] = z.reshape(z_ref.shape)


def second_body(near, far, z_ref, h_ref, s_ref, a_ref, b_ref, w_ref, h1_ref, s1_ref, keep_ref, send_ref, kx_ref, sx_ref):
    rows = h_ref.shape[1]
    parity, turn = bit_of("dp", 0), bit_of("dp", 1)
    above, below = halos(a_ref, b_ref, far, near)
    above, below = gelu(normed(above)[0]), gelu(normed(below)[0])
    ext = jnp.concatenate([above, s_ref[...].astype(F32), below], axis=1).astype(BF16)
    kx_ref[...], sx_ref[...] = quarters(ext, parity, turn)
    add_top = dot(flat(above).astype(BF16), w_ref[0, 0]).reshape(above.shape)
    add_low = dot(flat(below).astype(BF16), w_ref[0, 2]).reshape(below.shape)
    z = z_ref[...]
    z = jnp.concatenate([z[:, :near] + add_top, z[:, near : rows - near], z[:, rows - near :] + add_low], axis=1)
    h1 = (h_ref[...].astype(F32) + z).astype(BF16)
    h1_ref[...] = h1
    s1 = gelu(normed(h1)[0]).astype(BF16)
    s1_ref[...] = s1
    keep_ref[...], send_ref[...] = quarters(s1, parity, turn)


def back_conv(layer, dtype, above, below, q, w_ref, h_ref, g):
    before, own, after = windows(above.astype(dtype), q.astype(dtype), below.astype(dtype))
    e = dot_nt(own.astype(BF16), w_ref[layer, 1])
    e += dot_nt(after.astype(BF16), w_ref[layer, 0])
    e += dot_nt(before.astype(BF16), w_ref[layer, 2])
    act, recip, wide = normed(h_ref[...])
    through = e.reshape(act.shape) * gelu_slope(act)
    inner = jnp.mean(through * wide, axis=-1, keepdims=True)
    return g + recip * through - wide * (recip * recip * recip * inner)


def back_body(near, far, count, q_ref, a_ref, b_ref, w_ref, h_ref, s_ref, g_ref, out_ref, mixed_ref, na_ref, nb_ref):
    rows = q_ref.shape[1]
    above, below = halos(a_ref, b_ref, 0, far)
    g = back_conv(1, BF16, above, below, q_ref[...], w_ref, h_ref, q_ref[...].astype(F32))
    g_ref[...] = g
    q = g.astype(BF16)
    out_ref[...] = q
    mixed_ref[...] = by_low_bit(q, count, bit_of("seq", 0))
    s = jnp.concatenate([s_ref[:, :far], s_ref[:, rows - far :]], axis=1)
    store_edges(s, na_ref, nb_ref, 0)
    ends = jnp.concatenate([g[:, :near], g[:, rows - near :]], axis=1).astype(BF16)
    store_edges(ends, na_ref, nb_ref, far)


def last_back_body(near, far, q_ref, a_ref, b_ref, w_ref, h_ref, g_ref, out_ref):
    above, below = halos(a_ref, b_ref, far, near)
    out_ref[...] = back_conv(0, F32, above, below, q_ref[...], w_ref, h_ref, g_ref[...]).astype(BF16)


def last_body(far, s_ref, a_ref, b_ref, w_ref, h_ref, out_ref):
    above, below = halos(a_ref, b_ref, 0, far)
    before, own, after = windows(above, s_ref[...], below)
    z = dot(before, w_ref[1, 0]) + dot(own, w_ref[1, 1]) + dot(after, w_ref[1, 2])
    out_ref[...] = (h_ref[...].astype(F32) + z.reshape(h_ref.shape)).astype(BF16)


def store_grad(tap, d, keep_ref, send_ref):
    tall, wide = d.shape[0] // 2, d.shape[1] // 2
    first = bit_of("dp", 0) == 0
    right, low = d[:tall, wide:], d[tall:, :wide]
    keep_ref[0, tap] = d[:tall, :wide]
    keep_ref[1, tap] = jnp.where(first, right, low)
    send_ref[0, tap] = jnp.where(first, low, right).astype(BF16)
    send_ref[1, tap] = d[tall:, wide:].astype(BF16)


def grad_near_body(s_ref, s2_ref, q_ref, q2_ref, keep_ref, send_ref):
    rows = q_ref.shape[1]
    step = (s_ref.shape[1] - rows) // 2
    q = jnp.concatenate([flat(q_ref[...]), flat(q2_ref[...])], axis=0)
    for tap in range(3):
        cut = slice(tap * step, tap * step + rows)
        s = jnp.concatenate([flat(s_ref[:, cut]), flat(s2_ref[:, cut])], axis=0)
        store_grad(tap, dot_tn(s, q), keep_ref, send_ref)


def grad_far_body(far, count, s_ref, s2_ref, q_ref, q2_ref, a_ref, b_ref, a2_ref, b2_ref, keep_ref, send_ref):
    turn = bit_of("seq", 0)
    s = jnp.concatenate([flat(s_ref[...]), flat(s2_ref[...])], axis=0)
    taps = []
    for own_ref, at_a, at_b in ((q_ref, a_ref, b_ref), (q2_ref, a2_ref, b2_ref)):
        above, below = halos(at_a, at_b, 0, far)
        before, own, after = windows(*(by_low_bit(v, count, turn) for v in (above, own_ref[...], below)))
        taps.append((after, own, before))
    for tap in range(3):
        q = jnp.concatenate([taps[0][tap], taps[1][tap]], axis=0)
        store_grad(tap, dot_tn(s, q), keep_ref, send_ref)


def pass_body(keep_ref, got_ref, send_ref):
    for slot in range(send_ref.shape[0]):
        send_ref[slot] = (keep_ref[2 * slot + 1] + got_ref[2 * slot + 1].astype(F32)).astype(BF16)


def weave_body(count, keep_ref, got_ref, more_ref, out_ref, send_ref, all_ref):
    total = flat(keep_ref[0] + got_ref[0].astype(F32) + more_ref[0].astype(F32))
    w, r = total.shape[1] // count, total.shape[0] // count
    for block in range(count):
        all_ref[block] = jnp.concatenate(
            [total[g * r : (g + 1) * r, block * w : (block + 1) * w] for g in range(count)], axis=1
        )
    mine = lax.axis_index("seq") >> 1
    for slot in range(count // 2):
        out_ref[slot] = all_ref[mine ^ (2 * slot)]
        send_ref[slot] = all_ref[mine ^ (2 * slot + 1)].astype(BF16)


def final_body(count, factor, *refs):
    out_ref = refs[-1]
    for layer in range(out_ref.shape[0]):
        keep_ref, got_ref, more_ref = refs[3 * layer : 3 * layer + 3]
        total = (keep_ref[0] + got_ref[0].astype(F32) + more_ref[0].astype(F32)) * factor
        w = total.shape[1] // count
        rows = jnp.concatenate([total[:, g * w : (g + 1) * w] for g in range(count)], axis=0)
        out_ref[layer] = rows.reshape(out_ref.shape[1:])


def per_device(embeddings, kernels, cotangent):
    batches, rows, channels = embeddings.shape
    seqs, dps = lax.axis_size("seq"), lax.axis_size("dp")
    near, far = FIRST_DILATION, 2 * FIRST_DILATION
    conv_flops = 6 * batches * rows * channels * channels
    half = channels // 2
    own = (batches, rows, channels)
    edges = (batches, near + far, channels)

    def paired(partner):
        pairs = []
        for s in range(seqs):
            for d in range(dps):
                t, e = partner(s, d)
                if 0 <= t < seqs:
                    pairs.append((s * dps + d, t * dps + e))
        return partial(lax.ppermute, axis_name=("seq", "dp"), perm=pairs)

    swap = paired(lambda s, d: (s, d ^ 1))
    to_a = paired(lambda s, d: (s ^ 1, d))
    to_b = paired(lambda s, d: (((s + 1) ^ 1) - 1, d))
    cross_one = paired(lambda s, d: (s, d ^ 2) if d % 2 == 0 else (s ^ 1, d))
    cross_two = paired(lambda s, d: (s ^ 1, d) if d % 2 == 0 else (s, d ^ 2))

    def along(bit):
        return paired(lambda s, d: (s ^ bit, d))

    send_a, send_b = kernel_call(
        partial(edge_body, near, far), [embeddings, cotangent], [shape(edges), shape(edges)]
    )
    got_a, got_b = to_a(send_a), to_b(send_b)
    q1_other = swap(cotangent)
    s0, z0 = kernel_call(
        partial(first_body, near), [embeddings, kernels], [shape(own), shape(own, F32)], conv_flops
    )
    other_a, other_b = swap(got_a), swap(got_b)
    h1, s1, s1_keep, s1_send, s0_keep, s0_send = kernel_call(
        partial(second_body, near, far),
        [z0, embeddings, s0, got_a, got_b, kernels],
        [
            shape(own),
            shape(own),
            shape((batches, rows, half)),
            shape((batches, rows, half)),
            shape((batches, rows + 2 * near, half)),
            shape((batches, rows + 2 * near, half)),
        ],
        conv_flops // 10,
    )
    s1_other, s0_other = swap(s1_send), swap(s0_send)

    blocks = [shape((2, 3, half // 2, half), F32), shape((2, 3, half // 2, half))]
    count = seqs // 2
    strip = 3 * (half // 2) // count
    woven = strip % 16 == 0
    factor = 1.0 / math.sqrt(batches * dps * rows * seqs)

    def passed(keep, got):
        (send,) = kernel_call(pass_body, [keep, got], [shape((keep.shape[0] // 2, *keep.shape[1:]))])
        return send

    def reduced(keep, send):
        got = cross_one(send)
        more = cross_two(passed(keep, got))
        if woven:
            keep, send, _ = kernel_call(
                partial(weave_body, count),
                [keep, got, more],
                [
                    shape((count // 2, strip, half), F32),
                    shape((count // 2, strip, half)),
                    shape((count, strip, half), F32),
                ],
            )
        else:
            total = keep[0] + got[0].astype(F32) + more[0].astype(F32)
            total = total.reshape(count, strip, count, half // count)
            total = total.transpose(2, 1, 0, 3).reshape(count, strip, half)
            total = total[jnp.arange(count) ^ (lax.axis_index("seq") // 2)]
            keep, send = total[0::2], total[1::2].astype(BF16)
        got, bit = along(2)(send), 4
        while 2 * bit < seqs:
            total = keep + got.astype(F32)
            keep, got, bit = total[0::2], along(bit)(total[1::2].astype(BF16)), 2 * bit
        if bit < seqs:
            return keep, got, along(bit)(passed(keep, got))
        return keep, got, jnp.zeros_like(got)

    keep1, send1 = kernel_call(
        partial(grad_far_body, far, seqs),
        [s1_keep, s1_other, cotangent, q1_other, got_a, got_b, other_a, other_b],
        blocks,
        conv_flops,
    )
    parts1 = reduced(keep1, send1)

    g1, q0, q0_mixed, send_a, send_b = kernel_call(
        partial(back_body, near, far, seqs),
        [cotangent, got_a, got_b, kernels, h1, s1],
        [shape(own, F32), shape(own), shape(own), shape(edges), shape(edges)],
        conv_flops,
    )
    q0_other = swap(q0_mixed)
    keep0, send0 = kernel_call(
        grad_near_body, [s0_keep, s0_other, q0_mixed, q0_other], blocks, conv_flops
    )
    parts0 = reduced(keep0, send0)

    got_a, got_b = to_a(send_a), to_b(send_b)
    (out,) = kernel_call(
        partial(last_body, far), [s1, got_a, got_b, kernels, h1], [shape(own)], conv_flops
    )
    (grad_in,) = kernel_call(
        partial(last_back_body, near, far),
        [q0, got_a, got_b, kernels, embeddings, g1],
        [shape(own)],
        conv_flops,
    )
    final = (2, 3, half // 2, half // count)
    if woven:
        (grads,) = kernel_call(
            partial(final_body, count, factor), [*parts0, *parts1], [shape(final, F32)]
        )
        return out, grad_in, grads
    grads = []
    for keep, got, more in (parts0, parts1):
        total = (keep[0] + got[0].astype(F32) + more[0].astype(F32)) * factor
        grads.append(total.reshape(strip, count, half // count).transpose(1, 0, 2).reshape(final[1:]))
    return out, grad_in, jnp.stack(grads)


def solution(mesh):
    placed = (P("dp", "seq", None), P(), P("dp", "seq", None))
    return jax.shard_map(
        per_device,
        mesh=mesh,
        in_specs=placed,
        out_specs=(P("dp", "seq", None), P("dp", "seq", None), P(None, None, "dp", "seq")),
        check_vma=False,
    )
```

time: 122 us -> 91.8 us (0.75); the launches traced: 120 us -> 91.4 us
  starting transfers between devices: 39.7 us -> 24.7 us
  local copies, waits for them, and re-layouts: 19.1 us -> 4.2 us
  waiting for transfers between devices: 25.6 us -> 32.4 us
  other arithmetic: 2.61 us -> 0.01 us
  Pallas kernels: 31.9 us -> 29.4 us
    ppermute x17 -> x15, starting transfers between devices: 39.2 us -> 24.1 us  [the longest x2 7.16 us: reduced(): got, bit = (along(2)(send), 4)]
    ppermute x17 -> x15, waiting for transfers between devices: 22.1 us -> 32.4 us  [the longest x2 19.8 us: reduced(): got = cross_one(send)]
    unnamed x44 -> x10, local copies, waits for them, and re-layouts: 10 us -> 4.2 us
    squeeze x4 -> x0, local copies, waits for them, and re-layouts: 5.49 us -> none  [the longest x1 5.29 us: per_device(): kernels[1]]
    ppermute x2, waiting for transfers between devices: 3.53 us -> 0.01 us  [per_device(): s1_other, s0_other = (swap(s1_send), swap(s0_send))]
    slice x4 -> x0, local copies, waits for them, and re-layouts: 3.33 us -> none  [the longest x1 1.72 us: per_device(): q_up, q_down = (up(cotangent[:, rows - far:]), down(cotangent[:, :far]))]
    pallas_call x12 -> x15, Pallas kernels: 31.9 us -> 29.4 us  [kernel_call(): pl.pallas_call(body, out_shape=tuple(outs), in_specs=[VMEM] * len(args),...]
    add x4 -> x0, other arithmetic: 1.68 us -> none  [reduced(): total = keep + got.astype(F32)]
  transfers between devices with their start and end apart: 20 -> 18, of which waited for: 6 -> 7; matrix products, arithmetic and copies ran while one was open for 8% -> 0% of each run, Pallas kernels for 22% -> 30%
where the time goes in v2:
time: 91.8 us; the launch traced here: 91.4 us
  waiting for transfers between devices  32.4 us (35%)
  Pallas kernels  29.4 us (32%)
  starting transfers between devices  24.7 us (27%)
  local copies, waits for them, and re-layouts  4.2 us (5%)
    pallas_call x15, Pallas kernels, kernel_call(): pl.pallas_call(body, out_shape=tuple(outs), in_specs=[VMEM] * len(args),...  29.4 us
    ppermute x2, waiting for transfers between devices, reduced(): got = cross_one(send)  19.8 us
    ppermute x2, starting transfers between devices, reduced(): got, bit = (along(2)(send), 4)  7.16 us
    ppermute x2, waiting for transfers between devices, reduced(): more = cross_two(passed(keep, got))  5.71 us
    ppermute x2, starting transfers between devices, reduced(): more = cross_two(passed(keep, got))  5.09 us
    ppermute x2, starting transfers between devices, reduced(): return (keep, got, along(bit)(passed(keep, got)))  4.59 us
    ppermute x4, starting transfers between devices, per_device(): got_a, got_b = (to_a(send_a), to_b(send_b))  4.44 us
    unnamed x10, local copies, waits for them, and re-layouts  4.2 us
  transfers between devices with their start and end apart: 18, of which 7 were waited for; matrix products, arithmetic and copies ran while one was open for 0% of the time, Pallas kernels for 30%

profile of v2, /device:TPU:0, one launch (start us, length us, event | category | flops | bytes accessed | tf_op | source)
XLA Modules:
  0.0 91.4 jit_solution(701397053313719910)
XLA Ops:
  0.6 1.2 %copy-done.1 = bf16[6,96,768]{2,1,0:T(8,128)(2,1)S(1)} copy-done((bf16[6,96,768]{2,1,0:T(8,128)(2,1)S(1)}, bf16[6,96,768]{2,1,0:T(8,128)(2,1)}, u32[]{:S(2)}) %copy-start.1) | copy-done | bytes 884760
  1.8 1.2 %shard_map.59 = (bf16[6,24,768]{2,1,0:T(8,128)(2,1)S(1)}, bf16[6,24,768]{2,1,0:T(8,128)(2,1)S(1)}) custom-call(bf16[6,96,768]{2,1,0:T(8,128)(2,1)S(1)} %copy-done.1, bf16[6,96,768]{2,1,0:T(8,128)(2,1)} %q_ref.5), custom_call_target="tpu_custom_call" | custom-call | bytes 2211840 | tf_op jit(solution)/shard_map/pallas_call | solution.py:23
  3.0 3.0 %collective-permute-start = (bf16[6,24,768]{2,1,0:T(8,128)(2,1)S(1)}, bf16[6,24,768]{2,1,0:T(8,128)(2,1)S(1)}, u32[]{:S(2)}, u32[]{:S(2)}) collective-permute-start(bf16[6,24,768]{2,1,0:T(8,128)(2,1)S(1)} %get-tuple-element.28), channel_id=1, source_target_pairs={{0,4},{1,5},{2,6},{3,7},{4,0},{5,1},{6,2},{7,3},{8,12},{9,13},{10,... | collective-permute-start | bytes 663560 | tf_op jit(solution)/shard_map/ppermute | solution.py:274
  6.1 0.7 collective-permute-start.1
  6.8 3.0 %copy-done = bf16[2,3,768,768]{3,2,1,0:T(8,128)(2,1)S(1)} copy-done((bf16[2,3,768,768]{3,2,1,0:T(8,128)(2,1)S(1)}, bf16[2,3,768,768]{3,2,1,0:T(8,128)(2,1)}, u32[]{:S(2)}) %copy-start) | copy-done | bytes 7077912
  9.8 2.7 %shard_map.58 = (bf16[6,96,768]{2,1,0:T(8,128)(2,1)S(1)}, f32[6,96,768]{2,1,0:T(8,128)S(1)}) custom-call(bf16[6,96,768]{2,1,0:T(8,128)(2,1)S(1)} %copy-done.1, bf16[2,3,768,768]{3,2,1,0:T(8,128)(2,1)S(1)} %copy-done), custom_call_target="tpu_custom_call" | custom-call | flops 2038431744 | bytes 10616832 | tf_op jit(solution)/shard_map/pallas_call | solution.py:23
  12.5 2.9 %collective-permute-done.a_ref = bf16[6,24,768]{2,1,0:T(8,128)(2,1)S(1)} collective-permute-done((bf16[6,24,768]{2,1,0:T(8,128)(2,1)S(1)}, bf16[6,24,768]{2,1,0:T(8,128)(2,1)S(1)}, u32[]{:S(2)}, u32[]{:S(2)}) %collective-permute-start) | collective-permute-done | bytes 221216 | tf_op jit(solution)/shard_map/ppermute | solution.py:274
  15.5 1.8 %shard_map.60 = (bf16[6,96,768]{2,1,0:T(8,128)(2,1)S(1)}, bf16[6,96,768]{2,1,0:T(8,128)(2,1)S(1)}, bf16[6,96,384]{2,1,0:T(8,128)(2,1)S(1)}, bf16[6,96,384]{2,1,0...) custom-call(f32[6,96,768]{2,1,0:T(8,128)S(1)} %get-tuple-element.26.z_ref, ...), custom_call_target="tpu_custom_call" | custom-call | flops 203843168 | bytes 14745600 | tf_op jit(solution)/shard_map/pallas_call | solution.py:23
  17.3 5.1 %shard_map.61 = (f32[6,96,768]{2,1,0:T(8,128)S(1)}, bf16[6,96,768]{2,1,0:T(8,128)(2,1)S(1)}, bf16[6,96,768]{2,1,0:T(8,128)(2,1)S(1)}, bf16[6,24,768]{2,1,0:T(8,128)(2,1)S(1)}, bf16[6,24,768]{2,1,0:T(8,128)(2,1)S(1)}) custom-call(bf16[6,96,768]{2,1,0:T(8,128)(2,1)} %q_ref.5, bf16[6,24,768]{2,1,0:T(8,128)(2,1)S(1)} %collective-permute-done.a_ref, ...), custom_call_target="tpu_custom_call" | custom-call | flops 2038431744 | bytes 14155776 | tf_op jit(solution)/shard_map/pallas_call | solution.py:23
  22.5 0.5 collective-permute-start.12
  23.5 1.7 %collective-permute-done.12.a2_ref = bf16[6,24,768]{2,1,0:T(8,128)(2,1)S(1)} collective-permute-done((bf16[6,24,768]{2,1,0:T(8,128)(2,1)S(1)}, bf16[6,24,768]{2,1,0:T(8,128)(2,1)S(1)}, u32[]{:S(2)}, u32[]{:S(2)}) %collective-permute-start.12) | collective-permute-done | bytes 221216 | tf_op jit(solution)/shard_map/ppermute | solution.py:279
  25.4 1.5 %collective-permute-done.13.b2_ref = bf16[6,24,768]{2,1,0:T(8,128)(2,1)S(1)} collective-permute-done((bf16[6,24,768]{2,1,0:T(8,128)(2,1)S(1)}, bf16[6,24,768]{2,1,0:T(8,128)(2,1)S(1)}, u32[]{:S(2)}, u32[]{:S(2)}) %collective-permute-start.13) | collective-permute-done | bytes 221216 | tf_op jit(solution)/shard_map/ppermute | solution.py:279
  27.0 4.2 %shard_map.68 = (f32[2,3,192,384]{3,2,1,0:T(8,128)S(1)}, bf16[2,3,192,384]{3,2,1,0:T(8,128)(2,1)S(1)}) custom-call(bf16[6,96,384]{2,1,0:T(8,128)(2,1)S(1)} %get-tuple-element.43.s_ref, bf16[6,96,384]{2,1,0:T(8,128)(2,1)S(1)} %collective-permute-done.10.s2_ref, bf16[6,96,768]{2,1,0:T(8,128)(2,1)} %q_ref.5, ...), custom_call_target="tpu_custom_call" | custom-call | flops 2038431744 | bytes 6193152 | tf_op jit(solution)/shard_map/pallas_call | solution.py:23
  31.2 1.6 %collective-permute-start.14 = (bf16[2,3,192,384]{3,2,1,0:T(8,128)(2,1)S(1)}, bf16[2,3,192,384]{3,2,1,0:T(8,128)(2,1)S(1)}, u32[]{:S(2)}, u32[]{:S(2)}) collective-permute-start(bf16[2,3,192,384]{3,2,1,0:T(8,128)(2,1)S(1)} %get-tuple-element.46), channel_id=1, source_target_pairs={{0,2},{1,5},{2,0},{3,7},{4,6},{5,1},{6,4},{7,3},{8,10},{9,13},{10,... | collective-permute-start | bytes 2654216 | tf_op jit(solution)/shard_map/ppermute | solution.py:306
  32.7 2.7 %shard_map.64 = (f32[2,3,192,384]{3,2,1,0:T(8,128)S(1)}, bf16[2,3,192,384]{3,2,1,0:T(8,128)(2,1)S(1)}) custom-call(bf16[6,112,384]{2,1,0:T(8,128)(2,1)S(1)} %get-tuple-element.36.s_ref, bf16[6,112,384]{2,1,0:T(8,128)(2,1)S(1)} %collective-permute-done.4.s2_ref, bf16[6,96,768]{2,1,0:T(8,128)(2,1)S(1)} %get-tuple-element.38.q_ref, ...), custom_call_target="tpu_custom_call" | custom-call | flops 2038431744 | bytes 5455872 | tf_op jit(solution)/shard_map/pallas_call | solution.py:23
  35.5 0.6 collective-permute-start.6
  36.1 8.2 %collective-permute-done.14.got_ref = bf16[2,3,192,384]{3,2,1,0:T(8,128)(2,1)S(1)} collective-permute-done((bf16[2,3,192,384]{3,2,1,0:T(8,128)(2,1)S(1)}, bf16[2,3,192,384]{3,2,1,0:T(8,128)(2,1)S(1)}, u32[]{:S(2)}, u32[]{:S(2)}) %collective-permute-start.14) | collective-permute-done | bytes 884768 | tf_op jit(solution)/shard_map/ppermute | solution.py:306
  44.4 2.5 %collective-permute-start.15 = (bf16[1,3,192,384]{3,2,1,0:T(8,128)(2,1)S(1)}, bf16[1,3,192,384]{3,2,1,0:T(8,128)(2,1)S(1)}, u32[]{:S(2)}, u32[]{:S(2)}) collective-permute-start(bf16[1,3,192,384]{3,2,1,0:T(8,128)(2,1)S(1)} %shard_map.69), channel_id=1, source_target_pairs={{0,4},{1,3},{2,6},{3,1},{4,0},{5,7},{6,2},{7,5},{8,12},{9,11},{10,... | collective-permute-start | bytes 1327112 | tf_op jit(solution)/shard_map/ppermute | solution.py:307
  46.9 11.6 %collective-permute-done.6.got_ref = bf16[2,3,192,384]{3,2,1,0:T(8,128)(2,1)S(1)} collective-permute-done((bf16[2,3,192,384]{3,2,1,0:T(8,128)(2,1)S(1)}, bf16[2,3,192,384]{3,2,1,0:T(8,128)(2,1)S(1)}, u32[]{:S(2)}, u32[]{:S(2)}) %collective-permute-start.6) | collective-permute-done | bytes 884768 | tf_op jit(solution)/shard_map/ppermute | solution.py:306
  58.6 2.5 %collective-permute-start.7 = (bf16[1,3,192,384]{3,2,1,0:T(8,128)(2,1)S(1)}, bf16[1,3,192,384]{3,2,1,0:T(8,128)(2,1)S(1)}, u32[]{:S(2)}, u32[]{:S(2)}) collective-permute-start(bf16[1,3,192,384]{3,2,1,0:T(8,128)(2,1)S(1)} %shard_map.65), channel_id=1, source_target_pairs={{0,4},{1,3},{2,6},{3,1},{4,0},{5,7},{6,2},{7,5},{8,12},{9,11},{10,... | collective-permute-start | bytes 1327112 | tf_op jit(solution)/shard_map/ppermute | solution.py:307
  61.2 0.7 collective-permute-start.3
  61.9 1.4 %shard_map.70 = (f32[2,144,384]{2,1,0:T(8,128)S(1)}, bf16[2,144,384]{2,1,0:T(8,128)(2,1)S(1)}, f32[4,144,384]{2,1,0:T(8,128)}) custom-call(f32[2,3,192,384]{3,2,1,0:T(8,128)S(1)} %get-tuple-element.45.keep_ref, bf16[2,3,192,384]{3,2,1,0:T(8,128)(2,1)S(1)} %collective-permute-done.14.got_ref, bf16[1,3,192,384]{3,2,1,0:T(8,128)(2,1)S(1)} %collective-permute-done.15.more_ref), custom_call_target="tpu_custom_call" | custom-call | bytes 4644864 | tf_op jit(solution)/shard_map/pallas_call | solution.py:23
  63.3 4.6 %collective-permute-start.16 = (bf16[2,144,384]{2,1,0:T(8,128)(2,1)S(1)}, bf16[2,144,384]{2,1,0:T(8,128)(2,1)S(1)}, u32[]{:S(2)}, u32[]{:S(2)}) collective-permute-start(bf16[2,144,384]{2,1,0:T(8,128)(2,1)S(1)} %get-tuple-element.48), channel_id=1, source_target_pairs={{0,8},{1,9},{2,10},{3,11},{4,12},{5,13},{6,14},{7,15},{8,0},{9,1},... | collective-permute-start | bytes 663560 | tf_op jit(solution)/shard_map/ppermute | solution.py:324
  67.9 5.7 %collective-permute-done.7.more_ref = bf16[1,3,192,384]{3,2,1,0:T(8,128)(2,1)S(1)} collective-permute-done((bf16[1,3,192,384]{3,2,1,0:T(8,128)(2,1)S(1)}, bf16[1,3,192,384]{3,2,1,0:T(8,128)(2,1)S(1)}, u32[]{:S(2)}, u32[]{:S(2)}) %collective-permute-start.7) | collective-permute-done | bytes 442400 | tf_op jit(solution)/shard_map/ppermute | solution.py:307
  73.6 1.4 %shard_map.66 = (f32[2,144,384]{2,1,0:T(8,128)S(1)}, bf16[2,144,384]{2,1,0:T(8,128)(2,1)S(1)}, f32[4,144,384]{2,1,0:T(8,128)}) custom-call(f32[2,3,192,384]{3,2,1,0:T(8,128)S(1)} %get-tuple-element.39.keep_ref, bf16[2,3,192,384]{3,2,1,0:T(8,128)(2,1)S(1)} %collective-permute-done.6.got_ref, bf16[1,3,192,384]{3,2,1,0:T(8,128)(2,1)S(1)} %collective-permute-done.7.more_ref), custom_call_target="tpu_custom_call" | custom-call | bytes 4644864 | tf_op jit(solution)/shard_map/pallas_call | solution.py:23
  75.0 2.5 %collective-permute-start.8 = (bf16[2,144,384]{2,1,0:T(8,128)(2,1)S(1)}, bf16[2,144,384]{2,1,0:T(8,128)(2,1)S(1)}, u32[]{:S(2)}, u32[]{:S(2)}) collective-permute-start(bf16[2,144,384]{2,1,0:T(8,128)(2,1)S(1)} %get-tuple-element.42), channel_id=1, source_target_pairs={{0,8},{1,9},{2,10},{3,11},{4,12},{5,13},{6,14},{7,15},{8,0},{9,1},... | collective-permute-start | bytes 663560 | tf_op jit(solution)/shard_map/ppermute | solution.py:324
  77.5 3.1 %shard_map.62 = bf16[6,96,768]{2,1,0:T(8,128)(2,1)} custom-call(bf16[6,96,768]{2,1,0:T(8,128)(2,1)S(1)} %get-tuple-element.30.s_ref, bf16[6,24,768]{2,1,0:T(8,128)(2,1)S(1)} %collective-permute-done.2.a_ref, bf16[6,24,768]{2,1,0:T(8,128)(2,1)S(1)} %collective-permute-done.3.b_ref, bf16[2,3,768,768]{3,2,1,0:T(8,128)(2,1)S(1)} %bitcast.1, ...), custom_call_target="tpu_custom_call" | custom-call | flops 2038431744 | bytes 10174464 | tf_op jit(solution)/shard_map/pallas_call | solution.py:23
  80.7 2.7 %collective-permute-start.17 = (bf16[1,144,384]{2,1,0:T(8,128)(2,1)S(1)}, bf16[1,144,384]{2,1,0:T(8,128)(2,1)S(1)}, u32[]{:S(2)}, u32[]{:S(2)}) collective-permute-start(bf16[1,144,384]{2,1,0:T(8,128)(2,1)S(1)} %shard_map.71), channel_id=1, source_target_pairs={{0,16},{1,17},{2,18},{3,19},{4,20},{5,21},{6,22},{7,23},{8,24},{9,... | collective-permute-start | bytes 331784 | tf_op jit(solution)/shard_map/ppermute | solution.py:329
  83.4 1.9 %collective-permute-start.9 = (bf16[1,144,384]{2,1,0:T(8,128)(2,1)S(1)}, bf16[1,144,384]{2,1,0:T(8,128)(2,1)S(1)}, u32[]{:S(2)}, u32[]{:S(2)}) collective-permute-start(bf16[1,144,384]{2,1,0:T(8,128)(2,1)S(1)} %shard_map.67), channel_id=1, source_target_pairs={{0,16},{1,17},{2,18},{3,19},{4,20},{5,21},{6,22},{7,23},{8,24},{9,... | collective-permute-start | bytes 331784 | tf_op jit(solution)/shard_map/ppermute | solution.py:329
  85.3 4.4 %shard_map.63 = bf16[6,96,768]{2,1,0:T(8,128)(2,1)} custom-call(bf16[6,96,768]{2,1,0:T(8,128)(2,1)S(1)} %get-tuple-element.34.q_ref, bf16[6,24,768]{2,1,0:T(8,128)(2,1)S(1)} %collective-permute-done.2.a_ref, bf16[6,24,768]{2,1,0:T(8,128)(2,1)S(1)} %collective-permute-done.3.b_ref, bf16[2,3,768,768]{3,2,1,0:T(8,128)(2,1)S(1)} %bitcast.1, ...), custom_call_target="tpu_custom_call" | custom-call | flops 2038431744 | bytes 11943936 | tf_op jit(solution)/shard_map/pallas_call | solution.py:23
  89.7 0.6 collective-permute-done.9.refs_2_
  90.3 1.1 %shard_map.72 = f32[2,3,192,96]{3,2,1,0:T(8,128)} custom-call(f32[2,144,384]{2,1,0:T(8,128)S(1)} %get-tuple-element.41.keep_ref.refs_0_, bf16[2,144,384]{2,1,0:T(8,128)(2,1)S(1)} %collective-permute-done.8.got_ref.refs_1_, bf16[1,144,384]{2,1,0:T(8,128)(2,1)S(1)} %collective-permute-done.9.refs_2_, f32[2,144,384]{2,1,0:T(8,128)S(1)} %get-tuple-element.47.keep_ref.refs_3_, ...), custom_call_target="tpu_custom_call" | custom-call | bytes 1990656 | tf_op jit(solution)/shard_map/pallas_call | solution.py:23
  (30 shorter events, 1.2 us)
Async XLA Ops:
  0.6 1.2 %copy-start.1 = (bf16[6,96,768]{2,1,0:T(8,128)(2,1)S(1)}, bf16[6,96,768]{2,1,0:T(8,128)(2,1)}, u32[]{:S(2)}) copy-start(bf16[6,96,768]{2,1,0:T(8,128)(2,1)} %h_ref.7) | copy-start | bytes 2654212
  3.0 12.5 %collective-permute-start = (bf16[6,24,768]{2,1,0:T(8,128)(2,1)S(1)}, bf16[6,24,768]{2,1,0:T(8,128)(2,1)S(1)}, u32[]{:S(2)}, u32[]{:S(2)}) collective-permute-start(bf16[6,24,768]{2,1,0:T(8,128)(2,1)S(1)} %get-tuple-element.28), channel_id=1, source_target_pairs={{0,4},{1,5},{2,6},{3,7},{4,0},{5,1},{6,2},{7,3},{8,12},{9,13},{10,... | collective-permute-start | bytes 663560 | tf_op jit(solution)/shard_map/ppermute | solution.py:274
  6.1 9.4 %collective-permute-start.1 = (bf16[6,24,768]{2,1,0:T(8,128)(2,1)S(1)}, bf16[6,24,768]{2,1,0:T(8,128)(2,1)S(1)}, u32[]{:S(2)}, u32[]{:S(2)}) collective-permute-start(bf16[6,24,768]{2,1,0:T(8,128)(2,1)S(1)} %get-tuple-element.29), channel_id=1, source_target_pairs={{4,8},{5,9},{6,10},{7,11},{8,4},{9,5},{10,6},{11,7},{12,16},{13,17... | collective-permute-start | bytes 663560 | tf_op jit(solution)/shard_map/ppermute | solution.py:274
  6.7 20.2 %collective-permute-start.11 = (bf16[6,96,768]{2,1,0:T(8,128)(2,1)}, bf16[6,96,768]{2,1,0:T(8,128)(2,1)S(1)}, u32[]{:S(2)}, u32[]{:S(2)}) collective-permute-start(bf16[6,96,768]{2,1,0:T(8,128)(2,1)} %q_ref.5), channel_id=1, source_target_pairs={{0,1},{1,0},{2,3},{3,2},{4,5},{5,4},{6,7},{7,6},{8,9},{9,8},{10,11... | collective-permute-start | bytes 2654216 | tf_op jit(solution)/shard_map/ppermute | solution.py:275
  6.8 3.0 %copy-start = (bf16[2,3,768,768]{3,2,1,0:T(8,128)(2,1)S(1)}, bf16[2,3,768,768]{3,2,1,0:T(8,128)(2,1)}, u32[]{:S(2)}) copy-start(bf16[2,3,768,768]{3,2,1,0:T(8,128)(2,1)} %w_ref.9) | copy-start | bytes 21233668
  9.8 7.4 %slice-start = ((s8[7077888]{0:T(1024)(128)(4,1)}), s8[4194304]{0:T(1024)(128)(4,1)S(1)}, s32[]{:S(2)}) async-start(s8[7077888]{0:T(1024)(128)(4,1)} %bitcast), calls=%async_computation | async-start | bytes 8388608
  15.5 1.8 %slice-start.1 = ((s8[7077888]{0:T(1024)(128)(4,1)}), s8[2883584]{0:T(1024)(128)(4,1)S(1)}, s32[]{:S(2)}) async-start(s8[7077888]{0:T(1024)(128)(4,1)} %bitcast), calls=%async_computation.1 | async-start | bytes 5767168
  22.5 10.3 %collective-permute-start.5 = (bf16[6,96,768]{2,1,0:T(8,128)(2,1)S(1)}, bf16[6,96,768]{2,1,0:T(8,128)(2,1)S(1)}, u32[]{:S(2)}, u32[]{:S(2)}) collective-permute-start(bf16[6,96,768]{2,1,0:T(8,128)(2,1)S(1)} %get-tuple-element.38.q_ref), channel_id=1, source_target_pairs={{0,1},{1,0},{2,3},{3,2},{4,5},{5,4},{6,7},{7,6},{8,9},{9,8},{10,11... | collective-permute-start | bytes 2654216 | tf_op jit(solution)/shard_map/ppermute | solution.py:346
  22.5 2.7 %collective-permute-start.12 = (bf16[6,24,768]{2,1,0:T(8,128)(2,1)S(1)}, bf16[6,24,768]{2,1,0:T(8,128)(2,1)S(1)}, u32[]{:S(2)}, u32[]{:S(2)}) collective-permute-start(bf16[6,24,768]{2,1,0:T(8,128)(2,1)S(1)} %collective-permute-done.a_ref), channel_id=1, source_target_pairs={{0,1},{1,0},{2,3},{3,2},{4,5},{5,4},{6,7},{7,6},{8,9},{9,8},{10,11... | collective-permute-start | bytes 663560 | tf_op jit(solution)/shard_map/ppermute | solution.py:279
  23.0 3.9 %collective-permute-start.10 = (bf16[6,96,384]{2,1,0:T(8,128)(2,1)S(1)}, bf16[6,96,384]{2,1,0:T(8,128)(2,1)S(1)}, u32[]{:S(2)}, u32[]{:S(2)}) collective-permute-start(bf16[6,96,384]{2,1,0:T(8,128)(2,1)S(1)} %get-tuple-element.44), channel_id=1, source_target_pairs={{0,1},{1,0},{2,3},{3,2},{4,5},{5,4},{6,7},{7,6},{8,9},{9,8},{10,11... | collective-permute-start | bytes 1327112 | tf_op jit(solution)/shard_map/ppermute | solution.py:293
  23.1 9.6 %collective-permute-start.4 = (bf16[6,112,384]{2,1,0:T(8,128)(2,1)S(1)}, bf16[6,112,384]{2,1,0:T(8,128)(2,1)S(1)}, u32[]{:S(2)}, u32[]{:S(2)}) collective-permute-start(bf16[6,112,384]{2,1,0:T(8,128)(2,1)S(1)} %get-tuple-element.37), channel_id=1, source_target_pairs={{0,1},{1,0},{2,3},{3,2},{4,5},{5,4},{6,7},{7,6},{8,9},{9,8},{10,11... | collective-permute-start | bytes 1548296 | tf_op jit(solution)/shard_map/ppermute | solution.py:293
  25.3 1.7 %collective-permute-start.13 = (bf16[6,24,768]{2,1,0:T(8,128)(2,1)S(1)}, bf16[6,24,768]{2,1,0:T(8,128)(2,1)S(1)}, u32[]{:S(2)}, u32[]{:S(2)}) collective-permute-start(bf16[6,24,768]{2,1,0:T(8,128)(2,1)S(1)} %collective-permute-done.1.b_ref), channel_id=1, source_target_pairs={{0,1},{1,0},{2,3},{3,2},{4,5},{5,4},{6,7},{7,6},{8,9},{9,8},{10,11... | collective-permute-start | bytes 663560 | tf_op jit(solution)/shard_map/ppermute | solution.py:279
  31.2 13.1 %collective-permute-start.14 = (bf16[2,3,192,384]{3,2,1,0:T(8,128)(2,1)S(1)}, bf16[2,3,192,384]{3,2,1,0:T(8,128)(2,1)S(1)}, u32[]{:S(2)}, u32[]{:S(2)}) collective-permute-start(bf16[2,3,192,384]{3,2,1,0:T(8,128)(2,1)S(1)} %get-tuple-element.46), channel_id=1, source_target_pairs={{0,2},{1,5},{2,0},{3,7},{4,6},{5,1},{6,4},{7,3},{8,10},{9,13},{10,... | collective-permute-start | bytes 2654216 | tf_op jit(solution)/shard_map/ppermute | solution.py:306
  35.5 23.0 %collective-permute-start.6 = (bf16[2,3,192,384]{3,2,1,0:T(8,128)(2,1)S(1)}, bf16[2,3,192,384]{3,2,1,0:T(8,128)(2,1)S(1)}, u32[]{:S(2)}, u32[]{:S(2)}) collective-permute-start(bf16[2,3,192,384]{3,2,1,0:T(8,128)(2,1)S(1)} %get-tuple-element.40), channel_id=1, source_target_pairs={{0,2},{1,5},{2,0},{3,7},{4,6},{5,1},{6,4},{7,3},{8,10},{9,13},{10,... | collective-permute-start | bytes 2654216 | tf_op jit(solution)/shard_map/ppermute | solution.py:306
  44.4 17.5 %collective-permute-start.15 = (bf16[1,3,192,384]{3,2,1,0:T(8,128)(2,1)S(1)}, bf16[1,3,192,384]{3,2,1,0:T(8,128)(2,1)S(1)}, u32[]{:S(2)}, u32[]{:S(2)}) collective-permute-start(bf16[1,3,192,384]{3,2,1,0:T(8,128)(2,1)S(1)} %shard_map.69), channel_id=1, source_target_pairs={{0,4},{1,3},{2,6},{3,1},{4,0},{5,7},{6,2},{7,5},{8,12},{9,11},{10,... | collective-permute-start | bytes 1327112 | tf_op jit(solution)/shard_map/ppermute | solution.py:307
  58.6 15.0 %collective-permute-start.7 = (bf16[1,3,192,384]{3,2,1,0:T(8,128)(2,1)S(1)}, bf16[1,3,192,384]{3,2,1,0:T(8,128)(2,1)S(1)}, u32[]{:S(2)}, u32[]{:S(2)}) collective-permute-start(bf16[1,3,192,384]{3,2,1,0:T(8,128)(2,1)S(1)} %shard_map.65), channel_id=1, source_target_pairs={{0,4},{1,3},{2,6},{3,1},{4,0},{5,7},{6,2},{7,5},{8,12},{9,11},{10,... | collective-permute-start | bytes 1327112 | tf_op jit(solution)/shard_map/ppermute | solution.py:307
  61.2 16.4 %collective-permute-start.2 = (bf16[6,24,768]{2,1,0:T(8,128)(2,1)S(1)}, bf16[6,24,768]{2,1,0:T(8,128)(2,1)S(1)}, u32[]{:S(2)}, u32[]{:S(2)}) collective-permute-start(bf16[6,24,768]{2,1,0:T(8,128)(2,1)S(1)} %get-tuple-element.32), channel_id=1, source_target_pairs={{0,4},{1,5},{2,6},{3,7},{4,0},{5,1},{6,2},{7,3},{8,12},{9,13},{10,... | collective-permute-start | bytes 663560 | tf_op jit(solution)/shard_map/ppermute | solution.py:352
  61.2 16.3 %collective-permute-start.3 = (bf16[6,24,768]{2,1,0:T(8,128)(2,1)S(1)}, bf16[6,24,768]{2,1,0:T(8,128)(2,1)S(1)}, u32[]{:S(2)}, u32[]{:S(2)}) collective-permute-start(bf16[6,24,768]{2,1,0:T(8,128)(2,1)S(1)} %get-tuple-element.33), channel_id=1, source_target_pairs={{4,8},{5,9},{6,10},{7,11},{8,4},{9,5},{10,6},{11,7},{12,16},{13,17... | collective-permute-start | bytes 663560 | tf_op jit(solution)/shard_map/ppermute | solution.py:352
  63.3 17.4 %collective-permute-start.16 = (bf16[2,144,384]{2,1,0:T(8,128)(2,1)S(1)}, bf16[2,144,384]{2,1,0:T(8,128)(2,1)S(1)}, u32[]{:S(2)}, u32[]{:S(2)}) collective-permute-start(bf16[2,144,384]{2,1,0:T(8,128)(2,1)S(1)} %get-tuple-element.48), channel_id=1, source_target_pairs={{0,8},{1,9},{2,10},{3,11},{4,12},{5,13},{6,14},{7,15},{8,0},{9,1},... | collective-permute-start | bytes 663560 | tf_op jit(solution)/shard_map/ppermute | solution.py:324
  75.0 8.4 %collective-permute-start.8 = (bf16[2,144,384]{2,1,0:T(8,128)(2,1)S(1)}, bf16[2,144,384]{2,1,0:T(8,128)(2,1)S(1)}, u32[]{:S(2)}, u32[]{:S(2)}) collective-permute-start(bf16[2,144,384]{2,1,0:T(8,128)(2,1)S(1)} %get-tuple-element.42), channel_id=1, source_target_pairs={{0,8},{1,9},{2,10},{3,11},{4,12},{5,13},{6,14},{7,15},{8,0},{9,1},... | collective-permute-start | bytes 663560 | tf_op jit(solution)/shard_map/ppermute | solution.py:324
  80.7 4.7 %copy-start.2 = (bf16[6,96,768]{2,1,0:T(8,128)(2,1)S(1)}, bf16[6,96,768]{2,1,0:T(8,128)(2,1)}, u32[]{:S(2)}) copy-start(bf16[6,96,768]{2,1,0:T(8,128)(2,1)} %h_ref.7) | copy-start | bytes 2654212
  80.7 9.0 %collective-permute-start.17 = (bf16[1,144,384]{2,1,0:T(8,128)(2,1)S(1)}, bf16[1,144,384]{2,1,0:T(8,128)(2,1)S(1)}, u32[]{:S(2)}, u32[]{:S(2)}) collective-permute-start(bf16[1,144,384]{2,1,0:T(8,128)(2,1)S(1)} %shard_map.71), channel_id=1, source_target_pairs={{0,16},{1,17},{2,18},{3,19},{4,20},{5,21},{6,22},{7,23},{8,24},{9,... | collective-permute-start | bytes 331784 | tf_op jit(solution)/shard_map/ppermute | solution.py:329
  83.4 6.9 %collective-permute-start.9 = (bf16[1,144,384]{2,1,0:T(8,128)(2,1)S(1)}, bf16[1,144,384]{2,1,0:T(8,128)(2,1)S(1)}, u32[]{:S(2)}, u32[]{:S(2)}) collective-permute-start(bf16[1,144,384]{2,1,0:T(8,128)(2,1)S(1)} %shard_map.67), channel_id=1, source_target_pairs={{0,16},{1,17},{2,18},{3,19},{4,20},{5,21},{6,22},{7,23},{8,24},{9,... | collective-permute-start | bytes 331784 | tf_op jit(solution)/shard_map/ppermute | solution.py:329

commit v3 on v2

--- a/solution.py
+++ b/solution.py
@@ -17,17 +17,20 @@
 CUBE = 0.044715
 
 
-def kernel_call(body, args, outs, flops=0):
+def kernel_call(body, args, outs, flops=0, after=()):
+    if after:
+        inner, first = body, len(args)
+        body = lambda *refs: inner(*refs[:first], *refs[first + len(after) :])
     moved = sum(a.size * a.dtype.itemsize for a in args)
     moved += sum(math.prod(o.shape) * o.dtype.itemsize for o in outs)
     return pl.pallas_call(
         body,
         out_shape=tuple(outs),
-        in_specs=[VMEM] * len(args),
+        in_specs=[VMEM] * len(args) + [pl.BlockSpec(memory_space=pl.ANY)] * len(after),
         out_specs=tuple(VMEM for _ in outs),
         compiler_params=pltpu.CompilerParams(vmem_limit_bytes=VMEM_LIMIT),
         cost_estimate=pl.CostEstimate(flops=flops, bytes_accessed=moved, transcendentals=0),
-    )(*args)
+    )(*args, *after)
 
 
 def shape(dims, dtype=BF16):
@@ -125,12 +128,13 @@
     z_ref[...] = z.reshape(z_ref.shape)
 
 
-def second_body(near, far, z_ref, h_ref, s_ref, a_ref, b_ref, w_ref, h1_ref, s1_ref, keep_ref, send_ref, kx_ref, sx_ref):
+def second_body(near, far, z_ref, h_ref, s_ref, a_ref, b_ref, w_ref, h1_ref, s1_ref, keep_ref, send_ref, kx_ref, sx_ref, na_ref, nb_ref, ends_ref):
     rows = h_ref.shape[1]
     parity, turn = bit_of("dp", 0), bit_of("dp", 1)
     above, below = halos(a_ref, b_ref, far, near)
     above, below = gelu(normed(above)[0]), gelu(normed(below)[0])
     ext = jnp.concatenate([above, s_ref[...].astype(F32), below], axis=1).astype(BF16)
+    ends_ref[:, :far], ends_ref[:, far:] = halos(a_ref, b_ref, 0, far)
     kx_ref[...], sx_ref[...] = quarters(ext, parity, turn)
     add_top = dot(flat(above).astype(BF16), w_ref[0, 0]).reshape(above.shape)
     add_low = dot(flat(below).astype(BF16), w_ref[0, 2]).reshape(below.shape)
@@ -140,37 +144,48 @@
     h1_ref[...] = h1
     s1 = gelu(normed(h1)[0]).astype(BF16)
     s1_ref[...] = s1
+    store_edges(jnp.concatenate([s1[:, :far], s1[:, rows - far :]], axis=1), na_ref, nb_ref, 0)
     keep_ref[...], send_ref[...] = quarters(s1, parity, turn)
 
 
-def back_conv(layer, dtype, above, below, q, w_ref, h_ref, g):
+def back_conv(layer, dtype, above, below, q, w_ref):
     before, own, after = windows(above.astype(dtype), q.astype(dtype), below.astype(dtype))
     e = dot_nt(own.astype(BF16), w_ref[layer, 1])
     e += dot_nt(after.astype(BF16), w_ref[layer, 0])
-    e += dot_nt(before.astype(BF16), w_ref[layer, 2])
+    return e + dot_nt(before.astype(BF16), w_ref[layer, 2])
+
+
+def through_norm(e, h_ref, g):
     act, recip, wide = normed(h_ref[...])
     through = e.reshape(act.shape) * gelu_slope(act)
     inner = jnp.mean(through * wide, axis=-1, keepdims=True)
     return g + recip * through - wide * (recip * recip * recip * inner)
 
 
-def back_body(near, far, count, q_ref, a_ref, b_ref, w_ref, h_ref, s_ref, g_ref, out_ref, mixed_ref, na_ref, nb_ref):
+def back_inner_body(far, q_ref, w_ref, e_ref):
+    edge = jnp.zeros((q_ref.shape[0], far, q_ref.shape[2]), BF16)
+    e_ref[...] = back_conv(1, BF16, edge, edge, q_ref[...], w_ref).reshape(e_ref.shape)
+
+
+def back_body(near, far, count, e_ref, q_ref, a_ref, b_ref, w_ref, h_ref, g_ref, out_ref, mixed_ref, na_ref, nb_ref):
     rows = q_ref.shape[1]
     above, below = halos(a_ref, b_ref, 0, far)
-    g = back_conv(1, BF16, above, below, q_ref[...], w_ref, h_ref, q_ref[...].astype(F32))
+    top = e_ref[:, :far] + dot_nt(flat(above), w_ref[1, 2]).reshape(above.shape)
+    low = e_ref[:, rows - far :] + dot_nt(flat(below), w_ref[1, 0]).reshape(below.shape)
+    e = jnp.concatenate([top, e_ref[:, far : rows - far], low], axis=1)
+    g = through_norm(e, h_ref, q_ref[...].astype(F32))
     g_ref[...] = g
     q = g.astype(BF16)
     out_ref[...] = q
     mixed_ref[...] = by_low_bit(q, count, bit_of("seq", 0))
-    s = jnp.concatenate([s_ref[:, :far], s_ref[:, rows - far :]], axis=1)
-    store_edges(s, na_ref, nb_ref, 0)
     ends = jnp.concatenate([g[:, :near], g[:, rows - near :]], axis=1).astype(BF16)
-    store_edges(ends, na_ref, nb_ref, far)
-
-
-def last_back_body(near, far, q_ref, a_ref, b_ref, w_ref, h_ref, g_ref, out_ref):
-    above, below = halos(a_ref, b_ref, far, near)
-    out_ref[...] = back_conv(0, F32, above, below, q_ref[...], w_ref, h_ref, g_ref[...]).astype(BF16)
+    store_edges(ends, na_ref, nb_ref, 0)
+
+
+def last_back_body(near, q_ref, a_ref, b_ref, w_ref, h_ref, g_ref, out_ref):
+    above, below = halos(a_ref, b_ref, 0, near)
+    e = back_conv(0, F32, above, below, q_ref[...], w_ref)
+    out_ref[...] = through_norm(e, h_ref, g_ref[...]).astype(BF16)
 
 
 def last_body(far, s_ref, a_ref, b_ref, w_ref, h_ref, out_ref):
@@ -200,12 +215,12 @@
         store_grad(tap, dot_tn(s, q), keep_ref, send_ref)
 
 
-def grad_far_body(far, count, s_ref, s2_ref, q_ref, q2_ref, a_ref, b_ref, a2_ref, b2_ref, keep_ref, send_ref):
+def grad_far_body(far, count, s_ref, s2_ref, q_ref, q2_ref, ends_ref, ends2_ref, keep_ref, send_ref):
     turn = bit_of("seq", 0)
     s = jnp.concatenate([flat(s_ref[...]), flat(s2_ref[...])], axis=0)
     taps = []
-    for own_ref, at_a, at_b in ((q_ref, a_ref, b_ref), (q2_ref, a2_ref, b2_ref)):
-        above, below = halos(at_a, at_b, 0, far)
+    for own_ref, at_ref in ((q_ref, ends_ref), (q2_ref, ends2_ref)):
+        above, below = at_ref[:, :far], at_ref[:, far:]
         before, own, after = windows(*(by_low_bit(v, count, turn) for v in (above, own_ref[...], below)))
         taps.append((after, own, before))
     for tap in range(3):
@@ -276,8 +291,10 @@
     s0, z0 = kernel_call(
         partial(first_body, near), [embeddings, kernels], [shape(own), shape(own, F32)], conv_flops
     )
-    other_a, other_b = swap(got_a), swap(got_b)
-    h1, s1, s1_keep, s1_send, s0_keep, s0_send = kernel_call(
+    (e1,) = kernel_call(
+        partial(back_inner_body, far), [cotangent, kernels], [shape(own, F32)], conv_flops
+    )
+    h1, s1, s1_keep, s1_send, s0_keep, s0_send, s1_a, s1_b, ends = kernel_call(
         partial(second_body, near, far),
         [z0, embeddings, s0, got_a, got_b, kernels],
         [
@@ -287,10 +304,15 @@
             shape((batches, rows, half)),
             shape((batches, rows + 2 * near, half)),
             shape((batches, rows + 2 * near, half)),
+            shape((batches, far, channels)),
+            shape((batches, far, channels)),
+            shape((batches, 2 * far, channels)),
         ],
         conv_flops // 10,
-    )
-    s1_other, s0_other = swap(s1_send), swap(s0_send)
+        [e1],
+    )
+    ends_other, s1_other, s0_other = swap(ends), swap(s1_send), swap(s0_send)
+    s1_a, s1_b = to_a(s1_a), to_b(s1_b)
 
     blocks = [shape((2, 3, half // 2, half), F32), shape((2, 3, half // 2, half))]
     count = seqs // 2
@@ -298,13 +320,13 @@
     woven = strip % 16 == 0
     factor = 1.0 / math.sqrt(batches * dps * rows * seqs)
 
-    def passed(keep, got):
-        (send,) = kernel_call(pass_body, [keep, got], [shape((keep.shape[0] // 2, *keep.shape[1:]))])
+    def passed(keep, got, after=()):
+        sent = shape((keep.shape[0] // 2, *keep.shape[1:]))
+        (send,) = kernel_call(pass_body, [keep, got], [sent], after=after)
         return send
 
-    def reduced(keep, send):
-        got = cross_one(send)
-        more = cross_two(passed(keep, got))
+    def reduced(keep, got, after=()):
+        more = cross_two(passed(keep, got, after))
         if woven:
             keep, send, _ = kernel_call(
                 partial(weave_body, count),
@@ -329,33 +351,36 @@
             return keep, got, along(bit)(passed(keep, got))
         return keep, got, jnp.zeros_like(got)
 
+    g1, q0, q0_mixed, send_a, send_b = kernel_call(
+        partial(back_body, near, far, seqs),
+        [e1, cotangent, got_a, got_b, kernels, h1],
+        [shape(own, F32), shape(own), shape(own)] + [shape((batches, near, channels))] * 2,
+        conv_flops // 10,
+    )
+    q0_a, q0_b = to_a(send_a), to_b(send_b)
     keep1, send1 = kernel_call(
         partial(grad_far_body, far, seqs),
-        [s1_keep, s1_other, cotangent, q1_other, got_a, got_b, other_a, other_b],
+        [s1_keep, s1_other, cotangent, q1_other, ends, ends_other],
         blocks,
         conv_flops,
-    )
-    parts1 = reduced(keep1, send1)
-
-    g1, q0, q0_mixed, send_a, send_b = kernel_call(
-        partial(back_body, near, far, seqs),
-        [cotangent, got_a, got_b, kernels, h1, s1],
-        [shape(own, F32), shape(own), shape(own), shape(edges), shape(edges)],
-        conv_flops,
-    )
+        [g1],
+    )
+    half1 = cross_one(send1)
+
     q0_other = swap(q0_mixed)
     keep0, send0 = kernel_call(
-        grad_near_body, [s0_keep, s0_other, q0_mixed, q0_other], blocks, conv_flops
-    )
-    parts0 = reduced(keep0, send0)
-
-    got_a, got_b = to_a(send_a), to_b(send_b)
+        grad_near_body, [s0_keep, s0_other, q0_mixed, q0_other], blocks, conv_flops, [s1_a, s1_b]
+    )
+    half0 = cross_one(send0)
+    parts1 = reduced(keep1, half1, [send0])
+    parts0 = reduced(keep0, half0, [q0_a, q0_b])
+
     (out,) = kernel_call(
-        partial(last_body, far), [s1, got_a, got_b, kernels, h1], [shape(own)], conv_flops
+        partial(last_body, far), [s1, s1_a, s1_b, kernels, h1], [shape(own)], conv_flops
     )
     (grad_in,) = kernel_call(
-        partial(last_back_body, near, far),
-        [q0, got_a, got_b, kernels, embeddings, g1],
+        partial(last_back_body, near),
+        [q0, q0_a, q0_b, kernels, embeddings, g1],
         [shape(own)],
         conv_flops,
     )

time: 91.8 us -> 92.1 us (level)
  starting transfers between devices: 24.7 us -> 32.1 us
  waiting for transfers between devices: 32.4 us -> 27 us
  Pallas kernels: 29.4 us -> 26.1 us
  local copies, waits for them, and re-layouts: 4.2 us -> 5.85 us
    ppermute x8 -> x11, starting transfers between devices: 8.39 us -> 22.2 us  [the longest x2 9.65 us: reduced(): more = cross_two(passed(keep, got, after))]
    ppermute x8 -> x11, waiting for transfers between devices: 28.8 us -> 18.6 us  [the longest x1 8.82 us: per_device(): half0 = cross_one(send0)]
    ppermute x2, waiting for transfers between devices: 0.62 us -> 6.77 us  [reduced(): return (keep, got, along(bit)(passed(keep, got)))]
    ppermute x2, starting transfers between devices: 7.16 us -> 3.15 us  [reduced(): got, bit = (along(2)(send), 4)]
    pallas_call x15 -> x16, Pallas kernels: 29.4 us -> 26.1 us  [kernel_call(): pl.pallas_call(body, out_shape=tuple(outs), in_specs=[VMEM] * len(args) +...]
    ppermute x4 -> x2, waiting for transfers between devices: 2.95 us -> 0.92 us  [per_device(): got_a, got_b = (to_a(send_a), to_b(send_b))]
    ppermute x2, starting transfers between devices: 4.59 us -> 2.89 us  [reduced(): return (keep, got, along(bit)(passed(keep, got)))]
    unnamed x10 -> x12, local copies, waits for them, and re-layouts: 4.2 us -> 5.85 us
  transfers between devices with their start and end apart: 18 -> 19, of which waited for: 7 -> 8; matrix products, arithmetic and copies ran while one was open for 0% -> 0% of each run, Pallas kernels for 30% -> 27%
where the time goes in v3:
time: 92.1 us; the launch traced here: 91.8 us
  starting transfers between devices  32.1 us (35%)
  waiting for transfers between devices  27 us (29%)
  Pallas kernels  26.1 us (28%)
  local copies, waits for them, and re-layouts  5.85 us (6%)
    pallas_call x16, Pallas kernels, kernel_call(): pl.pallas_call(body, out_shape=tuple(outs), in_specs=[VMEM] * len(args) +...  26.1 us
    ppermute x2, starting transfers between devices, reduced(): more = cross_two(passed(keep, got, after))  9.65 us
    ppermute x1, waiting for transfers between devices, per_device(): half0 = cross_one(send0)  8.82 us
    ppermute x2, waiting for transfers between devices, reduced(): return (keep, got, along(bit)(passed(keep, got)))  6.77 us
    unnamed x12, local copies, waits for them, and re-layouts  5.85 us
    ppermute x2, starting transfers between devices, per_device(): q0_a, q0_b = (to_a(send_a), to_b(send_b))  5.19 us
    ppermute x2, starting transfers between devices, per_device(): s1_a, s1_b = (to_a(s1_a), to_b(s1_b))  4.22 us
    ppermute x2, waiting for transfers between devices, reduced(): more = cross_two(passed(keep, got, after))  3.34 us
  transfers between devices with their start and end apart: 19, of which 8 were waited for; matrix products, arithmetic and copies ran while one was open for 0% of the time, Pallas kernels for 27%

profile of v3, /device:TPU:0, one launch (start us, length us, event | category | flops | bytes accessed | tf_op | source)
XLA Modules:
  0.0 91.8 jit_solution(16883143496544501228)
XLA Ops:
  1.1 1.2 %copy-done.2 = bf16[6,96,768]{2,1,0:T(8,128)(2,1)S(1)} copy-done((bf16[6,96,768]{2,1,0:T(8,128)(2,1)S(1)}, bf16[6,96,768]{2,1,0:T(8,128)(2,1)}, u32[]{:S(2)}) %copy-start.2) | copy-done | bytes 884760
  2.3 1.2 %copy-done.4 = bf16[6,96,768]{2,1,0:T(8,128)(2,1)S(1)} copy-done((bf16[6,96,768]{2,1,0:T(8,128)(2,1)S(1)}, bf16[6,96,768]{2,1,0:T(8,128)(2,1)}, u32[]{:S(2)}) %copy-start.4) | copy-done | bytes 884760
  3.6 2.6 %collective-permute-start = (bf16[6,24,768]{2,1,0:T(8,128)(2,1)S(1)}, bf16[6,24,768]{2,1,0:T(8,128)(2,1)S(1)}, u32[]{:S(2)}, u32[]{:S(2)}) collective-permute-start(bf16[6,24,768]{2,1,0:T(8,128)(2,1)S(1)} %get-tuple-element.31), channel_id=1, source_target_pairs={{0,4},{1,5},{2,6},{3,7},{4,0},{5,1},{6,2},{7,3},{8,12},{9,13},{10,... | collective-permute-start | bytes 663560 | tf_op jit(solution)/shard_map/ppermute | solution.py:289
  6.8 3.0 %copy-done = bf16[2,3,768,768]{3,2,1,0:T(8,128)(2,1)S(1)} copy-done((bf16[2,3,768,768]{3,2,1,0:T(8,128)(2,1)S(1)}, bf16[2,3,768,768]{3,2,1,0:T(8,128)(2,1)}, u32[]{:S(2)}) %copy-start) | copy-done | bytes 7077912
  9.8 2.7 %shard_map.58 = (bf16[6,96,768]{2,1,0:T(8,128)(2,1)S(1)}, f32[6,96,768]{2,1,0:T(8,128)S(1)}) custom-call(bf16[6,96,768]{2,1,0:T(8,128)(2,1)S(1)} %copy-done.2, bf16[2,3,768,768]{3,2,1,0:T(8,128)(2,1)S(1)} %copy-done), custom_call_target="tpu_custom_call" | custom-call | flops 2038431744 | bytes 10616832 | tf_op jit(solution)/shard_map/pallas_call | solution.py:26
  13.1 2.3 %shard_map.60.refs_6_.e_ref = f32[6,96,768]{2,1,0:T(8,128)S(1)} custom-call(bf16[6,96,768]{2,1,0:T(8,128)(2,1)S(1)} %copy-done.5, bf16[2,3,768,768]{3,2,1,0:T(8,128)(2,1)S(1)} %copy-done.1), custom_call_target="tpu_custom_call" | custom-call | flops 2038431744 | bytes 9732096 | tf_op jit(solution)/shard_map/pallas_call | solution.py:26
  15.3 0.9 collective-permute-done.refs_3_.a_ref
  16.2 1.8 %shard_map.61 = (bf16[6,96,768]{2,1,0:T(8,128)(2,1)S(1)}, bf16[6,96,768]{2,1,0:T(8,128)(2,1)S(1)}, bf16[6,96,384]{2,1,0:T(8,128)(2,1)S(1)}, bf16[6,96,384]{2,1,0...) custom-call(f32[6,96,768]{2,1,0:T(8,128)S(1)} %get-tuple-element.29., ...), custom_call_target="tpu_custom_call" | custom-call | flops 203843168 | bytes 15335424 | tf_op jit(solution)/shard_map/pallas_call | solution.py:26
  18.1 2.2 %shard_map.63 = (f32[6,96,768]{2,1,0:T(8,128)S(1)}, bf16[6,96,768]{2,1,0:T(8,128)(2,1)S(1)}, bf16[6,96,768]{2,1,0:T(8,128)(2,1)S(1)}, bf16[6,8,768]{2,1,0:T(8,128)(2,1)S(1)}, bf16[6,8,768]{2,1,0:T(8,128)(2,1)S(1)}) custom-call(f32[6,96,768]{2,1,0:T(8,128)S(1)} %shard_map.60.refs_6_.e_ref, bf16[6,96,768]{2,1,0:T(8,128)(2,1)S(1)} %copy-done.5, ...), custom_call_target="tpu_custom_call" | custom-call | flops 203843168 | bytes 14745600 | tf_op jit(solution)/shard_map/pallas_call | solution.py:26
  21.3 3.2 %collective-permute-done.14.refs_5_ = bf16[6,32,768]{2,1,0:T(8,128)(2,1)S(1)} collective-permute-done((bf16[6,32,768]{2,1,0:T(8,128)(2,1)S(1)}, bf16[6,32,768]{2,1,0:T(8,128)(2,1)S(1)}, u32[]{:S(2)}, u32[]{:S(2)}) %collective-permute-start.14) | collective-permute-done | bytes 294944 | tf_op jit(solution)/shard_map/ppermute | solution.py:314
  24.5 3.4 %collective-permute-start.2 = (bf16[6,16,768]{2,1,0:T(8,128)(2,1)S(1)}, bf16[6,16,768]{2,1,0:T(8,128)(2,1)S(1)}, u32[]{:S(2)}, u32[]{:S(2)}) collective-permute-start(bf16[6,16,768]{2,1,0:T(8,128)(2,1)S(1)} %get-tuple-element.34), channel_id=1, source_target_pairs={{0,4},{1,5},{2,6},{3,7},{4,0},{5,1},{6,2},{7,3},{8,12},{9,13},{10,... | collective-permute-start | bytes 442376 | tf_op jit(solution)/shard_map/ppermute | solution.py:315
  27.9 0.8 collective-permute-start.3
  28.8 3.0 %shard_map.69 = (f32[2,3,192,384]{3,2,1,0:T(8,128)S(1)}, bf16[2,3,192,384]{3,2,1,0:T(8,128)(2,1)S(1)}) custom-call(bf16[6,96,384]{2,1,0:T(8,128)(2,1)S(1)} %get-tuple-element.48.refs_0_, bf16[6,96,384]{2,1,0:T(8,128)(2,1)S(1)} %collective-permute-done.12.refs_1_, bf16[6,96,768]{2,1,0:T(8,128)(2,1)S(1)} %copy-done.5, ...), custom_call_target="tpu_custom_call" | custom-call | flops 2038431744 | bytes 5898240 | tf_op jit(solution)/shard_map/pallas_call | solution.py:26
  31.8 1.6 %collective-permute-start.15 = (bf16[2,3,192,384]{3,2,1,0:T(8,128)(2,1)S(1)}, bf16[2,3,192,384]{3,2,1,0:T(8,128)(2,1)S(1)}, u32[]{:S(2)}, u32[]{:S(2)}) collective-permute-start(bf16[2,3,192,384]{3,2,1,0:T(8,128)(2,1)S(1)} %get-tuple-element.52), channel_id=1, source_target_pairs={{0,2},{1,5},{2,0},{3,7},{4,6},{5,1},{6,4},{7,3},{8,10},{9,13},{10,... | collective-permute-start | bytes 2654216 | tf_op jit(solution)/shard_map/ppermute | solution.py:368
  33.4 2.5 %shard_map.65 = (f32[2,3,192,384]{3,2,1,0:T(8,128)S(1)}, bf16[2,3,192,384]{3,2,1,0:T(8,128)(2,1)S(1)}) custom-call(bf16[6,112,384]{2,1,0:T(8,128)(2,1)S(1)} %get-tuple-element.41.refs_0_, bf16[6,112,384]{2,1,0:T(8,128)(2,1)S(1)} %collective-permute-done.6.refs_1_, bf16[6,96,768]{2,1,0:T(8,128)(2,1)S(1)} %get-tuple-element.43.refs_2_, ...), custom_call_target="tpu_custom_call" | custom-call | flops 2038431744 | bytes 5455872 | tf_op jit(solution)/shard_map/pallas_call | solution.py:26
  36.5 4.5 %collective-permute-start.4 = (bf16[6,8,768]{2,1,0:T(8,128)(2,1)S(1)}, bf16[6,8,768]{2,1,0:T(8,128)(2,1)S(1)}, u32[]{:S(2)}, u32[]{:S(2)}) collective-permute-start(bf16[6,8,768]{2,1,0:T(8,128)(2,1)S(1)} %get-tuple-element.38), channel_id=1, source_target_pairs={{0,4},{1,5},{2,6},{3,7},{4,0},{5,1},{6,2},{7,3},{8,12},{9,13},{10,... | collective-permute-start | bytes 221192 | tf_op jit(solution)/shard_map/ppermute | solution.py:360
  41.7 3.2 %collective-permute-done.15.refs_1_.got_ref = bf16[2,3,192,384]{3,2,1,0:T(8,128)(2,1)S(1)} collective-permute-done((bf16[2,3,192,384]{3,2,1,0:T(8,128)(2,1)S(1)}, bf16[2,3,192,384]{3,2,1,0:T(8,128)(2,1)S(1)}, u32[]{:S(2)}, u32[]{:S(2)}) %collective-permute-start.15) | collective-permute-done | bytes 884768 | tf_op jit(solution)/shard_map/ppermute | solution.py:368
  45.0 4.3 %collective-permute-start.16 = (bf16[1,3,192,384]{3,2,1,0:T(8,128)(2,1)S(1)}, bf16[1,3,192,384]{3,2,1,0:T(8,128)(2,1)S(1)}, u32[]{:S(2)}, u32[]{:S(2)}) collective-permute-start(bf16[1,3,192,384]{3,2,1,0:T(8,128)(2,1)S(1)} %shard_map.70), channel_id=1, source_target_pairs={{0,4},{1,3},{2,6},{3,1},{4,0},{5,7},{6,2},{7,5},{8,12},{9,11},{10,... | collective-permute-start | bytes 1327112 | tf_op jit(solution)/shard_map/ppermute | solution.py:329
  49.4 8.8 %collective-permute-done.8.refs_1_.got_ref = bf16[2,3,192,384]{3,2,1,0:T(8,128)(2,1)S(1)} collective-permute-done((bf16[2,3,192,384]{3,2,1,0:T(8,128)(2,1)S(1)}, bf16[2,3,192,384]{3,2,1,0:T(8,128)(2,1)S(1)}, u32[]{:S(2)}, u32[]{:S(2)}) %collective-permute-start.8) | collective-permute-done | bytes 884768 | tf_op jit(solution)/shard_map/ppermute | solution.py:374
  58.3 5.3 %collective-permute-start.9 = (bf16[1,3,192,384]{3,2,1,0:T(8,128)(2,1)S(1)}, bf16[1,3,192,384]{3,2,1,0:T(8,128)(2,1)S(1)}, u32[]{:S(2)}, u32[]{:S(2)}) collective-permute-start(bf16[1,3,192,384]{3,2,1,0:T(8,128)(2,1)S(1)} %shard_map.66), channel_id=1, source_target_pairs={{0,4},{1,3},{2,6},{3,1},{4,0},{5,7},{6,2},{7,5},{8,12},{9,11},{10,... | collective-permute-start | bytes 1327112 | tf_op jit(solution)/shard_map/ppermute | solution.py:329
  63.6 1.4 %shard_map.71 = (f32[2,144,384]{2,1,0:T(8,128)S(1)}, bf16[2,144,384]{2,1,0:T(8,128)(2,1)S(1)}, f32[4,144,384]{2,1,0:T(8,128)}) custom-call(f32[2,3,192,384]{3,2,1,0:T(8,128)S(1)} %get-tuple-element.51.refs_0_.keep_ref, bf16[2,3,192,384]{3,2,1,0:T(8,128)(2,1)S(1)} %collective-permute-done.15.refs_1_.got_ref, ...), custom_call_target="tpu_custom_call" | custom-call | bytes 4644864 | tf_op jit(solution)/shard_map/pallas_call | solution.py:26
  64.9 1.6 %collective-permute-start.17 = (bf16[2,144,384]{2,1,0:T(8,128)(2,1)S(1)}, bf16[2,144,384]{2,1,0:T(8,128)(2,1)S(1)}, u32[]{:S(2)}, u32[]{:S(2)}) collective-permute-start(bf16[2,144,384]{2,1,0:T(8,128)(2,1)S(1)} %get-tuple-element.54), channel_id=1, source_target_pairs={{0,8},{1,9},{2,10},{3,11},{4,12},{5,13},{6,14},{7,15},{8,0},{9,1},... | collective-permute-start | bytes 663560 | tf_op jit(solution)/shard_map/ppermute | solution.py:346
  66.5 3.3 %collective-permute-done.9.more_ref = bf16[1,3,192,384]{3,2,1,0:T(8,128)(2,1)S(1)} collective-permute-done((bf16[1,3,192,384]{3,2,1,0:T(8,128)(2,1)S(1)}, bf16[1,3,192,384]{3,2,1,0:T(8,128)(2,1)S(1)}, u32[]{:S(2)}, u32[]{:S(2)}) %collective-permute-start.9) | collective-permute-done | bytes 442400 | tf_op jit(solution)/shard_map/ppermute | solution.py:329
  69.9 1.4 %shard_map.67 = (f32[2,144,384]{2,1,0:T(8,128)S(1)}, bf16[2,144,384]{2,1,0:T(8,128)(2,1)S(1)}, f32[4,144,384]{2,1,0:T(8,128)}) custom-call(f32[2,3,192,384]{3,2,1,0:T(8,128)S(1)} %get-tuple-element.44.refs_0_.keep_ref, bf16[2,3,192,384]{3,2,1,0:T(8,128)(2,1)S(1)} %collective-permute-done.8.refs_1_.got_ref, ...), custom_call_target="tpu_custom_call" | custom-call | bytes 4644864 | tf_op jit(solution)/shard_map/pallas_call | solution.py:26
  71.2 1.6 %collective-permute-start.10 = (bf16[2,144,384]{2,1,0:T(8,128)(2,1)S(1)}, bf16[2,144,384]{2,1,0:T(8,128)(2,1)S(1)}, u32[]{:S(2)}, u32[]{:S(2)}) collective-permute-start(bf16[2,144,384]{2,1,0:T(8,128)(2,1)S(1)} %get-tuple-element.47), channel_id=1, source_target_pairs={{0,8},{1,9},{2,10},{3,11},{4,12},{5,13},{6,14},{7,15},{8,0},{9,1},... | collective-permute-start | bytes 663560 | tf_op jit(solution)/shard_map/ppermute | solution.py:346
  72.8 4.4 %shard_map.64 = bf16[6,96,768]{2,1,0:T(8,128)(2,1)} custom-call(bf16[6,96,768]{2,1,0:T(8,128)(2,1)S(1)} %get-tuple-element.37.q_ref, bf16[6,8,768]{2,1,0:T(8,128)(2,1)S(1)} %collective-permute-done.4.a_ref.refs_2_, bf16[6,8,768]{2,1,0:T(8,128)(2,1)S(1)} %collective-permute-done.5.b_ref.refs_3_, bf16[2,3,768,768]{3,2,1,0:T(8,128)(2,1)S(1)} %copy-done.1, ...), custom_call_target="tpu_custom_call" | custom-call | flops 2038431744 | bytes 11649024 | tf_op jit(solution)/shard_map/pallas_call | solution.py:26
  77.2 1.5 %collective-permute-start.18 = (bf16[1,144,384]{2,1,0:T(8,128)(2,1)S(1)}, bf16[1,144,384]{2,1,0:T(8,128)(2,1)S(1)}, u32[]{:S(2)}, u32[]{:S(2)}) collective-permute-start(bf16[1,144,384]{2,1,0:T(8,128)(2,1)S(1)} %shard_map.72), channel_id=1, source_target_pairs={{0,16},{1,17},{2,18},{3,19},{4,20},{5,21},{6,22},{7,23},{8,24},{9,... | collective-permute-start | bytes 331784 | tf_op jit(solution)/shard_map/ppermute | solution.py:351
  79.4 1.4 %collective-permute-start.11 = (bf16[1,144,384]{2,1,0:T(8,128)(2,1)S(1)}, bf16[1,144,384]{2,1,0:T(8,128)(2,1)S(1)}, u32[]{:S(2)}, u32[]{:S(2)}) collective-permute-start(bf16[1,144,384]{2,1,0:T(8,128)(2,1)S(1)} %shard_map.68), channel_id=1, source_target_pairs={{0,16},{1,17},{2,18},{3,19},{4,20},{5,21},{6,22},{7,23},{8,24},{9,... | collective-permute-start | bytes 331784 | tf_op jit(solution)/shard_map/ppermute | solution.py:351
  80.8 3.1 %shard_map.62 = bf16[6,96,768]{2,1,0:T(8,128)(2,1)} custom-call(bf16[6,96,768]{2,1,0:T(8,128)(2,1)S(1)} %get-tuple-element.33.s_ref, bf16[6,16,768]{2,1,0:T(8,128)(2,1)S(1)} %collective-permute-done.2.a_ref.refs_4_, bf16[6,16,768]{2,1,0:T(8,128)(2,1)S(1)} %collective-permute-done.3.b_ref.refs_5_, bf16[2,3,768,768]{3,2,1,0:T(8,128)(2,1)S(1)} %copy-done.1, ...), custom_call_target="tpu_custom_call" | custom-call | flops 2038431744 | bytes 10027008 | tf_op jit(solution)/shard_map/pallas_call | solution.py:26
  83.9 4.4 %collective-permute-done.18.refs_5_ = bf16[1,144,384]{2,1,0:T(8,128)(2,1)S(1)} collective-permute-done((bf16[1,144,384]{2,1,0:T(8,128)(2,1)S(1)}, bf16[1,144,384]{2,1,0:T(8,128)(2,1)S(1)}, u32[]{:S(2)}, u32[]{:S(2)}) %collective-permute-start.18) | collective-permute-done | bytes 110624 | tf_op jit(solution)/shard_map/ppermute | solution.py:351
  88.4 2.4 %collective-permute-done.11.refs_2_ = bf16[1,144,384]{2,1,0:T(8,128)(2,1)S(1)} collective-permute-done((bf16[1,144,384]{2,1,0:T(8,128)(2,1)S(1)}, bf16[1,144,384]{2,1,0:T(8,128)(2,1)S(1)}, u32[]{:S(2)}, u32[]{:S(2)}) %collective-permute-start.11) | collective-permute-done | bytes 110624 | tf_op jit(solution)/shard_map/ppermute | solution.py:351
  90.7 1.1 %shard_map.73 = f32[2,3,192,96]{3,2,1,0:T(8,128)} custom-call(f32[2,144,384]{2,1,0:T(8,128)S(1)} %get-tuple-element.46.keep_ref.refs_0_, bf16[2,144,384]{2,1,0:T(8,128)(2,1)S(1)} %collective-permute-done.10.got_ref.refs_1_, bf16[1,144,384]{2,1,0:T(8,128)(2,1)S(1)} %collective-permute-done.11.refs_2_, f32[2,144,384]{2,1,0:T(8,128)S(1)} %get-tuple-element.53.keep_ref.refs_3_, ...), custom_call_target="tpu_custom_call" | custom-call | bytes 1990656 | tf_op jit(solution)/shard_map/pallas_call | solution.py:26
  (34 shorter events, 5.0 us)
Async XLA Ops:
  0.6 28.1 %collective-permute-start.13 = (bf16[6,96,768]{2,1,0:T(8,128)(2,1)}, bf16[6,96,768]{2,1,0:T(8,128)(2,1)S(1)}, u32[]{:S(2)}, u32[]{:S(2)}) collective-permute-start(bf16[6,96,768]{2,1,0:T(8,128)(2,1)} %refs_2_.1), channel_id=1, source_target_pairs={{0,1},{1,0},{2,3},{3,2},{4,5},{5,4},{6,7},{7,6},{8,9},{9,8},{10,11... | collective-permute-start | bytes 2654216 | tf_op jit(solution)/shard_map/ppermute | solution.py:290
  1.1 1.2 %copy-start.2 = (bf16[6,96,768]{2,1,0:T(8,128)(2,1)S(1)}, bf16[6,96,768]{2,1,0:T(8,128)(2,1)}, u32[]{:S(2)}) copy-start(bf16[6,96,768]{2,1,0:T(8,128)(2,1)} %h_ref.5) | copy-start | bytes 2654212
  2.3 1.2 %copy-start.4 = (bf16[6,96,768]{2,1,0:T(8,128)(2,1)S(1)}, bf16[6,96,768]{2,1,0:T(8,128)(2,1)}, u32[]{:S(2)}) copy-start(bf16[6,96,768]{2,1,0:T(8,128)(2,1)} %refs_2_.1) | copy-start | bytes 2654212
  3.6 12.7 %collective-permute-start = (bf16[6,24,768]{2,1,0:T(8,128)(2,1)S(1)}, bf16[6,24,768]{2,1,0:T(8,128)(2,1)S(1)}, u32[]{:S(2)}, u32[]{:S(2)}) collective-permute-start(bf16[6,24,768]{2,1,0:T(8,128)(2,1)S(1)} %get-tuple-element.31), channel_id=1, source_target_pairs={{0,4},{1,5},{2,6},{3,7},{4,0},{5,1},{6,2},{7,3},{8,12},{9,13},{10,... | collective-permute-start | bytes 663560 | tf_op jit(solution)/shard_map/ppermute | solution.py:289
  6.2 10.1 %collective-permute-start.1 = (bf16[6,24,768]{2,1,0:T(8,128)(2,1)S(1)}, bf16[6,24,768]{2,1,0:T(8,128)(2,1)S(1)}, u32[]{:S(2)}, u32[]{:S(2)}) collective-permute-start(bf16[6,24,768]{2,1,0:T(8,128)(2,1)S(1)} %get-tuple-element.32), channel_id=1, source_target_pairs={{4,8},{5,9},{6,10},{7,11},{8,4},{9,5},{10,6},{11,7},{12,16},{13,17... | collective-permute-start | bytes 663560 | tf_op jit(solution)/shard_map/ppermute | solution.py:289
  6.8 3.0 %copy-start = (bf16[2,3,768,768]{3,2,1,0:T(8,128)(2,1)S(1)}, bf16[2,3,768,768]{3,2,1,0:T(8,128)(2,1)}, u32[]{:S(2)}) copy-start(bf16[2,3,768,768]{3,2,1,0:T(8,128)(2,1)} %w_ref.9) | copy-start | bytes 21233668
  9.8 3.0 %copy-start.1 = (bf16[2,3,768,768]{3,2,1,0:T(8,128)(2,1)S(1)}, bf16[2,3,768,768]{3,2,1,0:T(8,128)(2,1)}, u32[]{:S(2)}) copy-start(bf16[2,3,768,768]{3,2,1,0:T(8,128)(2,1)} %w_ref.9) | copy-start | bytes 21233668
  9.8 3.2 %copy-start.5 = (bf16[6,96,768]{2,1,0:T(8,128)(2,1)S(1)}, bf16[6,96,768]{2,1,0:T(8,128)(2,1)}, u32[]{:S(2)}) copy-start(bf16[6,96,768]{2,1,0:T(8,128)(2,1)} %refs_2_.1) | copy-start | bytes 2654212
  20.3 13.1 %collective-permute-start.7 = (bf16[6,96,768]{2,1,0:T(8,128)(2,1)S(1)}, bf16[6,96,768]{2,1,0:T(8,128)(2,1)S(1)}, u32[]{:S(2)}, u32[]{:S(2)}) collective-permute-start(bf16[6,96,768]{2,1,0:T(8,128)(2,1)S(1)} %get-tuple-element.43.refs_2_), channel_id=1, source_target_pairs={{0,1},{1,0},{2,3},{3,2},{4,5},{5,4},{6,7},{7,6},{8,9},{9,8},{10,11... | collective-permute-start | bytes 2654216 | tf_op jit(solution)/shard_map/ppermute | solution.py:370
  20.3 7.6 %collective-permute-start.12 = (bf16[6,96,384]{2,1,0:T(8,128)(2,1)S(1)}, bf16[6,96,384]{2,1,0:T(8,128)(2,1)S(1)}, u32[]{:S(2)}, u32[]{:S(2)}) collective-permute-start(bf16[6,96,384]{2,1,0:T(8,128)(2,1)S(1)} %get-tuple-element.49), channel_id=1, source_target_pairs={{0,1},{1,0},{2,3},{3,2},{4,5},{5,4},{6,7},{7,6},{8,9},{9,8},{10,11... | collective-permute-start | bytes 1327112 | tf_op jit(solution)/shard_map/ppermute | solution.py:314
  20.8 12.6 %collective-permute-start.6 = (bf16[6,112,384]{2,1,0:T(8,128)(2,1)S(1)}, bf16[6,112,384]{2,1,0:T(8,128)(2,1)S(1)}, u32[]{:S(2)}, u32[]{:S(2)}) collective-permute-start(bf16[6,112,384]{2,1,0:T(8,128)(2,1)S(1)} %get-tuple-element.42), channel_id=1, source_target_pairs={{0,1},{1,0},{2,3},{3,2},{4,5},{5,4},{6,7},{7,6},{8,9},{9,8},{10,11... | collective-permute-start | bytes 1548296 | tf_op jit(solution)/shard_map/ppermute | solution.py:314
  20.9 3.6 %collective-permute-start.14 = (bf16[6,32,768]{2,1,0:T(8,128)(2,1)S(1)}, bf16[6,32,768]{2,1,0:T(8,128)(2,1)S(1)}, u32[]{:S(2)}, u32[]{:S(2)}) collective-permute-start(bf16[6,32,768]{2,1,0:T(8,128)(2,1)S(1)} %get-tuple-element.50.refs_4_), channel_id=1, source_target_pairs={{0,1},{1,0},{2,3},{3,2},{4,5},{5,4},{6,7},{7,6},{8,9},{9,8},{10,11... | collective-permute-start | bytes 884744 | tf_op jit(solution)/shard_map/ppermute | solution.py:314
  24.5 8.8 %collective-permute-start.2 = (bf16[6,16,768]{2,1,0:T(8,128)(2,1)S(1)}, bf16[6,16,768]{2,1,0:T(8,128)(2,1)S(1)}, u32[]{:S(2)}, u32[]{:S(2)}) collective-permute-start(bf16[6,16,768]{2,1,0:T(8,128)(2,1)S(1)} %get-tuple-element.34), channel_id=1, source_target_pairs={{0,4},{1,5},{2,6},{3,7},{4,0},{5,1},{6,2},{7,3},{8,12},{9,13},{10,... | collective-permute-start | bytes 442376 | tf_op jit(solution)/shard_map/ppermute | solution.py:315
  27.9 5.5 %collective-permute-start.3 = (bf16[6,16,768]{2,1,0:T(8,128)(2,1)S(1)}, bf16[6,16,768]{2,1,0:T(8,128)(2,1)S(1)}, u32[]{:S(2)}, u32[]{:S(2)}) collective-permute-start(bf16[6,16,768]{2,1,0:T(8,128)(2,1)S(1)} %get-tuple-element.35), channel_id=1, source_target_pairs={{4,8},{5,9},{6,10},{7,11},{8,4},{9,5},{10,6},{11,7},{12,16},{13,17... | collective-permute-start | bytes 442376 | tf_op jit(solution)/shard_map/ppermute | solution.py:315
  31.8 13.1 %collective-permute-start.15 = (bf16[2,3,192,384]{3,2,1,0:T(8,128)(2,1)S(1)}, bf16[2,3,192,384]{3,2,1,0:T(8,128)(2,1)S(1)}, u32[]{:S(2)}, u32[]{:S(2)}) collective-permute-start(bf16[2,3,192,384]{3,2,1,0:T(8,128)(2,1)S(1)} %get-tuple-element.52), channel_id=1, source_target_pairs={{0,2},{1,5},{2,0},{3,7},{4,6},{5,1},{6,4},{7,3},{8,10},{9,13},{10,... | collective-permute-start | bytes 2654216 | tf_op jit(solution)/shard_map/ppermute | solution.py:368
  35.9 22.3 %collective-permute-start.8 = (bf16[2,3,192,384]{3,2,1,0:T(8,128)(2,1)S(1)}, bf16[2,3,192,384]{3,2,1,0:T(8,128)(2,1)S(1)}, u32[]{:S(2)}, u32[]{:S(2)}) collective-permute-start(bf16[2,3,192,384]{3,2,1,0:T(8,128)(2,1)S(1)} %get-tuple-element.45.refs_2_), channel_id=1, source_target_pairs={{0,2},{1,5},{2,0},{3,7},{4,6},{5,1},{6,4},{7,3},{8,10},{9,13},{10,... | collective-permute-start | bytes 2654216 | tf_op jit(solution)/shard_map/ppermute | solution.py:374
  36.5 12.9 %collective-permute-start.4 = (bf16[6,8,768]{2,1,0:T(8,128)(2,1)S(1)}, bf16[6,8,768]{2,1,0:T(8,128)(2,1)S(1)}, u32[]{:S(2)}, u32[]{:S(2)}) collective-permute-start(bf16[6,8,768]{2,1,0:T(8,128)(2,1)S(1)} %get-tuple-element.38), channel_id=1, source_target_pairs={{0,4},{1,5},{2,6},{3,7},{4,0},{5,1},{6,2},{7,3},{8,12},{9,13},{10,... | collective-permute-start | bytes 221192 | tf_op jit(solution)/shard_map/ppermute | solution.py:360
  41.0 8.3 %collective-permute-start.5 = (bf16[6,8,768]{2,1,0:T(8,128)(2,1)S(1)}, bf16[6,8,768]{2,1,0:T(8,128)(2,1)S(1)}, u32[]{:S(2)}, u32[]{:S(2)}) collective-permute-start(bf16[6,8,768]{2,1,0:T(8,128)(2,1)S(1)} %get-tuple-element.39), channel_id=1, source_target_pairs={{4,8},{5,9},{6,10},{7,11},{8,4},{9,5},{10,6},{11,7},{12,16},{13,17... | collective-permute-start | bytes 221192 | tf_op jit(solution)/shard_map/ppermute | solution.py:360
  45.0 18.6 %collective-permute-start.16 = (bf16[1,3,192,384]{3,2,1,0:T(8,128)(2,1)S(1)}, bf16[1,3,192,384]{3,2,1,0:T(8,128)(2,1)S(1)}, u32[]{:S(2)}, u32[]{:S(2)}) collective-permute-start(bf16[1,3,192,384]{3,2,1,0:T(8,128)(2,1)S(1)} %shard_map.70), channel_id=1, source_target_pairs={{0,4},{1,3},{2,6},{3,1},{4,0},{5,7},{6,2},{7,5},{8,12},{9,11},{10,... | collective-permute-start | bytes 1327112 | tf_op jit(solution)/shard_map/ppermute | solution.py:329
  58.3 11.6 %collective-permute-start.9 = (bf16[1,3,192,384]{3,2,1,0:T(8,128)(2,1)S(1)}, bf16[1,3,192,384]{3,2,1,0:T(8,128)(2,1)S(1)}, u32[]{:S(2)}, u32[]{:S(2)}) collective-permute-start(bf16[1,3,192,384]{3,2,1,0:T(8,128)(2,1)S(1)} %shard_map.66), channel_id=1, source_target_pairs={{0,4},{1,3},{2,6},{3,1},{4,0},{5,7},{6,2},{7,5},{8,12},{9,11},{10,... | collective-permute-start | bytes 1327112 | tf_op jit(solution)/shard_map/ppermute | solution.py:329
  64.9 7.9 %copy-start.3 = (bf16[6,96,768]{2,1,0:T(8,128)(2,1)S(1)}, bf16[6,96,768]{2,1,0:T(8,128)(2,1)}, u32[]{:S(2)}) copy-start(bf16[6,96,768]{2,1,0:T(8,128)(2,1)} %h_ref.5) | copy-start | bytes 2654212
  64.9 12.2 %collective-permute-start.17 = (bf16[2,144,384]{2,1,0:T(8,128)(2,1)S(1)}, bf16[2,144,384]{2,1,0:T(8,128)(2,1)S(1)}, u32[]{:S(2)}, u32[]{:S(2)}) collective-permute-start(bf16[2,144,384]{2,1,0:T(8,128)(2,1)S(1)} %get-tuple-element.54), channel_id=1, source_target_pairs={{0,8},{1,9},{2,10},{3,11},{4,12},{5,13},{6,14},{7,15},{8,0},{9,1},... | collective-permute-start | bytes 663560 | tf_op jit(solution)/shard_map/ppermute | solution.py:346
  71.2 8.2 %collective-permute-start.10 = (bf16[2,144,384]{2,1,0:T(8,128)(2,1)S(1)}, bf16[2,144,384]{2,1,0:T(8,128)(2,1)S(1)}, u32[]{:S(2)}, u32[]{:S(2)}) collective-permute-start(bf16[2,144,384]{2,1,0:T(8,128)(2,1)S(1)} %get-tuple-element.47), channel_id=1, source_target_pairs={{0,8},{1,9},{2,10},{3,11},{4,12},{5,13},{6,14},{7,15},{8,0},{9,1},... | collective-permute-start | bytes 663560 | tf_op jit(solution)/shard_map/ppermute | solution.py:346
  77.2 11.1 %collective-permute-start.18 = (bf16[1,144,384]{2,1,0:T(8,128)(2,1)S(1)}, bf16[1,144,384]{2,1,0:T(8,128)(2,1)S(1)}, u32[]{:S(2)}, u32[]{:S(2)}) collective-permute-start(bf16[1,144,384]{2,1,0:T(8,128)(2,1)S(1)} %shard_map.72), channel_id=1, source_target_pairs={{0,16},{1,17},{2,18},{3,19},{4,20},{5,21},{6,22},{7,23},{8,24},{9,... | collective-permute-start | bytes 331784 | tf_op jit(solution)/shard_map/ppermute | solution.py:351
  79.4 11.3 %collective-permute-start.11 = (bf16[1,144,384]{2,1,0:T(8,128)(2,1)S(1)}, bf16[1,144,384]{2,1,0:T(8,128)(2,1)S(1)}, u32[]{:S(2)}, u32[]{:S(2)}) collective-permute-start(bf16[1,144,384]{2,1,0:T(8,128)(2,1)S(1)} %shard_map.68), channel_id=1, source_target_pairs={{0,16},{1,17},{2,18},{3,19},{4,20},{5,21},{6,22},{7,23},{8,24},{9,... | collective-permute-start | bytes 331784 | tf_op jit(solution)/shard_map/ppermute | solution.py:351

commit v4 on v3

--- a/solution.py
+++ b/solution.py
@@ -242,8 +242,8 @@
         )
     mine = lax.axis_index("seq") >> 1
     for slot in range(count // 2):
-        out_ref[slot] = all_ref[mine ^ (2 * slot)]
-        send_ref[slot] = all_ref[mine ^ (2 * slot + 1)].astype(BF16)
+        out_ref[slot] = all_ref[mine ^ (3 * slot)]
+        send_ref[slot] = all_ref[mine ^ 1 ^ (3 * slot)].astype(BF16)
 
 
 def final_body(count, factor, *refs):
@@ -309,7 +309,7 @@
             shape((batches, 2 * far, channels)),
         ],
         conv_flops // 10,
-        [e1],
+        [e1, q1_other],
     )
     ends_other, s1_other, s0_other = swap(ends), swap(s1_send), swap(s0_send)
     s1_a, s1_b = to_a(s1_a), to_b(s1_b)
@@ -317,7 +317,7 @@
     blocks = [shape((2, 3, half // 2, half), F32), shape((2, 3, half // 2, half))]
     count = seqs // 2
     strip = 3 * (half // 2) // count
-    woven = strip % 16 == 0
+    woven = strip % 16 == 0 and count <= 4
     factor = 1.0 / math.sqrt(batches * dps * rows * seqs)
 
     def passed(keep, got, after=()):
@@ -348,7 +348,7 @@
             total = keep + got.astype(F32)
             keep, got, bit = total[0::2], along(bit)(total[1::2].astype(BF16)), 2 * bit
         if bit < seqs:
-            return keep, got, along(bit)(passed(keep, got))
+            return keep, got, along(bit + 2 if woven else bit)(passed(keep, got))
         return keep, got, jnp.zeros_like(got)
 
     g1, q0, q0_mixed, send_a, send_b = kernel_call(
@@ -356,6 +356,7 @@
         [e1, cotangent, got_a, got_b, kernels, h1],
         [shape(own, F32), shape(own), shape(own)] + [shape((batches, near, channels))] * 2,
         conv_flops // 10,
+        [s1_other, ends_other],
     )
     q0_a, q0_b = to_a(send_a), to_b(send_b)
     keep1, send1 = kernel_call(
@@ -369,11 +370,11 @@
 
     q0_other = swap(q0_mixed)
     keep0, send0 = kernel_call(
-        grad_near_body, [s0_keep, s0_other, q0_mixed, q0_other], blocks, conv_flops, [s1_a, s1_b]
+        grad_near_body, [s0_keep, s0_other, q0_mixed, q0_other], blocks, conv_flops
     )
     half0 = cross_one(send0)
     parts1 = reduced(keep1, half1, [send0])
-    parts0 = reduced(keep0, half0, [q0_a, q0_b])
+    parts0 = reduced(keep0, half0, [q0_a, q0_b, s1_a, s1_b])
 
     (out,) = kernel_call(
         partial(last_body, far), [s1, s1_a, s1_b, kernels, h1], [shape(own)], conv_flops

time: 92.1 us -> 94.8 us (1.029)
  the two profiles are of different devices: /device:TPU:0 before, /device:TPU:1 now
where the time goes in v4:
time: 94.8 us; the launch traced here: 94.5 us
  waiting for transfers between devices  36.5 us (39%)
  Pallas kernels  26.4 us (28%)
  starting transfers between devices  24.5 us (26%)
  local copies, waits for them, and re-layouts  6.26 us (7%)
    pallas_call x16, Pallas kernels, kernel_call(): pl.pallas_call(body, out_shape=tuple(outs), in_specs=[VMEM] * len(args) +...  26.4 us
    ppermute x2, waiting for transfers between devices, per_device(): s1_a, s1_b = (to_a(s1_a), to_b(s1_b))  21.4 us
    ppermute x1, waiting for transfers between devices, per_device(): half1 = cross_one(send1)  6.78 us
    ppermute x2, waiting for transfers between devices, reduced(): more = cross_two(passed(keep, got, after))  6.58 us
    unnamed x12, local copies, waits for them, and re-layouts  6.26 us
    ppermute x2, starting transfers between devices, per_device(): q0_a, q0_b = (to_a(send_a), to_b(send_b))  4.43 us
    ppermute x2, starting transfers between devices, reduced(): got, bit = (along(2)(send), 4)  3.84 us
    ppermute x1, starting transfers between devices, per_device(): half1 = cross_one(send1)  3.59 us
  transfers between devices with their start and end apart: 19, of which 5 were waited for; matrix products, arithmetic and copies ran while one was open for 0% of the time, Pallas kernels for 23%

profile of v4, /device:TPU:1, one launch (start us, length us, event | category | flops | bytes accessed | tf_op | source)
XLA Modules:
  0.0 94.5 jit_solution(14608563769435568322)
XLA Ops:
  0.8 1.2 %copy-done.2 = bf16[6,96,768]{2,1,0:T(8,128)(2,1)S(1)} copy-done((bf16[6,96,768]{2,1,0:T(8,128)(2,1)S(1)}, bf16[6,96,768]{2,1,0:T(8,128)(2,1)}, u32[]{:S(2)}) %copy-start.2) | copy-done | bytes 884760
  1.9 1.2 %copy-done.4 = bf16[6,96,768]{2,1,0:T(8,128)(2,1)S(1)} copy-done((bf16[6,96,768]{2,1,0:T(8,128)(2,1)S(1)}, bf16[6,96,768]{2,1,0:T(8,128)(2,1)}, u32[]{:S(2)}) %copy-start.4) | copy-done | bytes 884760
  3.2 2.8 %collective-permute-start = (bf16[6,24,768]{2,1,0:T(8,128)(2,1)S(1)}, bf16[6,24,768]{2,1,0:T(8,128)(2,1)S(1)}, u32[]{:S(2)}, u32[]{:S(2)}) collective-permute-start(bf16[6,24,768]{2,1,0:T(8,128)(2,1)S(1)} %get-tuple-element.31), channel_id=1, source_target_pairs={{0,4},{1,5},{2,6},{3,7},{4,0},{5,1},{6,2},{7,3},{8,12},{9,13},{10,... | collective-permute-start | bytes 663560 | tf_op jit(solution)/shard_map/ppermute | solution.py:289
  5.9 0.7 collective-permute-start.1
  6.6 3.0 %copy-done = bf16[2,3,768,768]{3,2,1,0:T(8,128)(2,1)S(1)} copy-done((bf16[2,3,768,768]{3,2,1,0:T(8,128)(2,1)S(1)}, bf16[2,3,768,768]{3,2,1,0:T(8,128)(2,1)}, u32[]{:S(2)}) %copy-start) | copy-done | bytes 7077912
  9.6 2.3 %shard_map.60.refs_6_.refs_0_ = f32[6,96,768]{2,1,0:T(8,128)S(1)} custom-call(bf16[6,96,768]{2,1,0:T(8,128)(2,1)S(1)} %copy-done.5, bf16[2,3,768,768]{3,2,1,0:T(8,128)(2,1)S(1)} %copy-done), custom_call_target="tpu_custom_call" | custom-call | flops 2038431744 | bytes 9732096 | tf_op jit(solution)/shard_map/pallas_call | solution.py:26
  11.9 0.7 copy-done.1
  12.8 2.7 %shard_map.58 = (bf16[6,96,768]{2,1,0:T(8,128)(2,1)S(1)}, f32[6,96,768]{2,1,0:T(8,128)S(1)}) custom-call(bf16[6,96,768]{2,1,0:T(8,128)(2,1)S(1)} %copy-done.3, bf16[2,3,768,768]{3,2,1,0:T(8,128)(2,1)S(1)} %copy-done.1), custom_call_target="tpu_custom_call" | custom-call | flops 2038431744 | bytes 10616832 | tf_op jit(solution)/shard_map/pallas_call | solution.py:26
  15.5 1.8 %shard_map.61 = (bf16[6,96,768]{2,1,0:T(8,128)(2,1)S(1)}, bf16[6,96,768]{2,1,0:T(8,128)(2,1)S(1)}, bf16[6,96,384]{2,1,0:T(8,128)(2,1)S(1)}, bf16[6,96,384]{2,1,0...) custom-call(f32[6,96,768]{2,1,0:T(8,128)S(1)} %get-tuple-element.29., ...), custom_call_target="tpu_custom_call" | custom-call | flops 203843168 | bytes 15335424 | tf_op jit(solution)/shard_map/pallas_call | solution.py:26
  17.4 0.8 collective-permute-start.5
  18.3 1.8 %collective-permute-done.6.refs_7_.refs_5_ = bf16[6,32,768]{2,1,0:T(8,128)(2,1)S(1)} collective-permute-done((bf16[6,32,768]{2,1,0:T(8,128)(2,1)S(1)}, bf16[6,32,768]{2,1,0:T(8,128)(2,1)S(1)}, u32[]{:S(2)}, u32[]{:S(2)}) %collective-permute-start.6) | collective-permute-done | bytes 294944 | tf_op jit(solution)/shard_map/ppermute | solution.py:314
  20.0 2.2 %shard_map.63 = (f32[6,96,768]{2,1,0:T(8,128)S(1)}, bf16[6,96,768]{2,1,0:T(8,128)(2,1)S(1)}, bf16[6,96,768]{2,1,0:T(8,128)(2,1)S(1)}, bf16[6,8,768]{2,1,0:T(8,128)(2,1)S(1)}, bf16[6,8,768]{2,1,0:T(8,128)(2,1)S(1)}) custom-call(f32[6,96,768]{2,1,0:T(8,128)S(1)} %shard_map.60.refs_6_.refs_0_, bf16[6,96,768]{2,1,0:T(8,128)(2,1)S(1)} %copy-done.5, ...), custom_call_target="tpu_custom_call" | custom-call | flops 203843168 | bytes 14745600 | tf_op jit(solution)/shard_map/pallas_call | solution.py:26
  22.8 3.0 %shard_map.69 = (f32[2,3,192,384]{3,2,1,0:T(8,128)S(1)}, bf16[2,3,192,384]{3,2,1,0:T(8,128)(2,1)S(1)}) custom-call(bf16[6,96,384]{2,1,0:T(8,128)(2,1)S(1)} %get-tuple-element.50.refs_0_, bf16[6,96,384]{2,1,0:T(8,128)(2,1)S(1)} %collective-permute-done.5.refs_6_.refs_1_, bf16[6,96,768]{2,1,0:T(8,128)(2,1)S(1)} %copy-done.5, ...), custom_call_target="tpu_custom_call" | custom-call | flops 2038431744 | bytes 5898240 | tf_op jit(solution)/shard_map/pallas_call | solution.py:26
  25.9 3.6 %collective-permute-start.15 = (bf16[2,3,192,384]{3,2,1,0:T(8,128)(2,1)S(1)}, bf16[2,3,192,384]{3,2,1,0:T(8,128)(2,1)S(1)}, u32[]{:S(2)}, u32[]{:S(2)}) collective-permute-start(bf16[2,3,192,384]{3,2,1,0:T(8,128)(2,1)S(1)} %get-tuple-element.52), channel_id=1, source_target_pairs={{0,2},{1,5},{2,0},{3,7},{4,6},{5,1},{6,4},{7,3},{8,10},{9,13},{10,... | collective-permute-start | bytes 2654216 | tf_op jit(solution)/shard_map/ppermute | solution.py:369
  29.5 2.7 %shard_map.65 = (f32[2,3,192,384]{3,2,1,0:T(8,128)S(1)}, bf16[2,3,192,384]{3,2,1,0:T(8,128)(2,1)S(1)}) custom-call(bf16[6,112,384]{2,1,0:T(8,128)(2,1)S(1)} %get-tuple-element.43.s_ref, bf16[6,112,384]{2,1,0:T(8,128)(2,1)S(1)} %collective-permute-done.9.s2_ref, bf16[6,96,768]{2,1,0:T(8,128)(2,1)S(1)} %get-tuple-element.45.q_ref, ...), custom_call_target="tpu_custom_call" | custom-call | flops 2038431744 | bytes 5455872 | tf_op jit(solution)/shard_map/pallas_call | solution.py:26
  32.3 1.4 %collective-permute-start.3 = (bf16[6,16,768]{2,1,0:T(8,128)(2,1)S(1)}, bf16[6,16,768]{2,1,0:T(8,128)(2,1)S(1)}, u32[]{:S(2)}, u32[]{:S(2)}) collective-permute-start(bf16[6,16,768]{2,1,0:T(8,128)(2,1)S(1)} %get-tuple-element.34), channel_id=1, source_target_pairs={{0,4},{1,5},{2,6},{3,7},{4,0},{5,1},{6,2},{7,3},{8,12},{9,13},{10,... | collective-permute-start | bytes 442376 | tf_op jit(solution)/shard_map/ppermute | solution.py:315
  34.4 3.8 %collective-permute-start.7 = (bf16[6,8,768]{2,1,0:T(8,128)(2,1)S(1)}, bf16[6,8,768]{2,1,0:T(8,128)(2,1)S(1)}, u32[]{:S(2)}, u32[]{:S(2)}) collective-permute-start(bf16[6,8,768]{2,1,0:T(8,128)(2,1)S(1)} %get-tuple-element.40), channel_id=1, source_target_pairs={{0,4},{1,5},{2,6},{3,7},{4,0},{5,1},{6,2},{7,3},{8,12},{9,13},{10,... | collective-permute-start | bytes 221192 | tf_op jit(solution)/shard_map/ppermute | solution.py:361
  38.2 6.8 %collective-permute-done.15.refs_1_.got_ref = bf16[2,3,192,384]{3,2,1,0:T(8,128)(2,1)S(1)} collective-permute-done((bf16[2,3,192,384]{3,2,1,0:T(8,128)(2,1)S(1)}, bf16[2,3,192,384]{3,2,1,0:T(8,128)(2,1)S(1)}, u32[]{:S(2)}, u32[]{:S(2)}) %collective-permute-start.15) | collective-permute-done | bytes 884768 | tf_op jit(solution)/shard_map/ppermute | solution.py:369
  45.7 21.4 %collective-permute-done.3.a_ref.refs_4_ = bf16[6,16,768]{2,1,0:T(8,128)(2,1)S(1)} collective-permute-done((bf16[6,16,768]{2,1,0:T(8,128)(2,1)S(1)}, bf16[6,16,768]{2,1,0:T(8,128)(2,1)S(1)}, u32[]{:S(2)}, u32[]{:S(2)}) %collective-permute-start.3) | collective-permute-done | bytes 147488 | tf_op jit(solution)/shard_map/ppermute | solution.py:315
  67.1 1.2 %collective-permute-start.16 = (bf16[1,3,192,384]{3,2,1,0:T(8,128)(2,1)S(1)}, bf16[1,3,192,384]{3,2,1,0:T(8,128)(2,1)S(1)}, u32[]{:S(2)}, u32[]{:S(2)}) collective-permute-start(bf16[1,3,192,384]{3,2,1,0:T(8,128)(2,1)S(1)} %shard_map.70), channel_id=1, source_target_pairs={{0,4},{1,3},{2,6},{3,1},{4,0},{5,7},{6,2},{7,5},{8,12},{9,11},{10,... | collective-permute-start | bytes 1327112 | tf_op jit(solution)/shard_map/ppermute | solution.py:329
  68.4 0.8 collective-permute-start.12
  69.2 5.3 %collective-permute-done.16.more_ref = bf16[1,3,192,384]{3,2,1,0:T(8,128)(2,1)S(1)} collective-permute-done((bf16[1,3,192,384]{3,2,1,0:T(8,128)(2,1)S(1)}, bf16[1,3,192,384]{3,2,1,0:T(8,128)(2,1)S(1)}, u32[]{:S(2)}, u32[]{:S(2)}) %collective-permute-start.16) | collective-permute-done | bytes 442400 | tf_op jit(solution)/shard_map/ppermute | solution.py:329
  74.5 1.4 %shard_map.71 = (f32[2,144,384]{2,1,0:T(8,128)S(1)}, bf16[2,144,384]{2,1,0:T(8,128)(2,1)S(1)}, f32[4,144,384]{2,1,0:T(8,128)}) custom-call(f32[2,3,192,384]{3,2,1,0:T(8,128)S(1)} %get-tuple-element.51.refs_0_.keep_ref, bf16[2,3,192,384]{3,2,1,0:T(8,128)(2,1)S(1)} %collective-permute-done.15.refs_1_.got_ref, ...), custom_call_target="tpu_custom_call" | custom-call | bytes 4644864 | tf_op jit(solution)/shard_map/pallas_call | solution.py:26
  75.9 1.8 %collective-permute-start.17 = (bf16[2,144,384]{2,1,0:T(8,128)(2,1)S(1)}, bf16[2,144,384]{2,1,0:T(8,128)(2,1)S(1)}, u32[]{:S(2)}, u32[]{:S(2)}) collective-permute-start(bf16[2,144,384]{2,1,0:T(8,128)(2,1)S(1)} %get-tuple-element.54), channel_id=1, source_target_pairs={{0,8},{1,9},{2,10},{3,11},{4,12},{5,13},{6,14},{7,15},{8,0},{9,1},... | collective-permute-start | bytes 663560 | tf_op jit(solution)/shard_map/ppermute | solution.py:346
  77.7 1.3 %collective-permute-done.12.more_ref = bf16[1,3,192,384]{3,2,1,0:T(8,128)(2,1)S(1)} collective-permute-done((bf16[1,3,192,384]{3,2,1,0:T(8,128)(2,1)S(1)}, bf16[1,3,192,384]{3,2,1,0:T(8,128)(2,1)S(1)}, u32[]{:S(2)}, u32[]{:S(2)}) %collective-permute-start.12) | collective-permute-done | bytes 442400 | tf_op jit(solution)/shard_map/ppermute | solution.py:329
  79.0 1.4 %shard_map.67 = (f32[2,144,384]{2,1,0:T(8,128)S(1)}, bf16[2,144,384]{2,1,0:T(8,128)(2,1)S(1)}, f32[4,144,384]{2,1,0:T(8,128)}) custom-call(f32[2,3,192,384]{3,2,1,0:T(8,128)S(1)} %get-tuple-element.46.refs_0_.keep_ref, bf16[2,3,192,384]{3,2,1,0:T(8,128)(2,1)S(1)} %collective-permute-done.11.refs_1_.got_ref, ...), custom_call_target="tpu_custom_call" | custom-call | bytes 4644864 | tf_op jit(solution)/shard_map/pallas_call | solution.py:26
  80.3 2.1 %collective-permute-start.13 = (bf16[2,144,384]{2,1,0:T(8,128)(2,1)S(1)}, bf16[2,144,384]{2,1,0:T(8,128)(2,1)S(1)}, u32[]{:S(2)}, u32[]{:S(2)}) collective-permute-start(bf16[2,144,384]{2,1,0:T(8,128)(2,1)S(1)} %get-tuple-element.49), channel_id=1, source_target_pairs={{0,8},{1,9},{2,10},{3,11},{4,12},{5,13},{6,14},{7,15},{8,0},{9,1},... | collective-permute-start | bytes 663560 | tf_op jit(solution)/shard_map/ppermute | solution.py:346
  82.4 3.1 %shard_map.62 = bf16[6,96,768]{2,1,0:T(8,128)(2,1)} custom-call(bf16[6,96,768]{2,1,0:T(8,128)(2,1)S(1)} %get-tuple-element.33.s_ref, bf16[6,16,768]{2,1,0:T(8,128)(2,1)S(1)} %collective-permute-done.3.a_ref.refs_4_, bf16[6,16,768]{2,1,0:T(8,128)(2,1)S(1)} %collective-permute-done.4.b_ref.refs_5_, bf16[2,3,768,768]{3,2,1,0:T(8,128)(2,1)S(1)} %copy-done.1, ...), custom_call_target="tpu_custom_call" | custom-call | flops 2038431744 | bytes 10027008 | tf_op jit(solution)/shard_map/pallas_call | solution.py:26
  85.6 2.3 %collective-permute-start.18 = (bf16[1,144,384]{2,1,0:T(8,128)(2,1)S(1)}, bf16[1,144,384]{2,1,0:T(8,128)(2,1)S(1)}, u32[]{:S(2)}, u32[]{:S(2)}) collective-permute-start(bf16[1,144,384]{2,1,0:T(8,128)(2,1)S(1)} %shard_map.72), channel_id=1, source_target_pairs={{0,24},{1,25},{2,26},{3,27},{4,28},{5,29},{6,30},{7,31},{8,16},{9,... | collective-permute-start | bytes 331784 | tf_op jit(solution)/shard_map/ppermute | solution.py:351
  87.9 1.1 %collective-permute-start.14 = (bf16[1,144,384]{2,1,0:T(8,128)(2,1)S(1)}, bf16[1,144,384]{2,1,0:T(8,128)(2,1)S(1)}, u32[]{:S(2)}, u32[]{:S(2)}) collective-permute-start(bf16[1,144,384]{2,1,0:T(8,128)(2,1)S(1)} %shard_map.68), channel_id=1, source_target_pairs={{0,24},{1,25},{2,26},{3,27},{4,28},{5,29},{6,30},{7,31},{8,16},{9,... | collective-permute-start | bytes 331784 | tf_op jit(solution)/shard_map/ppermute | solution.py:351
  89.0 4.4 %shard_map.64 = bf16[6,96,768]{2,1,0:T(8,128)(2,1)} custom-call(bf16[6,96,768]{2,1,0:T(8,128)(2,1)S(1)} %get-tuple-element.39.q_ref, bf16[6,8,768]{2,1,0:T(8,128)(2,1)S(1)} %collective-permute-done.7.a_ref.refs_2_, bf16[6,8,768]{2,1,0:T(8,128)(2,1)S(1)} %collective-permute-done.8.b_ref.refs_3_, bf16[2,3,768,768]{3,2,1,0:T(8,128)(2,1)S(1)} %copy-done.1, ...), custom_call_target="tpu_custom_call" | custom-call | flops 2038431744 | bytes 11649024 | tf_op jit(solution)/shard_map/pallas_call | solution.py:26
  93.4 1.1 %shard_map.73 = f32[2,3,192,96]{3,2,1,0:T(8,128)} custom-call(f32[2,144,384]{2,1,0:T(8,128)S(1)} %get-tuple-element.48.keep_ref.refs_0_, bf16[2,144,384]{2,1,0:T(8,128)(2,1)S(1)} %collective-permute-done.13.got_ref.refs_1_, bf16[1,144,384]{2,1,0:T(8,128)(2,1)S(1)} %collective-permute-done.14.refs_2_, f32[2,144,384]{2,1,0:T(8,128)S(1)} %get-tuple-element.53.keep_ref.refs_3_, ...), custom_call_target="tpu_custom_call" | custom-call | bytes 1990656 | tf_op jit(solution)/shard_map/pallas_call | solution.py:26
  (34 shorter events, 2.7 us)
Async XLA Ops:
  0.6 14.9 %collective-permute-start.2 = (bf16[6,96,768]{2,1,0:T(8,128)(2,1)}, bf16[6,96,768]{2,1,0:T(8,128)(2,1)S(1)}, u32[]{:S(2)}, u32[]{:S(2)}) collective-permute-start(bf16[6,96,768]{2,1,0:T(8,128)(2,1)} %refs_2_.1), channel_id=1, source_target_pairs={{0,1},{1,0},{2,3},{3,2},{4,5},{5,4},{6,7},{7,6},{8,9},{9,8},{10,11... | collective-permute-start | bytes 2654216 | tf_op jit(solution)/shard_map/ppermute | solution.py:290
  0.8 1.2 %copy-start.2 = (bf16[6,96,768]{2,1,0:T(8,128)(2,1)S(1)}, bf16[6,96,768]{2,1,0:T(8,128)(2,1)}, u32[]{:S(2)}) copy-start(bf16[6,96,768]{2,1,0:T(8,128)(2,1)} %h_ref.5) | copy-start | bytes 2654212
  1.9 1.2 %copy-start.4 = (bf16[6,96,768]{2,1,0:T(8,128)(2,1)S(1)}, bf16[6,96,768]{2,1,0:T(8,128)(2,1)}, u32[]{:S(2)}) copy-start(bf16[6,96,768]{2,1,0:T(8,128)(2,1)} %refs_2_.1) | copy-start | bytes 2654212
  3.1 3.5 %copy-start.5 = (bf16[6,96,768]{2,1,0:T(8,128)(2,1)S(1)}, bf16[6,96,768]{2,1,0:T(8,128)(2,1)}, u32[]{:S(2)}) copy-start(bf16[6,96,768]{2,1,0:T(8,128)(2,1)} %refs_2_.1) | copy-start | bytes 2654212
  3.2 12.3 %collective-permute-start = (bf16[6,24,768]{2,1,0:T(8,128)(2,1)S(1)}, bf16[6,24,768]{2,1,0:T(8,128)(2,1)S(1)}, u32[]{:S(2)}, u32[]{:S(2)}) collective-permute-start(bf16[6,24,768]{2,1,0:T(8,128)(2,1)S(1)} %get-tuple-element.31), channel_id=1, source_target_pairs={{0,4},{1,5},{2,6},{3,7},{4,0},{5,1},{6,2},{7,3},{8,12},{9,13},{10,... | collective-permute-start | bytes 663560 | tf_op jit(solution)/shard_map/ppermute | solution.py:289
  5.9 9.6 %collective-permute-start.1 = (bf16[6,24,768]{2,1,0:T(8,128)(2,1)S(1)}, bf16[6,24,768]{2,1,0:T(8,128)(2,1)S(1)}, u32[]{:S(2)}, u32[]{:S(2)}) collective-permute-start(bf16[6,24,768]{2,1,0:T(8,128)(2,1)S(1)} %get-tuple-element.32), channel_id=1, source_target_pairs={{4,8},{5,9},{6,10},{7,11},{8,4},{9,5},{10,6},{11,7},{12,16},{13,17... | collective-permute-start | bytes 663560 | tf_op jit(solution)/shard_map/ppermute | solution.py:289
  6.6 3.0 %copy-start = (bf16[2,3,768,768]{3,2,1,0:T(8,128)(2,1)S(1)}, bf16[2,3,768,768]{3,2,1,0:T(8,128)(2,1)}, u32[]{:S(2)}) copy-start(bf16[2,3,768,768]{3,2,1,0:T(8,128)(2,1)} %w_ref.7) | copy-start | bytes 21233668
  9.6 3.0 %copy-start.1 = (bf16[2,3,768,768]{3,2,1,0:T(8,128)(2,1)S(1)}, bf16[2,3,768,768]{3,2,1,0:T(8,128)(2,1)}, u32[]{:S(2)}) copy-start(bf16[2,3,768,768]{3,2,1,0:T(8,128)(2,1)} %w_ref.7) | copy-start | bytes 21233668
  9.6 3.2 %copy-start.3 = (bf16[6,96,768]{2,1,0:T(8,128)(2,1)S(1)}, bf16[6,96,768]{2,1,0:T(8,128)(2,1)}, u32[]{:S(2)}) copy-start(bf16[6,96,768]{2,1,0:T(8,128)(2,1)} %h_ref.5) | copy-start | bytes 2654212
  17.4 2.7 %collective-permute-start.5 = (bf16[6,96,384]{2,1,0:T(8,128)(2,1)S(1)}, bf16[6,96,384]{2,1,0:T(8,128)(2,1)S(1)}, u32[]{:S(2)}, u32[]{:S(2)}) collective-permute-start(bf16[6,96,384]{2,1,0:T(8,128)(2,1)S(1)} %get-tuple-element.37), channel_id=1, source_target_pairs={{0,1},{1,0},{2,3},{3,2},{4,5},{5,4},{6,7},{7,6},{8,9},{9,8},{10,11... | collective-permute-start | bytes 1327112 | tf_op jit(solution)/shard_map/ppermute | solution.py:314
  18.2 1.8 %collective-permute-start.6 = (bf16[6,32,768]{2,1,0:T(8,128)(2,1)S(1)}, bf16[6,32,768]{2,1,0:T(8,128)(2,1)S(1)}, u32[]{:S(2)}, u32[]{:S(2)}) collective-permute-start(bf16[6,32,768]{2,1,0:T(8,128)(2,1)S(1)} %get-tuple-element.38.refs_4_), channel_id=1, source_target_pairs={{0,1},{1,0},{2,3},{3,2},{4,5},{5,4},{6,7},{7,6},{8,9},{9,8},{10,11... | collective-permute-start | bytes 884744 | tf_op jit(solution)/shard_map/ppermute | solution.py:314
  22.2 7.2 %collective-permute-start.10 = (bf16[6,96,768]{2,1,0:T(8,128)(2,1)S(1)}, bf16[6,96,768]{2,1,0:T(8,128)(2,1)S(1)}, u32[]{:S(2)}, u32[]{:S(2)}) collective-permute-start(bf16[6,96,768]{2,1,0:T(8,128)(2,1)S(1)} %get-tuple-element.45.q_ref), channel_id=1, source_target_pairs={{0,1},{1,0},{2,3},{3,2},{4,5},{5,4},{6,7},{7,6},{8,9},{9,8},{10,11... | collective-permute-start | bytes 2654216 | tf_op jit(solution)/shard_map/ppermute | solution.py:371
  22.7 6.8 %collective-permute-start.9 = (bf16[6,112,384]{2,1,0:T(8,128)(2,1)S(1)}, bf16[6,112,384]{2,1,0:T(8,128)(2,1)S(1)}, u32[]{:S(2)}, u32[]{:S(2)}) collective-permute-start(bf16[6,112,384]{2,1,0:T(8,128)(2,1)S(1)} %get-tuple-element.44), channel_id=1, source_target_pairs={{0,1},{1,0},{2,3},{3,2},{4,5},{5,4},{6,7},{7,6},{8,9},{9,8},{10,11... | collective-permute-start | bytes 1548296 | tf_op jit(solution)/shard_map/ppermute | solution.py:314
  25.9 19.1 %collective-permute-start.15 = (bf16[2,3,192,384]{3,2,1,0:T(8,128)(2,1)S(1)}, bf16[2,3,192,384]{3,2,1,0:T(8,128)(2,1)S(1)}, u32[]{:S(2)}, u32[]{:S(2)}) collective-permute-start(bf16[2,3,192,384]{3,2,1,0:T(8,128)(2,1)S(1)} %get-tuple-element.52), channel_id=1, source_target_pairs={{0,2},{1,5},{2,0},{3,7},{4,6},{5,1},{6,4},{7,3},{8,10},{9,13},{10,... | collective-permute-start | bytes 2654216 | tf_op jit(solution)/shard_map/ppermute | solution.py:369
  32.2 36.1 %collective-permute-start.11 = (bf16[2,3,192,384]{3,2,1,0:T(8,128)(2,1)S(1)}, bf16[2,3,192,384]{3,2,1,0:T(8,128)(2,1)S(1)}, u32[]{:S(2)}, u32[]{:S(2)}) collective-permute-start(bf16[2,3,192,384]{3,2,1,0:T(8,128)(2,1)S(1)} %get-tuple-element.47.refs_2_), channel_id=1, source_target_pairs={{0,2},{1,5},{2,0},{3,7},{4,6},{5,1},{6,4},{7,3},{8,10},{9,13},{10,... | collective-permute-start | bytes 2654216 | tf_op jit(solution)/shard_map/ppermute | solution.py:375
  32.3 34.8 %collective-permute-start.3 = (bf16[6,16,768]{2,1,0:T(8,128)(2,1)S(1)}, bf16[6,16,768]{2,1,0:T(8,128)(2,1)S(1)}, u32[]{:S(2)}, u32[]{:S(2)}) collective-permute-start(bf16[6,16,768]{2,1,0:T(8,128)(2,1)S(1)} %get-tuple-element.34), channel_id=1, source_target_pairs={{0,4},{1,5},{2,6},{3,7},{4,0},{5,1},{6,2},{7,3},{8,12},{9,13},{10,... | collective-permute-start | bytes 442376 | tf_op jit(solution)/shard_map/ppermute | solution.py:315
  33.7 34.6 %collective-permute-start.4 = (bf16[6,16,768]{2,1,0:T(8,128)(2,1)S(1)}, bf16[6,16,768]{2,1,0:T(8,128)(2,1)S(1)}, u32[]{:S(2)}, u32[]{:S(2)}) collective-permute-start(bf16[6,16,768]{2,1,0:T(8,128)(2,1)S(1)} %get-tuple-element.35), channel_id=1, source_target_pairs={{4,8},{5,9},{6,10},{7,11},{8,4},{9,5},{10,6},{11,7},{12,16},{13,17... | collective-permute-start | bytes 442376 | tf_op jit(solution)/shard_map/ppermute | solution.py:315
  34.4 33.9 %collective-permute-start.7 = (bf16[6,8,768]{2,1,0:T(8,128)(2,1)S(1)}, bf16[6,8,768]{2,1,0:T(8,128)(2,1)S(1)}, u32[]{:S(2)}, u32[]{:S(2)}) collective-permute-start(bf16[6,8,768]{2,1,0:T(8,128)(2,1)S(1)} %get-tuple-element.40), channel_id=1, source_target_pairs={{0,4},{1,5},{2,6},{3,7},{4,0},{5,1},{6,2},{7,3},{8,12},{9,13},{10,... | collective-permute-start | bytes 221192 | tf_op jit(solution)/shard_map/ppermute | solution.py:361
  45.0 23.4 %collective-permute-start.8 = (bf16[6,8,768]{2,1,0:T(8,128)(2,1)S(1)}, bf16[6,8,768]{2,1,0:T(8,128)(2,1)S(1)}, u32[]{:S(2)}, u32[]{:S(2)}) collective-permute-start(bf16[6,8,768]{2,1,0:T(8,128)(2,1)S(1)} %get-tuple-element.41), channel_id=1, source_target_pairs={{4,8},{5,9},{6,10},{7,11},{8,4},{9,5},{10,6},{11,7},{12,16},{13,17... | collective-permute-start | bytes 221192 | tf_op jit(solution)/shard_map/ppermute | solution.py:361
  67.1 7.4 %collective-permute-start.16 = (bf16[1,3,192,384]{3,2,1,0:T(8,128)(2,1)S(1)}, bf16[1,3,192,384]{3,2,1,0:T(8,128)(2,1)S(1)}, u32[]{:S(2)}, u32[]{:S(2)}) collective-permute-start(bf16[1,3,192,384]{3,2,1,0:T(8,128)(2,1)S(1)} %shard_map.70), channel_id=1, source_target_pairs={{0,4},{1,3},{2,6},{3,1},{4,0},{5,7},{6,2},{7,5},{8,12},{9,11},{10,... | collective-permute-start | bytes 1327112 | tf_op jit(solution)/shard_map/ppermute | solution.py:329
  68.4 10.5 %collective-permute-start.12 = (bf16[1,3,192,384]{3,2,1,0:T(8,128)(2,1)S(1)}, bf16[1,3,192,384]{3,2,1,0:T(8,128)(2,1)S(1)}, u32[]{:S(2)}, u32[]{:S(2)}) collective-permute-start(bf16[1,3,192,384]{3,2,1,0:T(8,128)(2,1)S(1)} %shard_map.66), channel_id=1, source_target_pairs={{0,4},{1,3},{2,6},{3,1},{4,0},{5,7},{6,2},{7,5},{8,12},{9,11},{10,... | collective-permute-start | bytes 1327112 | tf_op jit(solution)/shard_map/ppermute | solution.py:329
  75.9 9.6 %collective-permute-start.17 = (bf16[2,144,384]{2,1,0:T(8,128)(2,1)S(1)}, bf16[2,144,384]{2,1,0:T(8,128)(2,1)S(1)}, u32[]{:S(2)}, u32[]{:S(2)}) collective-permute-start(bf16[2,144,384]{2,1,0:T(8,128)(2,1)S(1)} %get-tuple-element.54), channel_id=1, source_target_pairs={{0,8},{1,9},{2,10},{3,11},{4,12},{5,13},{6,14},{7,15},{8,0},{9,1},... | collective-permute-start | bytes 663560 | tf_op jit(solution)/shard_map/ppermute | solution.py:346
  80.3 7.5 %collective-permute-start.13 = (bf16[2,144,384]{2,1,0:T(8,128)(2,1)S(1)}, bf16[2,144,384]{2,1,0:T(8,128)(2,1)S(1)}, u32[]{:S(2)}, u32[]{:S(2)}) collective-permute-start(bf16[2,144,384]{2,1,0:T(8,128)(2,1)S(1)} %get-tuple-element.49), channel_id=1, source_target_pairs={{0,8},{1,9},{2,10},{3,11},{4,12},{5,13},{6,14},{7,15},{8,0},{9,1},... | collective-permute-start | bytes 663560 | tf_op jit(solution)/shard_map/ppermute | solution.py:346
  85.6 7.8 %collective-permute-start.18 = (bf16[1,144,384]{2,1,0:T(8,128)(2,1)S(1)}, bf16[1,144,384]{2,1,0:T(8,128)(2,1)S(1)}, u32[]{:S(2)}, u32[]{:S(2)}) collective-permute-start(bf16[1,144,384]{2,1,0:T(8,128)(2,1)S(1)} %shard_map.72), channel_id=1, source_target_pairs={{0,24},{1,25},{2,26},{3,27},{4,28},{5,29},{6,30},{7,31},{8,16},{9,... | collective-permute-start | bytes 331784 | tf_op jit(solution)/shard_map/ppermute | solution.py:351
  87.9 5.5 %collective-permute-start.14 = (bf16[1,144,384]{2,1,0:T(8,128)(2,1)S(1)}, bf16[1,144,384]{2,1,0:T(8,128)(2,1)S(1)}, u32[]{:S(2)}, u32[]{:S(2)}) collective-permute-start(bf16[1,144,384]{2,1,0:T(8,128)(2,1)S(1)} %shard_map.68), channel_id=1, source_target_pairs={{0,24},{1,25},{2,26},{3,27},{4,28},{5,29},{6,30},{7,31},{8,16},{9,... | collective-permute-start | bytes 331784 | tf_op jit(solution)/shard_map/ppermute | solution.py:351

commit v5 on v4

--- a/solution.py
+++ b/solution.py
@@ -374,7 +374,7 @@
     )
     half0 = cross_one(send0)
     parts1 = reduced(keep1, half1, [send0])
-    parts0 = reduced(keep0, half0, [q0_a, q0_b, s1_a, s1_b])
+    parts0 = reduced(keep0, half0)
 
     (out,) = kernel_call(
         partial(last_body, far), [s1, s1_a, s1_b, kernels, h1], [shape(own)], conv_flops

time: 94.8 us -> 89.8 us (0.947)
  the two profiles are of different devices: /device:TPU:1 before, /device:TPU:0 now
where the time goes in v5:
time: 89.8 us; the launch traced here: 89.5 us
  starting transfers between devices  29.4 us (33%)
  waiting for transfers between devices  26.7 us (30%)
  Pallas kernels  26.4 us (29%)
  local copies, waits for them, and re-layouts  6.26 us (7%)
    pallas_call x16, Pallas kernels, kernel_call(): pl.pallas_call(body, out_shape=tuple(outs), in_specs=[VMEM] * len(args) +...  26.4 us
    ppermute x1, waiting for transfers between devices, per_device(): half0 = cross_one(send0)  10.3 us
    ppermute x1, waiting for transfers between devices, per_device(): half1 = cross_one(send1)  8.2 us
    ppermute x2, starting transfers between devices, reduced(): more = cross_two(passed(keep, got, after))  7.74 us
    ppermute x2, starting transfers between devices, reduced(): got, bit = (along(2)(send), 4)  7.22 us
    unnamed x12, local copies, waits for them, and re-layouts  6.26 us
    ppermute x2, starting transfers between devices, reduced(): return (keep, got, along(bit + 2 if woven else bit)(passed(keep, got)))  4.2 us
    ppermute x2, waiting for transfers between devices, reduced(): more = cross_two(passed(keep, got, after))  3.84 us
  transfers between devices with their start and end apart: 19, of which 6 were waited for; matrix products, arithmetic and copies ran while one was open for 0% of the time, Pallas kernels for 24%

profile of v5, /device:TPU:0, one launch (start us, length us, event | category | flops | bytes accessed | tf_op | source)
XLA Modules:
  0.0 89.5 jit_solution(6517359456177235437)
XLA Ops:
  1.1 1.2 %copy-done.2 = bf16[6,96,768]{2,1,0:T(8,128)(2,1)S(1)} copy-done((bf16[6,96,768]{2,1,0:T(8,128)(2,1)S(1)}, bf16[6,96,768]{2,1,0:T(8,128)(2,1)}, u32[]{:S(2)}) %copy-start.2) | copy-done | bytes 884760
  2.3 1.2 %copy-done.4 = bf16[6,96,768]{2,1,0:T(8,128)(2,1)S(1)} copy-done((bf16[6,96,768]{2,1,0:T(8,128)(2,1)S(1)}, bf16[6,96,768]{2,1,0:T(8,128)(2,1)}, u32[]{:S(2)}) %copy-start.4) | copy-done | bytes 884760
  3.6 2.6 %collective-permute-start = (bf16[6,24,768]{2,1,0:T(8,128)(2,1)S(1)}, bf16[6,24,768]{2,1,0:T(8,128)(2,1)S(1)}, u32[]{:S(2)}, u32[]{:S(2)}) collective-permute-start(bf16[6,24,768]{2,1,0:T(8,128)(2,1)S(1)} %get-tuple-element.31), channel_id=1, source_target_pairs={{0,4},{1,5},{2,6},{3,7},{4,0},{5,1},{6,2},{7,3},{8,12},{9,13},{10,... | collective-permute-start | bytes 663560 | tf_op jit(solution)/shard_map/ppermute | solution.py:289
  6.2 0.7 collective-permute-start.1
  6.8 3.0 %copy-done = bf16[2,3,768,768]{3,2,1,0:T(8,128)(2,1)S(1)} copy-done((bf16[2,3,768,768]{3,2,1,0:T(8,128)(2,1)S(1)}, bf16[2,3,768,768]{3,2,1,0:T(8,128)(2,1)}, u32[]{:S(2)}) %copy-start) | copy-done | bytes 7077912
  9.8 2.3 %shard_map.60.refs_6_.refs_0_ = f32[6,96,768]{2,1,0:T(8,128)S(1)} custom-call(bf16[6,96,768]{2,1,0:T(8,128)(2,1)S(1)} %copy-done.5, bf16[2,3,768,768]{3,2,1,0:T(8,128)(2,1)S(1)} %copy-done), custom_call_target="tpu_custom_call" | custom-call | flops 2038431744 | bytes 9732096 | tf_op jit(solution)/shard_map/pallas_call | solution.py:26
  12.1 0.7 copy-done.1
  13.0 2.7 %shard_map.58 = (bf16[6,96,768]{2,1,0:T(8,128)(2,1)S(1)}, f32[6,96,768]{2,1,0:T(8,128)S(1)}) custom-call(bf16[6,96,768]{2,1,0:T(8,128)(2,1)S(1)} %copy-done.3, bf16[2,3,768,768]{3,2,1,0:T(8,128)(2,1)S(1)} %copy-done.1), custom_call_target="tpu_custom_call" | custom-call | flops 2038431744 | bytes 10616832 | tf_op jit(solution)/shard_map/pallas_call | solution.py:26
  16.2 1.8 %shard_map.61 = (bf16[6,96,768]{2,1,0:T(8,128)(2,1)S(1)}, bf16[6,96,768]{2,1,0:T(8,128)(2,1)S(1)}, bf16[6,96,384]{2,1,0:T(8,128)(2,1)S(1)}, bf16[6,96,384]{2,1,0...) custom-call(f32[6,96,768]{2,1,0:T(8,128)S(1)} %get-tuple-element.29., ...), custom_call_target="tpu_custom_call" | custom-call | flops 203843168 | bytes 15335424 | tf_op jit(solution)/shard_map/pallas_call | solution.py:26
  18.6 1.7 %collective-permute-done.6.refs_7_.refs_5_ = bf16[6,32,768]{2,1,0:T(8,128)(2,1)S(1)} collective-permute-done((bf16[6,32,768]{2,1,0:T(8,128)(2,1)S(1)}, bf16[6,32,768]{2,1,0:T(8,128)(2,1)S(1)}, u32[]{:S(2)}, u32[]{:S(2)}) %collective-permute-start.6) | collective-permute-done | bytes 294944 | tf_op jit(solution)/shard_map/ppermute | solution.py:314
  20.3 2.2 %shard_map.63 = (f32[6,96,768]{2,1,0:T(8,128)S(1)}, bf16[6,96,768]{2,1,0:T(8,128)(2,1)S(1)}, bf16[6,96,768]{2,1,0:T(8,128)(2,1)S(1)}, bf16[6,8,768]{2,1,0:T(8,128)(2,1)S(1)}, bf16[6,8,768]{2,1,0:T(8,128)(2,1)S(1)}) custom-call(f32[6,96,768]{2,1,0:T(8,128)S(1)} %shard_map.60.refs_6_.refs_0_, bf16[6,96,768]{2,1,0:T(8,128)(2,1)S(1)} %copy-done.5, ...), custom_call_target="tpu_custom_call" | custom-call | flops 203843168 | bytes 14745600 | tf_op jit(solution)/shard_map/pallas_call | solution.py:26
  23.1 3.0 %shard_map.69 = (f32[2,3,192,384]{3,2,1,0:T(8,128)S(1)}, bf16[2,3,192,384]{3,2,1,0:T(8,128)(2,1)S(1)}) custom-call(bf16[6,96,384]{2,1,0:T(8,128)(2,1)S(1)} %get-tuple-element.50.refs_0_, bf16[6,96,384]{2,1,0:T(8,128)(2,1)S(1)} %collective-permute-done.5.refs_6_.refs_1_, bf16[6,96,768]{2,1,0:T(8,128)(2,1)S(1)} %copy-done.5, ...), custom_call_target="tpu_custom_call" | custom-call | flops 2038431744 | bytes 5898240 | tf_op jit(solution)/shard_map/pallas_call | solution.py:26
  26.2 1.6 %collective-permute-start.15 = (bf16[2,3,192,384]{3,2,1,0:T(8,128)(2,1)S(1)}, bf16[2,3,192,384]{3,2,1,0:T(8,128)(2,1)S(1)}, u32[]{:S(2)}, u32[]{:S(2)}) collective-permute-start(bf16[2,3,192,384]{3,2,1,0:T(8,128)(2,1)S(1)} %get-tuple-element.52), channel_id=1, source_target_pairs={{0,2},{1,5},{2,0},{3,7},{4,6},{5,1},{6,4},{7,3},{8,10},{9,13},{10,... | collective-permute-start | bytes 2654216 | tf_op jit(solution)/shard_map/ppermute | solution.py:369
  27.7 2.7 %shard_map.65 = (f32[2,3,192,384]{3,2,1,0:T(8,128)S(1)}, bf16[2,3,192,384]{3,2,1,0:T(8,128)(2,1)S(1)}) custom-call(bf16[6,112,384]{2,1,0:T(8,128)(2,1)S(1)} %get-tuple-element.43.s_ref, bf16[6,112,384]{2,1,0:T(8,128)(2,1)S(1)} %collective-permute-done.9.s2_ref, bf16[6,96,768]{2,1,0:T(8,128)(2,1)S(1)} %get-tuple-element.45.q_ref, ...), custom_call_target="tpu_custom_call" | custom-call | flops 2038431744 | bytes 5455872 | tf_op jit(solution)/shard_map/pallas_call | solution.py:26
  30.5 0.6 collective-permute-start.11
  31.1 8.2 %collective-permute-done.15.refs_1_.got_ref = bf16[2,3,192,384]{3,2,1,0:T(8,128)(2,1)S(1)} collective-permute-done((bf16[2,3,192,384]{3,2,1,0:T(8,128)(2,1)S(1)}, bf16[2,3,192,384]{3,2,1,0:T(8,128)(2,1)S(1)}, u32[]{:S(2)}, u32[]{:S(2)}) %collective-permute-start.15) | collective-permute-done | bytes 884768 | tf_op jit(solution)/shard_map/ppermute | solution.py:369
  39.4 3.9 %collective-permute-start.16 = (bf16[1,3,192,384]{3,2,1,0:T(8,128)(2,1)S(1)}, bf16[1,3,192,384]{3,2,1,0:T(8,128)(2,1)S(1)}, u32[]{:S(2)}, u32[]{:S(2)}) collective-permute-start(bf16[1,3,192,384]{3,2,1,0:T(8,128)(2,1)S(1)} %shard_map.70), channel_id=1, source_target_pairs={{0,4},{1,3},{2,6},{3,1},{4,0},{5,7},{6,2},{7,5},{8,12},{9,11},{10,... | collective-permute-start | bytes 1327112 | tf_op jit(solution)/shard_map/ppermute | solution.py:329
  43.2 10.3 %collective-permute-done.11.got_ref = bf16[2,3,192,384]{3,2,1,0:T(8,128)(2,1)S(1)} collective-permute-done((bf16[2,3,192,384]{3,2,1,0:T(8,128)(2,1)S(1)}, bf16[2,3,192,384]{3,2,1,0:T(8,128)(2,1)S(1)}, u32[]{:S(2)}, u32[]{:S(2)}) %collective-permute-start.11) | collective-permute-done | bytes 884768 | tf_op jit(solution)/shard_map/ppermute | solution.py:375
  53.6 3.9 %collective-permute-start.12 = (bf16[1,3,192,384]{3,2,1,0:T(8,128)(2,1)S(1)}, bf16[1,3,192,384]{3,2,1,0:T(8,128)(2,1)S(1)}, u32[]{:S(2)}, u32[]{:S(2)}) collective-permute-start(bf16[1,3,192,384]{3,2,1,0:T(8,128)(2,1)S(1)} %shard_map.66), channel_id=1, source_target_pairs={{0,4},{1,3},{2,6},{3,1},{4,0},{5,7},{6,2},{7,5},{8,12},{9,11},{10,... | collective-permute-start | bytes 1327112 | tf_op jit(solution)/shard_map/ppermute | solution.py:329
  57.5 0.7 collective-permute-start.4
  58.2 1.4 %shard_map.71 = (f32[2,144,384]{2,1,0:T(8,128)S(1)}, bf16[2,144,384]{2,1,0:T(8,128)(2,1)S(1)}, f32[4,144,384]{2,1,0:T(8,128)}) custom-call(f32[2,3,192,384]{3,2,1,0:T(8,128)S(1)} %get-tuple-element.51.refs_0_.keep_ref, bf16[2,3,192,384]{3,2,1,0:T(8,128)(2,1)S(1)} %collective-permute-done.15.refs_1_.got_ref, ...), custom_call_target="tpu_custom_call" | custom-call | bytes 4644864 | tf_op jit(solution)/shard_map/pallas_call | solution.py:26
  59.6 4.6 %collective-permute-start.17 = (bf16[2,144,384]{2,1,0:T(8,128)(2,1)S(1)}, bf16[2,144,384]{2,1,0:T(8,128)(2,1)S(1)}, u32[]{:S(2)}, u32[]{:S(2)}) collective-permute-start(bf16[2,144,384]{2,1,0:T(8,128)(2,1)S(1)} %get-tuple-element.54), channel_id=1, source_target_pairs={{0,8},{1,9},{2,10},{3,11},{4,12},{5,13},{6,14},{7,15},{8,0},{9,1},... | collective-permute-start | bytes 663560 | tf_op jit(solution)/shard_map/ppermute | solution.py:346
  64.2 3.8 %collective-permute-done.12.more_ref = bf16[1,3,192,384]{3,2,1,0:T(8,128)(2,1)S(1)} collective-permute-done((bf16[1,3,192,384]{3,2,1,0:T(8,128)(2,1)S(1)}, bf16[1,3,192,384]{3,2,1,0:T(8,128)(2,1)S(1)}, u32[]{:S(2)}, u32[]{:S(2)}) %collective-permute-start.12) | collective-permute-done | bytes 442400 | tf_op jit(solution)/shard_map/ppermute | solution.py:329
  68.1 1.4 %shard_map.67 = (f32[2,144,384]{2,1,0:T(8,128)S(1)}, bf16[2,144,384]{2,1,0:T(8,128)(2,1)S(1)}, f32[4,144,384]{2,1,0:T(8,128)}) custom-call(f32[2,3,192,384]{3,2,1,0:T(8,128)S(1)} %get-tuple-element.46.keep_ref, bf16[2,3,192,384]{3,2,1,0:T(8,128)(2,1)S(1)} %collective-permute-done.11.got_ref, bf16[1,3,192,384]{3,2,1,0:T(8,128)(2,1)S(1)} %collective-permute-done.12.more_ref), custom_call_target="tpu_custom_call" | custom-call | bytes 4644864 | tf_op jit(solution)/shard_map/pallas_call | solution.py:26
  69.4 2.6 %collective-permute-start.13 = (bf16[2,144,384]{2,1,0:T(8,128)(2,1)S(1)}, bf16[2,144,384]{2,1,0:T(8,128)(2,1)S(1)}, u32[]{:S(2)}, u32[]{:S(2)}) collective-permute-start(bf16[2,144,384]{2,1,0:T(8,128)(2,1)S(1)} %get-tuple-element.49), channel_id=1, source_target_pairs={{0,8},{1,9},{2,10},{3,11},{4,12},{5,13},{6,14},{7,15},{8,0},{9,1},... | collective-permute-start | bytes 663560 | tf_op jit(solution)/shard_map/ppermute | solution.py:346
  72.0 1.8 %collective-permute-start.7 = (bf16[6,8,768]{2,1,0:T(8,128)(2,1)S(1)}, bf16[6,8,768]{2,1,0:T(8,128)(2,1)S(1)}, u32[]{:S(2)}, u32[]{:S(2)}) collective-permute-start(bf16[6,8,768]{2,1,0:T(8,128)(2,1)S(1)} %get-tuple-element.40), channel_id=1, source_target_pairs={{0,4},{1,5},{2,6},{3,7},{4,0},{5,1},{6,2},{7,3},{8,12},{9,13},{10,... | collective-permute-start | bytes 221192 | tf_op jit(solution)/shard_map/ppermute | solution.py:361
  73.8 0.7 collective-permute-start.8
  74.5 3.2 %shard_map.62 = bf16[6,96,768]{2,1,0:T(8,128)(2,1)} custom-call(bf16[6,96,768]{2,1,0:T(8,128)(2,1)S(1)} %get-tuple-element.33.s_ref, bf16[6,16,768]{2,1,0:T(8,128)(2,1)S(1)} %collective-permute-done.3.a_ref, bf16[6,16,768]{2,1,0:T(8,128)(2,1)S(1)} %collective-permute-done.4.b_ref, bf16[2,3,768,768]{3,2,1,0:T(8,128)(2,1)S(1)} %copy-done.1, ...), custom_call_target="tpu_custom_call" | custom-call | flops 2038431744 | bytes 10027008 | tf_op jit(solution)/shard_map/pallas_call | solution.py:26
  77.6 4.1 %collective-permute-start.18 = (bf16[1,144,384]{2,1,0:T(8,128)(2,1)S(1)}, bf16[1,144,384]{2,1,0:T(8,128)(2,1)S(1)}, u32[]{:S(2)}, u32[]{:S(2)}) collective-permute-start(bf16[1,144,384]{2,1,0:T(8,128)(2,1)S(1)} %shard_map.72), channel_id=1, source_target_pairs={{0,24},{1,25},{2,26},{3,27},{4,28},{5,29},{6,30},{7,31},{8,16},{9,... | collective-permute-start | bytes 331784 | tf_op jit(solution)/shard_map/ppermute | solution.py:351
  81.9 4.4 %shard_map.64 = bf16[6,96,768]{2,1,0:T(8,128)(2,1)} custom-call(bf16[6,96,768]{2,1,0:T(8,128)(2,1)S(1)} %get-tuple-element.39.q_ref, bf16[6,8,768]{2,1,0:T(8,128)(2,1)S(1)} %collective-permute-done.7.a_ref, bf16[6,8,768]{2,1,0:T(8,128)(2,1)S(1)} %collective-permute-done.8.b_ref, bf16[2,3,768,768]{3,2,1,0:T(8,128)(2,1)S(1)} %copy-done.1, ...), custom_call_target="tpu_custom_call" | custom-call | flops 2038431744 | bytes 11649024 | tf_op jit(solution)/shard_map/pallas_call | solution.py:26
  86.3 2.1 %collective-permute-done.14.refs_2_ = bf16[1,144,384]{2,1,0:T(8,128)(2,1)S(1)} collective-permute-done((bf16[1,144,384]{2,1,0:T(8,128)(2,1)S(1)}, bf16[1,144,384]{2,1,0:T(8,128)(2,1)S(1)}, u32[]{:S(2)}, u32[]{:S(2)}) %collective-permute-start.14) | collective-permute-done | bytes 110624 | tf_op jit(solution)/shard_map/ppermute | solution.py:351
  88.4 1.1 %shard_map.73 = f32[2,3,192,96]{3,2,1,0:T(8,128)} custom-call(f32[2,144,384]{2,1,0:T(8,128)S(1)} %get-tuple-element.48.keep_ref.refs_0_, bf16[2,144,384]{2,1,0:T(8,128)(2,1)S(1)} %collective-permute-done.13.got_ref.refs_1_, bf16[1,144,384]{2,1,0:T(8,128)(2,1)S(1)} %collective-permute-done.14.refs_2_, f32[2,144,384]{2,1,0:T(8,128)S(1)} %get-tuple-element.53.keep_ref.refs_3_, ...), custom_call_target="tpu_custom_call" | custom-call | bytes 1990656 | tf_op jit(solution)/shard_map/pallas_call | solution.py:26
  (34 shorter events, 2.8 us)
Async XLA Ops:
  0.6 15.6 %collective-permute-start.2 = (bf16[6,96,768]{2,1,0:T(8,128)(2,1)}, bf16[6,96,768]{2,1,0:T(8,128)(2,1)S(1)}, u32[]{:S(2)}, u32[]{:S(2)}) collective-permute-start(bf16[6,96,768]{2,1,0:T(8,128)(2,1)} %refs_2_.1), channel_id=1, source_target_pairs={{0,1},{1,0},{2,3},{3,2},{4,5},{5,4},{6,7},{7,6},{8,9},{9,8},{10,11... | collective-permute-start | bytes 2654216 | tf_op jit(solution)/shard_map/ppermute | solution.py:290
  1.1 1.2 %copy-start.2 = (bf16[6,96,768]{2,1,0:T(8,128)(2,1)S(1)}, bf16[6,96,768]{2,1,0:T(8,128)(2,1)}, u32[]{:S(2)}) copy-start(bf16[6,96,768]{2,1,0:T(8,128)(2,1)} %h_ref.5) | copy-start | bytes 2654212
  2.3 1.2 %copy-start.4 = (bf16[6,96,768]{2,1,0:T(8,128)(2,1)S(1)}, bf16[6,96,768]{2,1,0:T(8,128)(2,1)}, u32[]{:S(2)}) copy-start(bf16[6,96,768]{2,1,0:T(8,128)(2,1)} %refs_2_.1) | copy-start | bytes 2654212
  3.5 3.3 %copy-start.5 = (bf16[6,96,768]{2,1,0:T(8,128)(2,1)S(1)}, bf16[6,96,768]{2,1,0:T(8,128)(2,1)}, u32[]{:S(2)}) copy-start(bf16[6,96,768]{2,1,0:T(8,128)(2,1)} %refs_2_.1) | copy-start | bytes 2654212
  3.6 12.7 %collective-permute-start = (bf16[6,24,768]{2,1,0:T(8,128)(2,1)S(1)}, bf16[6,24,768]{2,1,0:T(8,128)(2,1)S(1)}, u32[]{:S(2)}, u32[]{:S(2)}) collective-permute-start(bf16[6,24,768]{2,1,0:T(8,128)(2,1)S(1)} %get-tuple-element.31), channel_id=1, source_target_pairs={{0,4},{1,5},{2,6},{3,7},{4,0},{5,1},{6,2},{7,3},{8,12},{9,13},{10,... | collective-permute-start | bytes 663560 | tf_op jit(solution)/shard_map/ppermute | solution.py:289
  6.2 10.1 %collective-permute-start.1 = (bf16[6,24,768]{2,1,0:T(8,128)(2,1)S(1)}, bf16[6,24,768]{2,1,0:T(8,128)(2,1)S(1)}, u32[]{:S(2)}, u32[]{:S(2)}) collective-permute-start(bf16[6,24,768]{2,1,0:T(8,128)(2,1)S(1)} %get-tuple-element.32), channel_id=1, source_target_pairs={{4,8},{5,9},{6,10},{7,11},{8,4},{9,5},{10,6},{11,7},{12,16},{13,17... | collective-permute-start | bytes 663560 | tf_op jit(solution)/shard_map/ppermute | solution.py:289
  6.8 3.0 %copy-start = (bf16[2,3,768,768]{3,2,1,0:T(8,128)(2,1)S(1)}, bf16[2,3,768,768]{3,2,1,0:T(8,128)(2,1)}, u32[]{:S(2)}) copy-start(bf16[2,3,768,768]{3,2,1,0:T(8,128)(2,1)} %w_ref.7) | copy-start | bytes 21233668
  9.8 3.0 %copy-start.1 = (bf16[2,3,768,768]{3,2,1,0:T(8,128)(2,1)S(1)}, bf16[2,3,768,768]{3,2,1,0:T(8,128)(2,1)}, u32[]{:S(2)}) copy-start(bf16[2,3,768,768]{3,2,1,0:T(8,128)(2,1)} %w_ref.7) | copy-start | bytes 21233668
  9.8 3.2 %copy-start.3 = (bf16[6,96,768]{2,1,0:T(8,128)(2,1)S(1)}, bf16[6,96,768]{2,1,0:T(8,128)(2,1)}, u32[]{:S(2)}) copy-start(bf16[6,96,768]{2,1,0:T(8,128)(2,1)} %h_ref.5) | copy-start | bytes 2654212
  18.1 2.3 %collective-permute-start.5 = (bf16[6,96,384]{2,1,0:T(8,128)(2,1)S(1)}, bf16[6,96,384]{2,1,0:T(8,128)(2,1)S(1)}, u32[]{:S(2)}, u32[]{:S(2)}) collective-permute-start(bf16[6,96,384]{2,1,0:T(8,128)(2,1)S(1)} %get-tuple-element.37), channel_id=1, source_target_pairs={{0,1},{1,0},{2,3},{3,2},{4,5},{5,4},{6,7},{7,6},{8,9},{9,8},{10,11... | collective-permute-start | bytes 1327112 | tf_op jit(solution)/shard_map/ppermute | solution.py:314
  18.1 2.2 %collective-permute-start.6 = (bf16[6,32,768]{2,1,0:T(8,128)(2,1)S(1)}, bf16[6,32,768]{2,1,0:T(8,128)(2,1)S(1)}, u32[]{:S(2)}, u32[]{:S(2)}) collective-permute-start(bf16[6,32,768]{2,1,0:T(8,128)(2,1)S(1)} %get-tuple-element.38.refs_4_), channel_id=1, source_target_pairs={{0,1},{1,0},{2,3},{3,2},{4,5},{5,4},{6,7},{7,6},{8,9},{9,8},{10,11... | collective-permute-start | bytes 884744 | tf_op jit(solution)/shard_map/ppermute | solution.py:314
  22.5 5.2 %collective-permute-start.10 = (bf16[6,96,768]{2,1,0:T(8,128)(2,1)S(1)}, bf16[6,96,768]{2,1,0:T(8,128)(2,1)S(1)}, u32[]{:S(2)}, u32[]{:S(2)}) collective-permute-start(bf16[6,96,768]{2,1,0:T(8,128)(2,1)S(1)} %get-tuple-element.45.q_ref), channel_id=1, source_target_pairs={{0,1},{1,0},{2,3},{3,2},{4,5},{5,4},{6,7},{7,6},{8,9},{9,8},{10,11... | collective-permute-start | bytes 2654216 | tf_op jit(solution)/shard_map/ppermute | solution.py:371
  22.7 5.0 %collective-permute-start.9 = (bf16[6,112,384]{2,1,0:T(8,128)(2,1)S(1)}, bf16[6,112,384]{2,1,0:T(8,128)(2,1)S(1)}, u32[]{:S(2)}, u32[]{:S(2)}) collective-permute-start(bf16[6,112,384]{2,1,0:T(8,128)(2,1)S(1)} %get-tuple-element.44), channel_id=1, source_target_pairs={{0,1},{1,0},{2,3},{3,2},{4,5},{5,4},{6,7},{7,6},{8,9},{9,8},{10,11... | collective-permute-start | bytes 1548296 | tf_op jit(solution)/shard_map/ppermute | solution.py:314
  26.2 13.1 %collective-permute-start.15 = (bf16[2,3,192,384]{3,2,1,0:T(8,128)(2,1)S(1)}, bf16[2,3,192,384]{3,2,1,0:T(8,128)(2,1)S(1)}, u32[]{:S(2)}, u32[]{:S(2)}) collective-permute-start(bf16[2,3,192,384]{3,2,1,0:T(8,128)(2,1)S(1)} %get-tuple-element.52), channel_id=1, source_target_pairs={{0,2},{1,5},{2,0},{3,7},{4,6},{5,1},{6,4},{7,3},{8,10},{9,13},{10,... | collective-permute-start | bytes 2654216 | tf_op jit(solution)/shard_map/ppermute | solution.py:369
  30.5 23.0 %collective-permute-start.11 = (bf16[2,3,192,384]{3,2,1,0:T(8,128)(2,1)S(1)}, bf16[2,3,192,384]{3,2,1,0:T(8,128)(2,1)S(1)}, u32[]{:S(2)}, u32[]{:S(2)}) collective-permute-start(bf16[2,3,192,384]{3,2,1,0:T(8,128)(2,1)S(1)} %get-tuple-element.47.refs_2_), channel_id=1, source_target_pairs={{0,2},{1,5},{2,0},{3,7},{4,6},{5,1},{6,4},{7,3},{8,10},{9,13},{10,... | collective-permute-start | bytes 2654216 | tf_op jit(solution)/shard_map/ppermute | solution.py:375
  39.4 18.8 %collective-permute-start.16 = (bf16[1,3,192,384]{3,2,1,0:T(8,128)(2,1)S(1)}, bf16[1,3,192,384]{3,2,1,0:T(8,128)(2,1)S(1)}, u32[]{:S(2)}, u32[]{:S(2)}) collective-permute-start(bf16[1,3,192,384]{3,2,1,0:T(8,128)(2,1)S(1)} %shard_map.70), channel_id=1, source_target_pairs={{0,4},{1,3},{2,6},{3,1},{4,0},{5,7},{6,2},{7,5},{8,12},{9,11},{10,... | collective-permute-start | bytes 1327112 | tf_op jit(solution)/shard_map/ppermute | solution.py:329
  53.6 14.5 %collective-permute-start.12 = (bf16[1,3,192,384]{3,2,1,0:T(8,128)(2,1)S(1)}, bf16[1,3,192,384]{3,2,1,0:T(8,128)(2,1)S(1)}, u32[]{:S(2)}, u32[]{:S(2)}) collective-permute-start(bf16[1,3,192,384]{3,2,1,0:T(8,128)(2,1)S(1)} %shard_map.66), channel_id=1, source_target_pairs={{0,4},{1,3},{2,6},{3,1},{4,0},{5,7},{6,2},{7,5},{8,12},{9,11},{10,... | collective-permute-start | bytes 1327112 | tf_op jit(solution)/shard_map/ppermute | solution.py:329
  57.5 16.3 %collective-permute-start.3 = (bf16[6,16,768]{2,1,0:T(8,128)(2,1)S(1)}, bf16[6,16,768]{2,1,0:T(8,128)(2,1)S(1)}, u32[]{:S(2)}, u32[]{:S(2)}) collective-permute-start(bf16[6,16,768]{2,1,0:T(8,128)(2,1)S(1)} %get-tuple-element.34), channel_id=1, source_target_pairs={{0,4},{1,5},{2,6},{3,7},{4,0},{5,1},{6,2},{7,3},{8,12},{9,13},{10,... | collective-permute-start | bytes 442376 | tf_op jit(solution)/shard_map/ppermute | solution.py:315
  57.5 16.9 %collective-permute-start.4 = (bf16[6,16,768]{2,1,0:T(8,128)(2,1)S(1)}, bf16[6,16,768]{2,1,0:T(8,128)(2,1)S(1)}, u32[]{:S(2)}, u32[]{:S(2)}) collective-permute-start(bf16[6,16,768]{2,1,0:T(8,128)(2,1)S(1)} %get-tuple-element.35), channel_id=1, source_target_pairs={{4,8},{5,9},{6,10},{7,11},{8,4},{9,5},{10,6},{11,7},{12,16},{13,17... | collective-permute-start | bytes 442376 | tf_op jit(solution)/shard_map/ppermute | solution.py:315
  59.6 18.0 %collective-permute-start.17 = (bf16[2,144,384]{2,1,0:T(8,128)(2,1)S(1)}, bf16[2,144,384]{2,1,0:T(8,128)(2,1)S(1)}, u32[]{:S(2)}, u32[]{:S(2)}) collective-permute-start(bf16[2,144,384]{2,1,0:T(8,128)(2,1)S(1)} %get-tuple-element.54), channel_id=1, source_target_pairs={{0,8},{1,9},{2,10},{3,11},{4,12},{5,13},{6,14},{7,15},{8,0},{9,1},... | collective-permute-start | bytes 663560 | tf_op jit(solution)/shard_map/ppermute | solution.py:346
  69.4 12.3 %collective-permute-start.13 = (bf16[2,144,384]{2,1,0:T(8,128)(2,1)S(1)}, bf16[2,144,384]{2,1,0:T(8,128)(2,1)S(1)}, u32[]{:S(2)}, u32[]{:S(2)}) collective-permute-start(bf16[2,144,384]{2,1,0:T(8,128)(2,1)S(1)} %get-tuple-element.49), channel_id=1, source_target_pairs={{0,8},{1,9},{2,10},{3,11},{4,12},{5,13},{6,14},{7,15},{8,0},{9,1},... | collective-permute-start | bytes 663560 | tf_op jit(solution)/shard_map/ppermute | solution.py:346
  72.0 9.9 %collective-permute-start.7 = (bf16[6,8,768]{2,1,0:T(8,128)(2,1)S(1)}, bf16[6,8,768]{2,1,0:T(8,128)(2,1)S(1)}, u32[]{:S(2)}, u32[]{:S(2)}) collective-permute-start(bf16[6,8,768]{2,1,0:T(8,128)(2,1)S(1)} %get-tuple-element.40), channel_id=1, source_target_pairs={{0,4},{1,5},{2,6},{3,7},{4,0},{5,1},{6,2},{7,3},{8,12},{9,13},{10,... | collective-permute-start | bytes 221192 | tf_op jit(solution)/shard_map/ppermute | solution.py:361
  73.8 8.1 %collective-permute-start.8 = (bf16[6,8,768]{2,1,0:T(8,128)(2,1)S(1)}, bf16[6,8,768]{2,1,0:T(8,128)(2,1)S(1)}, u32[]{:S(2)}, u32[]{:S(2)}) collective-permute-start(bf16[6,8,768]{2,1,0:T(8,128)(2,1)S(1)} %get-tuple-element.41), channel_id=1, source_target_pairs={{4,8},{5,9},{6,10},{7,11},{8,4},{9,5},{10,6},{11,7},{12,16},{13,17... | collective-permute-start | bytes 221192 | tf_op jit(solution)/shard_map/ppermute | solution.py:361
  77.6 8.6 %collective-permute-start.18 = (bf16[1,144,384]{2,1,0:T(8,128)(2,1)S(1)}, bf16[1,144,384]{2,1,0:T(8,128)(2,1)S(1)}, u32[]{:S(2)}, u32[]{:S(2)}) collective-permute-start(bf16[1,144,384]{2,1,0:T(8,128)(2,1)S(1)} %shard_map.72), channel_id=1, source_target_pairs={{0,24},{1,25},{2,26},{3,27},{4,28},{5,29},{6,30},{7,31},{8,16},{9,... | collective-permute-start | bytes 331784 | tf_op jit(solution)/shard_map/ppermute | solution.py:351
  81.8 6.6 %collective-permute-start.14 = (bf16[1,144,384]{2,1,0:T(8,128)(2,1)S(1)}, bf16[1,144,384]{2,1,0:T(8,128)(2,1)S(1)}, u32[]{:S(2)}, u32[]{:S(2)}) collective-permute-start(bf16[1,144,384]{2,1,0:T(8,128)(2,1)S(1)} %shard_map.68), channel_id=1, source_target_pairs={{0,24},{1,25},{2,26},{3,27},{4,28},{5,29},{6,30},{7,31},{8,16},{9,... | collective-permute-start | bytes 331784 | tf_op jit(solution)/shard_map/ppermute | solution.py:351
